TPU v7x, 32 devices: a whole 2x2x4 slice. The times are simulated.
32 devices in a mesh: dp: 8 (over z, x), tensor: 4 (over y, core).
Axes of the slice: x: 2, y: 2, z: 4, core: 2. Of those that a mesh axis runs over, the one named last changes fastest.
Arguments:
- hidden_in: bfloat16 [8, 512, 2048], P('dp', 'tensor'), may hold values from -6 to 6
- out_grad: bfloat16 [8, 512, 2048], P('dp', 'tensor'), may hold values from -6 to 6
- doc_lengths: int32 [8, 4], P('dp'), may hold values from 1 to 384, 512 in all within a row
- norm_gains: float32 [2, 2048], replicated, may hold values from 0.5 to 1.5
- w_query: float32 [2048, 2048], P('dp', 'tensor'), may hold values from -0.125 to 0.125
- w_keyval: float32 [2, 2048, 512], P(None, 'dp', 'tensor'), may hold values from -0.125 to 0.125
- w_out: float32 [2048, 2048], P('tensor', 'dp'), may hold values from -1 to 1
- w_gateup: float32 [2, 2048, 8192], P(None, 'dp', 'tensor'), may hold values from -0.125 to 0.125
- w_down: float32 [8192, 2048], P('tensor', 'dp'), may hold values from -0.0625 to 0.0625
- moment_gains: float32 [2, 2048], replicated, may hold values from -448 to 448
- moment_query: float32 [2048, 2048], P('dp', 'tensor'), may hold values from -192 to 192
- moment_keyval: float32 [2, 2048, 512], P(None, 'dp', 'tensor'), may hold values from -256 to 256
- moment_out: float32 [2048, 2048], P('tensor', 'dp'), may hold values from -56 to 56
- moment_gateup: float32 [2, 2048, 8192], P(None, 'dp', 'tensor'), may hold values from -192 to 192
- moment_down: float32 [8192, 2048], P('tensor', 'dp'), may hold values from -224 to 224
- second_gains: float32 [2, 2048], replicated, may hold values from 5898.24 to 23592.96
- second_query: float32 [2048, 2048], P('dp', 'tensor'), may hold values from 1024 to 4096
- second_keyval: float32 [2, 2048, 512], P(None, 'dp', 'tensor'), may hold values from 2007.04 to 8028.16
- second_out: float32 [2048, 2048], P('tensor', 'dp'), may hold values from 92.16 to 368.64
- second_gateup: float32 [2, 2048, 8192], P(None, 'dp', 'tensor'), may hold values from 1024 to 4096
- second_down: float32 [8192, 2048], P('tensor', 'dp'), may hold values from 1474.56 to 5898.24
Outputs:
- block_out: bfloat16 [8, 512, 2048], P('dp', 'tensor')
- input_grad: float32 [8, 512, 2048], P('dp', 'tensor')
- grad_gains: float32 [2, 2048], replicated
- grad_query: float32 [2048, 2048], P('dp', 'tensor')
- grad_keyval: float32 [2, 2048, 512], P(None, 'dp', 'tensor')
- grad_out: float32 [2048, 2048], P('tensor', 'dp')
- grad_gateup: float32 [2, 2048, 8192], P(None, 'dp', 'tensor')
- grad_down: float32 [8192, 2048], P('tensor', 'dp')
- new_gains: float32 [2, 2048], replicated
- new_query: float32 [2048, 2048], P('dp', 'tensor')
- new_keyval: float32 [2, 2048, 512], P(None, 'dp', 'tensor')
- new_out: float32 [2048, 2048], P('tensor', 'dp')
- new_gateup: float32 [2, 2048, 8192], P(None, 'dp', 'tensor')
- new_down: float32 [8192, 2048], P('tensor', 'dp')
- new_moment_gains: float32 [2, 2048], replicated
- new_moment_query: float32 [2048, 2048], P('dp', 'tensor')
- new_moment_keyval: float32 [2, 2048, 512], P(None, 'dp', 'tensor')
- new_moment_out: float32 [2048, 2048], P('tensor', 'dp')
- new_moment_gateup: float32 [2, 2048, 8192], P(None, 'dp', 'tensor')
- new_moment_down: float32 [8192, 2048], P('tensor', 'dp')
- new_second_gains: float32 [2, 2048], replicated
- new_second_query: float32 [2048, 2048], P('dp', 'tensor')
- new_second_keyval: float32 [2, 2048, 512], P(None, 'dp', 'tensor')
- new_second_out: float32 [2048, 2048], P('tensor', 'dp')
- new_second_gateup: float32 [2, 2048, 8192], P(None, 'dp', 'tensor')
- new_second_down: float32 [8192, 2048], P('tensor', 'dp')
- weight_norms: float32 [9], replicated
- update_norms: float32 [9], replicated
- trust_ratios: float32 [9], replicated
Inputs may be any that keep to these rules, and one draw needn't show every extreme that they name: `doc_lengths`: each row's 4 lengths add up to 512, and the longest is exactly 384.
All inputs are finite; a program needn't handle non-finite values.
Results may differ from a plain program's by a relative error of at most 0.015.
Values may be sent and summed in bfloat16 or wider, within the bound.
No kernel may reach another device: no remote copies, remote signals or barrier semaphores. Data moves between devices by JAX's collectives and lax.ppermute only.
A program may use at most 256 MiB of HBM per device.

v0:
```python
import jax
import jax.numpy as jnp
import numpy as np
from jax import lax
from jax.sharding import PartitionSpec as P

HD = 64


EPS_NORM = 1e-05
BETA = 0.5
LAMB_EPS = 1e-06
DECAY = 0.01
RATE = 0.5
NEG_FILL = -1e30


def rope_inverse(half_dim):
    exponent = np.arange(half_dim, dtype=np.float32) * np.float32(2.0 / (2 * half_dim))
    base_freq = np.float32(1.0) / np.power(np.float32(500000.0), exponent)
    wave_len = np.float32(2.0 * np.pi) / base_freq
    smooth = (np.float32(8192.0) / wave_len - np.float32(1.0)) / np.float32(3.0)
    middle = (np.float32(1.0) - smooth) * base_freq / np.float32(32.0) + smooth * base_freq
    scaled = np.where(
        wave_len < 2048.0,
        base_freq,
        np.where(wave_len > 8192.0, base_freq / np.float32(32.0), middle),
    )
    return scaled.astype(np.float32)


def doc_layout(lengths, row_len):
    doc_ends = jnp.cumsum(lengths, dtype=jnp.int32)
    starts_at = doc_ends - lengths
    position = jnp.arange(row_len, dtype=jnp.int32)
    segment = jnp.sum(
        (position[:, None] >= doc_ends[None, :]).astype(jnp.int32), axis=1, dtype=jnp.int32
    )
    onehot_doc = (
        segment[:, None] == jnp.arange(lengths.shape[0], dtype=jnp.int32)[None, :]
    ).astype(jnp.int32)
    doc_place = position - jnp.sum(onehot_doc * starts_at[None, :], axis=1, dtype=jnp.int32)
    return (segment, doc_place)


def rope_tables(doc_place, head_dim):
    inverse = jnp.asarray(rope_inverse(head_dim // 2))
    angles = doc_place.astype(jnp.float32)[:, None] * inverse[None, :]
    return (jnp.cos(angles), jnp.sin(angles))


def rotate(vectors, cosine, sine_part):
    half_dim = vectors.shape[-1] // 2
    front_half = vectors[..., :half_dim]
    back_half = vectors[..., half_dim:]
    cos_wide = cosine[:, None, :]
    sin_wide = sine_part[:, None, :]
    return jnp.concatenate(
        [
            front_half * cos_wide - back_half * sin_wide,
            back_half * cos_wide + front_half * sin_wide,
        ],
        axis=-1,
    )


def unrotate(gradient, cosine, sine_part):
    half_dim = gradient.shape[-1] // 2
    front_half = gradient[..., :half_dim]
    back_half = gradient[..., half_dim:]
    cos_wide = cosine[:, None, :]
    sin_wide = sine_part[:, None, :]
    return jnp.concatenate(
        [
            front_half * cos_wide + back_half * sin_wide,
            back_half * cos_wide - front_half * sin_wide,
        ],
        axis=-1,
    )


def dot_rows(left_side, right_side):
    return lax.dot_general(
        left_side, right_side, (((1,), (1,)), ((), ())), preferred_element_type=jnp.float32
    )


def dot_cols(left_side, right_side):
    return lax.dot_general(
        left_side, right_side, (((0,), (0,)), ((), ())), preferred_element_type=jnp.float32
    )


def pair_sums(left_parts, right_parts):
    pieces = []
    for left_side, right_side, stacked in zip(
        left_parts, right_parts, (False, True, False, True, False)
    ):
        product = left_side * right_side
        if stacked:
            pieces.append(jnp.sum(product, axis=(1, 2)))
        else:
            pieces.append(jnp.sum(product)[None])
    return jnp.concatenate(pieces)


def scale_parts(parts, factors):
    return (
        parts[0] * factors[0],
        parts[1] * factors[1:3][:, None, None],
        parts[2] * factors[3],
        parts[3] * factors[4:6][:, None, None],
        parts[4] * factors[6],
    )


def lamb_moments(gradient, moment, second):
    new_moment = BETA * moment + (1.0 - BETA) * gradient
    new_second = BETA * second + (1.0 - BETA) * gradient * gradient
    return (new_moment, new_second, new_moment / (jnp.sqrt(new_second) + LAMB_EPS))


def per_device(
    hidden_in,
    out_grad,
    doc_lengths,
    norm_gains,
    w_query,
    w_keyval,
    w_out,
    w_gateup,
    w_down,
    moment_gains,
    moment_query,
    moment_keyval,
    moment_out,
    moment_gateup,
    moment_down,
    second_gains,
    second_query,
    second_keyval,
    second_out,
    second_gateup,
    second_down,
):
    tok_local = hidden_in.shape[1]
    row_len = tok_local * lax.axis_size("tensor")
    local_heads = w_query.shape[1] // HD
    local_kv = w_keyval.shape[2] // HD
    group_size = local_heads // local_kv
    block_rows = min(512, row_len)
    count_blocks = row_len // block_rows
    score_scale = HD ** (-0.5)
    segment, doc_place = doc_layout(doc_lengths[0], row_len)
    cosine, sine_part = rope_tables(doc_place, HD)
    key_pos = jnp.arange(row_len, dtype=jnp.int32)
    masters = (w_query, w_keyval, w_out, w_gateup, w_down)
    query_shard = w_query.astype(jnp.bfloat16)
    keyval_shard = w_keyval.astype(jnp.bfloat16)
    out_shard = w_out.astype(jnp.bfloat16)
    gateup_shard = w_gateup.astype(jnp.bfloat16)
    down_shard = w_down.astype(jnp.bfloat16)
    gathered = (
        lax.all_gather(query_shard, "dp", axis=0, tiled=True),
        lax.all_gather(keyval_shard, "dp", axis=1, tiled=True),
        lax.all_gather(out_shard, "dp", axis=1, tiled=True),
        lax.all_gather(gateup_shard, "dp", axis=1, tiled=True),
        lax.all_gather(down_shard, "dp", axis=1, tiled=True),
    )
    query_w, keyval_w, out_w, gateup_w, down_w = gathered
    x_float = hidden_in[0].astype(jnp.float32)
    gain_attn = norm_gains[0]
    gain_ffn = norm_gains[1]
    inv_one = lax.rsqrt(jnp.mean(x_float * x_float, axis=-1, keepdims=True) + EPS_NORM)
    normed_one = x_float * inv_one
    attn_input = lax.all_gather(
        (normed_one * gain_attn).astype(jnp.bfloat16), "tensor", axis=0, tiled=True
    )
    query_raw = jnp.dot(attn_input, query_w, preferred_element_type=jnp.float32).reshape(
        row_len, local_heads, HD
    )
    key_raw = jnp.dot(attn_input, keyval_w[0], preferred_element_type=jnp.float32).reshape(
        row_len, local_kv, HD
    )
    values = (
        jnp.dot(attn_input, keyval_w[1], preferred_element_type=jnp.float32)
        .astype(jnp.bfloat16)
        .reshape(row_len, local_kv, HD)
    )
    queries = rotate(query_raw, cosine, sine_part).astype(jnp.bfloat16)
    key_rot = rotate(key_raw, cosine, sine_part).astype(jnp.bfloat16)

    def scores_for(block_index):
        first_row = block_index * block_rows
        query_block = lax.dynamic_slice_in_dim(queries, first_row, block_rows, 0).reshape(
            block_rows, local_kv, group_size, HD
        )
        pos_block = first_row + jnp.arange(block_rows, dtype=jnp.int32)
        allowed = (segment[:, None] == segment[None, :]) & (key_pos[None, :] <= pos_block[:, None])
        raw_scores = jnp.einsum(
            "qkgd,tkd->kgqt", query_block, key_rot, preferred_element_type=jnp.float32
        )
        return (jnp.where(allowed[None, None], raw_scores * score_scale, NEG_FILL), query_block)

    def attend(block_index):
        scores, query_block = scores_for(block_index)
        row_max = jnp.max(scores, axis=-1, keepdims=True)
        shifted = jnp.exp(scores - row_max)
        row_total = jnp.sum(shifted, axis=-1, keepdims=True)
        probabilities = (shifted / row_total).astype(jnp.bfloat16)
        context_block = jnp.einsum(
            "kgqt,tkd->qkgd", probabilities, values, preferred_element_type=jnp.float32
        )
        return (
            context_block.reshape(block_rows, local_heads * HD).astype(jnp.bfloat16),
            (row_max + jnp.log(row_total))[..., 0],
        )

    contexts, log_totals = lax.map(attend, jnp.arange(count_blocks, dtype=jnp.int32))
    context = contexts.reshape(row_len, local_heads * HD)
    row_slice = context
    mid_stream = x_float + lax.psum_scatter(
        jnp.dot(row_slice, out_w, preferred_element_type=jnp.float32),
        "tensor",
        scatter_dimension=0,
        tiled=True,
    )
    inv_two = lax.rsqrt(jnp.mean(mid_stream * mid_stream, axis=-1, keepdims=True) + EPS_NORM)
    normed_two = mid_stream * inv_two
    ffn_input = lax.all_gather(
        (normed_two * gain_ffn).astype(jnp.bfloat16), "tensor", axis=0, tiled=True
    )
    gate_pre = jnp.dot(ffn_input, gateup_w[0], preferred_element_type=jnp.float32)
    up_pre = jnp.dot(ffn_input, gateup_w[1], preferred_element_type=jnp.float32)
    sigmoid_gate = jax.nn.sigmoid(gate_pre)
    silu_gate = gate_pre * sigmoid_gate
    hidden_act = (silu_gate * up_pre).astype(jnp.bfloat16)
    row_slice = hidden_act
    result_rows = mid_stream + lax.psum_scatter(
        jnp.dot(row_slice, down_w, preferred_element_type=jnp.float32).astype(jnp.bfloat16),
        "tensor",
        scatter_dimension=0,
        tiled=True,
    ).astype(jnp.float32)
    block_out = result_rows.astype(jnp.bfloat16)[None]
    query_w, keyval_w, out_w, gateup_w, down_w = (
        lax.all_gather(query_shard, "dp", axis=0, tiled=True),
        lax.all_gather(keyval_shard, "dp", axis=1, tiled=True),
        lax.all_gather(out_shard, "dp", axis=1, tiled=True),
        lax.all_gather(gateup_shard, "dp", axis=1, tiled=True),
        lax.all_gather(down_shard, "dp", axis=1, tiled=True),
    )
    grad_local = out_grad[0].astype(jnp.float32)
    grad_full = lax.all_gather(out_grad[0], "tensor", axis=0, tiled=True)
    grad_hidden = dot_rows(grad_full, down_w)
    grad_gate = grad_hidden * up_pre * (sigmoid_gate * (1.0 + gate_pre * (1.0 - sigmoid_gate)))
    grad_up = grad_hidden * silu_gate
    grad_pair = jnp.stack([grad_gate.astype(jnp.bfloat16), grad_up.astype(jnp.bfloat16)])
    row_slice = grad_pair
    grad_ffn_in = lax.psum_scatter(
        jnp.einsum("stf,sdf->td", row_slice, gateup_w, preferred_element_type=jnp.float32),
        "tensor",
        scatter_dimension=0,
        tiled=True,
    )
    gain_grad_ffn = jnp.sum(grad_ffn_in * normed_two, axis=0)
    grad_normed_two = grad_ffn_in * gain_ffn
    grad_mid = grad_local + inv_two * (
        grad_normed_two
        - normed_two * jnp.mean(grad_normed_two * normed_two, axis=-1, keepdims=True)
    )
    grad_mid_full = lax.all_gather(grad_mid.astype(jnp.bfloat16), "tensor", axis=0, tiled=True)
    grad_context = (
        dot_rows(grad_mid_full, out_w)
        .astype(jnp.bfloat16)
        .reshape(row_len, local_kv, group_size, HD)
    )

    def back_block(running, block_index):
        grad_keys, grad_values = running
        scores, query_block = scores_for(block_index)
        probabilities = jnp.exp(scores - log_totals[block_index][..., None])
        grad_probs = jnp.einsum(
            "qkgd,tkd->kgqt", grad_context, values, preferred_element_type=jnp.float32
        )
        inner_sum = jnp.sum(probabilities * grad_probs, axis=-1, keepdims=True)
        grad_scores = (probabilities * (grad_probs - inner_sum) * score_scale).astype(jnp.bfloat16)
        grad_queries = jnp.einsum(
            "kgqt,tkd->qkgd", grad_scores, key_rot, preferred_element_type=jnp.float32
        )
        grad_keys = grad_keys + jnp.einsum(
            "kgqt,qkgd->tkd", grad_scores, query_block, preferred_element_type=jnp.float32
        )
        grad_values = grad_values + jnp.einsum(
            "kgqt,qkgd->tkd",
            probabilities.astype(jnp.bfloat16),
            grad_context,
            preferred_element_type=jnp.float32,
        )
        return ((grad_keys, grad_values), grad_queries.reshape(block_rows, local_heads, HD))

    zero_kv = jnp.zeros((row_len, local_kv, HD), jnp.float32)
    (grad_keys, grad_values), grad_queries = lax.scan(
        back_block, (zero_kv, zero_kv), jnp.arange(count_blocks, dtype=jnp.int32)
    )
    grad_query_all = (
        unrotate(grad_queries.reshape(row_len, local_heads, HD), cosine, sine_part)
        .reshape(row_len, local_heads * HD)
        .astype(jnp.bfloat16)
    )
    grad_key_all = (
        unrotate(grad_keys, cosine, sine_part).reshape(row_len, local_kv * HD).astype(jnp.bfloat16)
    )
    grad_value_all = grad_values.reshape(row_len, local_kv * HD).astype(jnp.bfloat16)
    kv_pair = jnp.stack([grad_key_all, grad_value_all])
    grad_attn_in = lax.psum_scatter(
        dot_rows(grad_query_all, query_w)
        + jnp.einsum("stc,sdc->td", kv_pair, keyval_w, preferred_element_type=jnp.float32),
        "tensor",
        scatter_dimension=0,
        tiled=True,
    )
    gain_grad_attn = jnp.sum(grad_attn_in * normed_one, axis=0)
    grad_normed_one = grad_attn_in * gain_attn
    input_grad = grad_mid + inv_one * (
        grad_normed_one
        - normed_one * jnp.mean(grad_normed_one * normed_one, axis=-1, keepdims=True)
    )
    grad_query_w = dot_cols(attn_input, grad_query_all)
    grad_keyval_w = jnp.einsum(
        "td,stc->sdc", attn_input, kv_pair, preferred_element_type=jnp.float32
    )
    grad_out_w = dot_cols(context, grad_mid_full)
    grad_gateup_w = jnp.einsum(
        "td,stf->sdf", ffn_input, grad_pair, preferred_element_type=jnp.float32
    )
    grad_down_w = dot_cols(hidden_act, grad_full)
    grad_parts = (
        lax.psum_scatter(grad_query_w, "dp", scatter_dimension=0, tiled=True),
        lax.psum_scatter(grad_keyval_w, "dp", scatter_dimension=1, tiled=True),
        lax.psum_scatter(grad_out_w, "dp", scatter_dimension=1, tiled=True),
        lax.psum_scatter(grad_gateup_w, "dp", scatter_dimension=1, tiled=True),
        lax.psum_scatter(grad_down_w, "dp", scatter_dimension=1, tiled=True),
    )
    gain_local = jnp.stack([gain_grad_attn, gain_grad_ffn])
    moments = (moment_query, moment_keyval, moment_out, moment_gateup, moment_down)
    seconds = (second_query, second_keyval, second_out, second_gateup, second_down)
    results = [lamb_moments(grad_parts[slot], moments[slot], seconds[slot]) for slot in range(5)]
    new_moments = tuple((entry[0] for entry in results))
    new_seconds = tuple((entry[1] for entry in results))
    directions = tuple((entry[2] for entry in results))
    updates = tuple((directions[slot] + DECAY * masters[slot] for slot in range(5)))
    weight_sq_local = pair_sums(masters, masters)
    grad_gains, weight_sq = lax.psum((gain_local, weight_sq_local), ("dp", "tensor"))
    update_sq = lax.psum(pair_sums(updates, updates), ("dp", "tensor"))
    gain_moment, gain_second, gain_direction = lamb_moments(grad_gains, moment_gains, second_gains)
    gain_update = gain_direction + DECAY * norm_gains
    weight_norms = jnp.concatenate(
        [jnp.sqrt(weight_sq), jnp.sqrt(jnp.sum(norm_gains * norm_gains, axis=1))]
    )
    update_norms = jnp.concatenate(
        [jnp.sqrt(update_sq), jnp.sqrt(jnp.sum(gain_update * gain_update, axis=1))]
    )
    trust_ratios = weight_norms / update_norms
    steps_taken = scale_parts(updates, trust_ratios[:7])
    new_parts = tuple((masters[slot] - RATE * steps_taken[slot] for slot in range(5)))
    new_gains = norm_gains - RATE * trust_ratios[7:9][:, None] * gain_update
    return (
        block_out,
        input_grad[None],
        grad_gains,
        grad_parts[0],
        grad_parts[1],
        grad_parts[2],
        grad_parts[3],
        grad_parts[4],
        new_gains,
        new_parts[0],
        new_parts[1],
        new_parts[2],
        new_parts[3],
        new_parts[4],
        gain_moment,
        new_moments[0],
        new_moments[1],
        new_moments[2],
        new_moments[3],
        new_moments[4],
        gain_second,
        new_seconds[0],
        new_seconds[1],
        new_seconds[2],
        new_seconds[3],
        new_seconds[4],
        weight_norms,
        update_norms,
        trust_ratios,
    )


def solution(mesh):
    in_specs = (
        P("dp", "tensor", None),
        P("dp", "tensor", None),
        P("dp", None),
        P(),
        P("dp", "tensor"),
        P(None, "dp", "tensor"),
        P("tensor", "dp"),
        P(None, "dp", "tensor"),
        P("tensor", "dp"),
        P(),
        P("dp", "tensor"),
        P(None, "dp", "tensor"),
        P("tensor", "dp"),
        P(None, "dp", "tensor"),
        P("tensor", "dp"),
        P(),
        P("dp", "tensor"),
        P(None, "dp", "tensor"),
        P("tensor", "dp"),
        P(None, "dp", "tensor"),
        P("tensor", "dp"),
    )
    out_specs = (
        P("dp", "tensor", None),
        P("dp", "tensor", None),
        P(),
        P("dp", "tensor"),
        P(None, "dp", "tensor"),
        P("tensor", "dp"),
        P(None, "dp", "tensor"),
        P("tensor", "dp"),
        P(),
        P("dp", "tensor"),
        P(None, "dp", "tensor"),
        P("tensor", "dp"),
        P(None, "dp", "tensor"),
        P("tensor", "dp"),
        P(),
        P("dp", "tensor"),
        P(None, "dp", "tensor"),
        P("tensor", "dp"),
        P(None, "dp", "tensor"),
        P("tensor", "dp"),
        P(),
        P("dp", "tensor"),
        P(None, "dp", "tensor"),
        P("tensor", "dp"),
        P(None, "dp", "tensor"),
        P("tensor", "dp"),
        P(),
        P(),
        P(),
    )
    return jax.shard_map(
        per_device, mesh=mesh, in_specs=in_specs, out_specs=out_specs, check_vma=False
    )
```

profile of v0, /device:TPU:0, one launch (start us, length us, event | category | flops | bytes accessed | tf_op | source)
XLA Modules:
  0.0 2033.8 jit_solution(2962718250650657658)
XLA Ops:
  19.6 34.1 %all-gather.13.cloned.1.call-done = bf16[2,2048,128]{2,1,0:T(8,128)(2,1)} async-done(((bf16[2,256,128]{2,1,0:T(8,128)(2,1)}), bf16[2,2048,128]{2,1,0:T(8,128)(2,1)}) %all-gather.13.cloned.1.call-update) | async-done | bytes 1048592 | tf_op jit(solution)/shard_map/all_gather | solution.py:165
  56.0 21.3 %all-gather.11.cloned.1.call-done = bf16[512,2048]{1,0:T(8,128)(2,1)} async-done(((bf16[128,2048]{1,0:T(8,128)(2,1)}), bf16[512,2048]{1,0:T(8,128)(2,1)}) %all-gather.11.cloned.1.call-update) | async-done | bytes 2097168 | tf_op jit(solution)/shard_map/all_gather | solution.py:176
  83.1 46.2 %all-gather.15.cloned.1.call-done = bf16[2048,512]{1,0:T(8,128)(2,1)} async-done(((bf16[256,512]{1,0:T(8,128)(2,1)}), bf16[2048,512]{1,0:T(8,128)(2,1)}) %all-gather.15.cloned.1.call-update) | async-done | bytes 2097168 | tf_op jit(solution)/shard_map/all_gather | solution.py:164
  138.8 42.6 %all-gather.17.cloned.1.call-done = bf16[512,2048]{1,0:T(8,128)(2,1)} async-done(((bf16[512,256]{1,0:T(8,128)(2,1)}), bf16[512,2048]{1,0:T(8,128)(2,1)}) %all-gather.17.cloned.1.call-update) | async-done | bytes 2097168 | tf_op jit(solution)/shard_map/all_gather | solution.py:166
  181.4 4.9 fusion.81
  186.4 42.8 %reduce-scatter.10.cloned.1.call-done = f32[128,2048]{1,0:T(8,128)} async-done(((f32[512,2048]{1,0:T(8,128)}), f32[128,2048]{1,0:T(8,128)}) %reduce-scatter.10.cloned.1.call-update) | async-done | bytes 1048592 | tf_op jit(solution)/shard_map/reduce_scatter | solution.py:222
  231.8 6.1 multiply_reduce_fusion.1
  242.0 12.4 all-gather.19.cloned.1.call-done
  254.5 230.6 %all-gather.21.cloned.1.call-done = bf16[2,2048,2048]{2,1,0:T(8,128)(2,1)} async-done(((bf16[2,256,2048]{2,1,0:T(8,128)(2,1)}), bf16[2,2048,2048]{2,1,0:T(8,128)(2,1)}) %all-gather.21.cloned.1.call-update) | async-done | bytes 16777232 | tf_op jit(solution)/shard_map/all_gather | solution.py:167
  485.1 10.7 fusion.2
  496.2 6.1 fusion.1
  502.3 5.3 all-gather.27.cloned.1.call-done
  507.5 128.2 %all-gather.23.cloned.1.call-done = bf16[2048,2048]{1,0:T(8,128)(2,1)} async-done(((bf16[2048,256]{1,0:T(8,128)(2,1)}), bf16[2048,2048]{1,0:T(8,128)(2,1)}) %all-gather.23.cloned.1.call-update) | async-done | bytes 8388624 | tf_op jit(solution)/shard_map/all_gather | solution.py:168
  635.8 13.6 fusion.27
  651.4 13.8 convolution_bitcast_fusion.1
  665.2 42.8 %reduce-scatter.14.cloned.1.call-done = f32[128,2048]{1,0:T(8,128)} async-done(((f32[512,2048]{1,0:T(8,128)}), f32[128,2048]{1,0:T(8,128)}) %reduce-scatter.14.cloned.1.call-update) | async-done | bytes 1048592 | tf_op jit(solution)/shard_map/reduce_scatter | solution.py:260
  713.2 21.6 %all-gather.25.cloned.1.call-done = bf16[512,2048]{1,0:T(8,128)(2,1)} async-done(((bf16[128,2048]{1,0:T(8,128)(2,1)}), bf16[512,2048]{1,0:T(8,128)(2,1)}) %all-gather.25.cloned.1.call-update) | async-done | bytes 2097168 | tf_op jit(solution)/shard_map/all_gather | solution.py:272
  734.8 3.6 convolution_convert_fusion.1
  738.5 4.6 fusion.82
  744.6 15.4 fusion.33
  765.1 15.7 fusion.16
  782.2 3.1 fusion.83
  788.2 4.4 fusion.84
  794.2 4.3 fusion.85
  798.6 10.0 convolution_convert_fusion
  808.7 9.9 fusion.20
  820.1 17.6 convolution_bitcast_fusion
  838.8 5.5 copy.90
  844.6 5.5 copy.89
  850.1 5.5 copy.88
  860.4 19.3 reduce-scatter.16.cloned.1.call-done
  881.3 91.6 %reduce-scatter.18.cloned.1.call-done = f32[256,512]{1,0:T(8,128)} async-done(((f32[2048,512]{1,0:T(8,128)}), f32[256,512]{1,0:T(8,128)}) %reduce-scatter.18.cloned.1.call-update) | async-done | bytes 524304 | tf_op jit(solution)/shard_map/reduce_scatter | solution.py:339
  972.9 3.3 multiply_reduce_fusion.8
  976.2 89.6 %reduce-scatter.22.cloned.1.call-done = f32[512,256]{1,0:T(8,128)} async-done(((f32[512,2048]{1,0:T(8,128)}), f32[512,256]{1,0:T(8,128)}) %reduce-scatter.22.cloned.1.call-update) | async-done | bytes 524304 | tf_op jit(solution)/shard_map/reduce_scatter | solution.py:341
  1065.8 3.4 multiply_reduce_fusion.7
  1069.2 30.9 %reduce-scatter.12.cloned.1.call-done = bf16[128,2048]{1,0:T(8,128)(2,1)} async-done(((bf16[512,2048]{1,0:T(8,128)(2,1)}), bf16[128,2048]{1,0:T(8,128)(2,1)}) %reduce-scatter.12.cloned.1.call-update) | async-done | bytes 524304 | tf_op jit(solution)/shard_map/reduce_scatter | solution.py:239
  1100.1 3.6 fusion.45
  1103.7 283.2 %reduce-scatter.26.cloned.1.call-done = f32[2048,256]{1,0:T(8,128)} async-done(((f32[2048,2048]{1,0:T(8,128)}), f32[2048,256]{1,0:T(8,128)}) %reduce-scatter.26.cloned.1.call-update) | async-done | bytes 2097168 | tf_op jit(solution)/shard_map/reduce_scatter | solution.py:343
  1386.9 6.9 multiply_reduce_fusion.2
  1395.9 537.4 %reduce-scatter.24.cloned.1.call-done = f32[2,256,2048]{1,2,0:T(8,128)} async-done(((f32[2,2048,2048]{1,2,0:T(8,128)}), f32[2,256,2048]{1,2,0:T(8,128)}) %reduce-scatter.24.cloned.1.call-update) | async-done | bytes 4194320 | tf_op jit(solution)/shard_map/reduce_scatter | solution.py:342
  1933.3 9.3 multiply_reduce_fusion
  1944.6 38.8 %all-reduce = (f32[2,2048]{1,0:T(2,128)S(1)}, f32[7]{0:T(128)S(1)}, f32[7]{0:T(128)S(1)}) all-reduce(f32[2,2048]{1,0:T(2,128)S(1)} %pad_maximum_fusion.11, f32[7]{0:T(128)S(1)} %concatenate.39, f32[7]{0:T(128)S(1)} %concatenate.41), channel_id=1, replica_groups=mesh['dp'=8,'tensor'=4] {'dp','tensor'}, use_global_device_ids=true, to_apply=%region_16.17 | all-reduce | flops 4110 | bytes 32880 | tf_op jit(solution)/shard_map/psum | solution.py:354
  1986.6 5.3 copy.98
  1991.9 5.4 copy.100
  1997.3 8.7 multiply_subtract_fusion
  2006.0 5.4 copy.96
  2012.1 3.2 multiply_subtract_fusion.3
  2021.2 5.3 copy.94
  (208 shorter events, 79.7 us)
Async XLA Ops:
  7.2 12.1 copy-start.42
  7.2 10.8 copy-start.47
  7.2 46.6 %all-gather.13.cloned.1.call-start = ((), (), s32[]{:S(2)}) async-start(), calls=%async_computation.10 | async-start | bytes 1179648 | tf_op jit(solution)/shard_map/all_gather | solution.py:165
  9.5 67.7 %all-gather.11.cloned.1.call-start = ((), (), s32[]{:S(2)}) async-start(), calls=%async_computation.9 | async-start | bytes 2621440 | tf_op jit(solution)/shard_map/all_gather | solution.py:176
  14.3 115.0 %all-gather.15.cloned.1.call-start = ((), (), s32[]{:S(2)}) async-start(), calls=%async_computation.11 | async-start | bytes 2359296 | tf_op jit(solution)/shard_map/all_gather | solution.py:164
  16.1 165.2 %all-gather.17.cloned.1.call-start = ((), (), s32[]{:S(2)}) async-start(), calls=%async_computation.12 | async-start | bytes 2359296 | tf_op jit(solution)/shard_map/all_gather | solution.py:166
  18.0 211.2 %reduce-scatter.10.cloned.1.call-start = ((), (), s32[]{:S(2)}) async-start(), calls=%async_computation.13 | async-start | bytes 5242880 | tf_op jit(solution)/shard_map/reduce_scatter | solution.py:222
  53.8 26.8 %copy-start.10 = (bf16[2,2048,128]{2,1,0:T(8,128)(2,1)S(1)}, bf16[2,2048,128]{2,1,0:T(8,128)(2,1)}, u32[]{:S(2)}) copy-start(bf16[2,2048,128]{2,1,0:T(8,128)(2,1)} %all-gather.13.cloned.1.call-done) | copy-start | bytes 3145732
  77.3 52.0 %copy-start.1 = (bf16[512,2048]{1,0:T(8,128)(2,1)S(1)}, bf16[512,2048]{1,0:T(8,128)(2,1)}, u32[]{:S(2)}) copy-start(bf16[512,2048]{1,0:T(8,128)(2,1)} %all-gather.11.cloned.1.call-done) | copy-start | bytes 6291460
  80.6 51.8 %copy-start.28 = (bf16[512,2,32]{0,2,1:T(8,128)(2,1)}, bf16[512,2,32]{0,2,1:T(8,128)(2,1)S(1)}, u32[]{:S(2)}) copy-start(bf16[512,2,32]{0,2,1:T(8,128)(2,1)S(1)} %get-tuple-element.191) | copy-start | bytes 196612
  83.1 49.3 %copy-start.21 = (pred[512,512]{0,1:T(8,128)(4,1)S(1)}, pred[512,512]{0,1:T(8,128)(4,1)}, u32[]{:S(2)}) copy-start(pred[512,512]{0,1:T(8,128)(4,1)} %fusion.48) | copy-start | bytes 786436
  83.1 49.3 %copy-start.29 = (bf16[512,2,32]{0,2,1:T(8,128)(2,1)S(1)}, bf16[512,2,32]{0,2,1:T(8,128)(2,1)}, u32[]{:S(2)}) copy-start(bf16[512,2,32]{0,2,1:T(8,128)(2,1)} %get-tuple-element.192) | copy-start | bytes 196612
  138.8 47.5 %copy-start.17 = (bf16[2,64,4,512]{3,1,2,0:T(8,128)(2,1)}, bf16[2,64,4,512]{3,1,2,0:T(8,128)(2,1)S(1)}, u32[]{:S(2)}) copy-start(bf16[2,64,4,512]{3,1,2,0:T(8,128)(2,1)S(1)} %fusion.32) | copy-start | bytes 1572868
  186.3 68.2 %all-gather.19.cloned.1.call-start = ((), (), s32[]{:S(2)}) async-start(), calls=%async_computation.14 | async-start | bytes 2621440 | tf_op jit(solution)/shard_map/all_gather | solution.py:230
  230.8 478.8 %copy-start.34 = (f32[128]{0:T(128)}, f32[128]{0:T(128)S(1)}, u32[]{:S(2)}) copy-start(f32[128]{0:T(128)S(1)} %add_rsqrt_fusion) | copy-start | bytes 1540
  231.7 253.3 %all-gather.21.cloned.1.call-start = ((), (), s32[]{:S(2)}) async-start(), calls=%async_computation.15 | async-start | bytes 18874368 | tf_op jit(solution)/shard_map/all_gather | solution.py:167
  238.0 269.6 %all-gather.27.cloned.1.call-start = ((), (), s32[]{:S(2)}) async-start(), calls=%async_computation.26 | async-start | bytes 2621440 | tf_op jit(solution)/shard_map/all_gather | solution.py:254
  238.7 397.1 %all-gather.23.cloned.1.call-start = ((), (), s32[]{:S(2)}) async-start(), calls=%async_computation.16 | async-start | bytes 9437184 | tf_op jit(solution)/shard_map/all_gather | solution.py:168
  241.8 466.2 %reduce-scatter.14.cloned.1.call-start = ((), (), s32[]{:S(2)}) async-start(), calls=%async_computation.18 | async-start | bytes 5242880 | tf_op jit(solution)/shard_map/reduce_scatter | solution.py:260
  485.1 10.7 copy-start.43
  485.1 11.1 copy-start.44
  665.1 69.7 %all-gather.25.cloned.1.call-start = ((), (), s32[]{:S(2)}) async-start(), calls=%async_computation.19 | async-start | bytes 2621440 | tf_op jit(solution)/shard_map/all_gather | solution.py:272
  709.6 28.9 %copy-start.38 = (f32[128]{0:T(128)}, f32[128]{0:T(128)S(1)}, u32[]{:S(2)}) copy-start(f32[128]{0:T(128)S(1)} %broadcast_multiply_fusion.1) | copy-start | bytes 1540
  712.1 143.5 %reduce-scatter.20.cloned.1.call-start = ((), (), s32[]{:S(2)}) async-start(), calls=%async_computation.22 | async-start | bytes 2359296 | tf_op jit(solution)/shard_map/reduce_scatter | solution.py:340
  764.8 114.8 %reduce-scatter.16.cloned.1.call-start = ((), (), s32[]{:S(2)}) async-start(), calls=%async_computation.20 | async-start | bytes 5242880 | tf_op jit(solution)/shard_map/reduce_scatter | solution.py:316
  788.2 184.7 %reduce-scatter.18.cloned.1.call-start = ((), (), s32[]{:S(2)}) async-start(), calls=%async_computation.21 | async-start | bytes 4718592 | tf_op jit(solution)/shard_map/reduce_scatter | solution.py:339
  792.6 273.1 %reduce-scatter.22.cloned.1.call-start = ((), (), s32[]{:S(2)}) async-start(), calls=%async_computation.23 | async-start | bytes 4718592 | tf_op jit(solution)/shard_map/reduce_scatter | solution.py:341
  798.6 301.5 %reduce-scatter.12.cloned.1.call-start = ((), (), s32[]{:S(2)}) async-start(), calls=%async_computation.17 | async-start | bytes 2621440 | tf_op jit(solution)/shard_map/reduce_scatter | solution.py:239
  798.6 10.1 copy-start.46
  808.6 578.3 %reduce-scatter.26.cloned.1.call-start = ((), (), s32[]{:S(2)}) async-start(), calls=%async_computation.25 | async-start | bytes 18874368 | tf_op jit(solution)/shard_map/reduce_scatter | solution.py:343
  818.6 1114.8 %reduce-scatter.24.cloned.1.call-start = ((), (), s32[]{:S(2)}) async-start(), calls=%async_computation.24 | async-start | bytes 37748736 | tf_op jit(solution)/shard_map/reduce_scatter | solution.py:342
  850.1 29.6 %copy-start.3 = (bf16[1,128,2048]{2,1,0:T(8,128)(2,1)S(1)}, bf16[1,128,2048]{2,1,0:T(8,128)(2,1)}, u32[]{:S(2)}) copy-start(bf16[1,128,2048]{2,1,0:T(8,128)(2,1)} %param.22) | copy-start | bytes 1572868
  850.1 29.6 %copy-start.26 = (f32[1,2048]{1,0:T(1,128)S(1)}, f32[1,2048]{1,0:T(1,128)}, u32[]{:S(2)}) copy-start(f32[1,2048]{1,0:T(1,128)} %copy-done.25) | copy-start | bytes 24580
  850.1 29.6 %copy-start.37 = (f32[128]{0:T(128)S(1)}, f32[128]{0:T(128)}, u32[]{:S(2)}) copy-start(f32[128]{0:T(128)} %copy-done.36) | copy-start | bytes 1540
  855.6 117.3 %copy-start.7 = (f32[256,512]{1,0:T(8,128)S(1)}, f32[256,512]{1,0:T(8,128)}, u32[]{:S(2)}) copy-start(f32[256,512]{1,0:T(8,128)} %param.26) | copy-start | bytes 1572868
  856.9 116.0 %copy-start.12 = (f32[2,256,128]{1,2,0:T(8,128)}, f32[2,256,128]{1,2,0:T(8,128)S(1)}, u32[]{:S(2)}) copy-start(f32[2,256,128]{1,2,0:T(8,128)S(1)} %get-tuple-element.168) | copy-start | bytes 786436
  856.9 116.0 %copy-start.14 = (f32[2,256,128]{1,2,0:T(8,128)}, f32[2,256,128]{1,2,0:T(8,128)S(1)}, u32[]{:S(2)}) copy-start(f32[2,256,128]{1,2,0:T(8,128)S(1)} %get-tuple-element.169) | copy-start | bytes 786436
  858.6 241.5 %copy-start.35 = (f32[128]{0:T(128)S(1)}, f32[128]{0:T(128)}, u32[]{:S(2)}) copy-start(f32[128]{0:T(128)} %copy-done.34) | copy-start | bytes 1540
  858.6 241.5 %copy-start.39 = (f32[128]{0:T(128)S(1)}, f32[128]{0:T(128)}, u32[]{:S(2)}) copy-start(f32[128]{0:T(128)} %copy-done.38) | copy-start | bytes 1540
  976.2 410.7 %copy-start.2 = (f32[2048,256]{1,0:T(8,128)S(1)}, f32[2048,256]{1,0:T(8,128)}, u32[]{:S(2)}) copy-start(f32[2048,256]{1,0:T(8,128)} %param.30) | copy-start | bytes 6291460
  1103.7 290.2 %copy-start.40 = (f32[2]{0:T(128)S(1)}, f32[2]{0:T(128)}, u32[]{:S(2)}) copy-start(f32[2]{0:T(128)} %get-tuple-element.193) | copy-start | bytes 28
  1103.7 290.2 %copy-start.41 = (f32[2]{0:T(128)S(1)}, f32[2]{0:T(128)}, u32[]{:S(2)}) copy-start(f32[2]{0:T(128)} %get-tuple-element.181) | copy-start | bytes 28
  1395.9 587.6 %copy-start.24 = (f32[2,2048]{1,0:T(2,128)S(1)}, f32[2,2048]{1,0:T(2,128)}, u32[]{:S(2)}) copy-start(f32[2,2048]{1,0:T(2,128)} %param.25) | copy-start | bytes 49156
  1395.9 587.6 %copy-start.31 = (f32[2,2048]{1,0:T(2,128)S(1)}, f32[2,2048]{1,0:T(2,128)}, u32[]{:S(2)}) copy-start(f32[2,2048]{1,0:T(2,128)} %param.37) | copy-start | bytes 49156
  1395.9 587.6 %copy-start.32 = (f32[2,2048]{1,0:T(2,128)S(1)}, f32[2,2048]{1,0:T(2,128)}, u32[]{:S(2)}) copy-start(f32[2,2048]{1,0:T(2,128)} %param.31) | copy-start | bytes 49156
  1395.9 589.7 %copy-start.13 = (f32[2,256,128]{1,2,0:T(8,128)S(1)}, f32[2,256,128]{1,2,0:T(8,128)}, u32[]{:S(2)}) copy-start(f32[2,256,128]{1,2,0:T(8,128)} %copy-done.12) | copy-start | bytes 786436
  1395.9 589.7 %copy-start.15 = (f32[2,256,128]{1,2,0:T(8,128)S(1)}, f32[2,256,128]{1,2,0:T(8,128)}, u32[]{:S(2)}) copy-start(f32[2,256,128]{1,2,0:T(8,128)} %copy-done.14) | copy-start | bytes 786436
  2006.0 9.3 copy-start.9
  (22 other events, 85.3 us)
Sparse Core Ops, SparseCore 0:
  10.8 42.9 all-gather.12
  55.9 21.3 all-gather.10
  80.0 49.2 all-gather.14
  131.8 49.5 all-gather.16
  186.4 42.7 reduce-scatter.9
  231.9 22.5 all-gather.18
  257.5 227.5 all-gather.20
  486.7 20.7 all-gather.26
  510.4 125.3 all-gather.22
  665.3 42.6 reduce-scatter.13
  712.2 22.5 all-gather.24
  765.0 68.0 reduce-scatter.19
  836.1 43.4 reduce-scatter.15
  884.7 88.1 reduce-scatter.17
  977.5 88.1 reduce-scatter.21
  1068.9 31.1 reduce-scatter.11
  1104.3 282.5 reduce-scatter.25
  1391.0 542.2 reduce-scatter.23
where the time goes:
time: 2040 us; the launch traced here: 2030 us
  waiting for transfers between devices  1680 us (82%)
  matrix products  155 us (8%)
  other arithmetic  81.6 us (4%)
  local copies, waits for them, and re-layouts  60.5 us (3%)
  blocking collectives  38.8 us (2%)
    reduce_scatter x1, waiting for transfers between devices, per_device(): lax.psum_scatter(grad_gateup_w, 'dp', scatter_dimension=1, tiled=True)  537 us
    reduce_scatter x1, waiting for transfers between devices, per_device(): lax.psum_scatter(grad_down_w, 'dp', scatter_dimension=1, tiled=True)  283 us
    all_gather x1, waiting for transfers between devices, per_device(): lax.all_gather(gateup_shard, 'dp', axis=1, tiled=True)  231 us
    all_gather x1, waiting for transfers between devices, per_device(): lax.all_gather(down_shard, 'dp', axis=1, tiled=True)  128 us
    reduce_scatter x1, waiting for transfers between devices, per_device(): lax.psum_scatter(grad_query_w, 'dp', scatter_dimension=0, tiled=True)  91.6 us
    reduce_scatter x1, waiting for transfers between devices, per_device(): lax.psum_scatter(grad_out_w, 'dp', scatter_dimension=1, tiled=True)  89.6 us
    unnamed x118, local copies, waits for them, and re-layouts  51.7 us
    all_gather x1, waiting for transfers between devices, per_device(): lax.all_gather(query_shard, 'dp', axis=0, tiled=True)  46.2 us
  transfers between devices with their start and end apart: 18, of which 17 were waited for; matrix products, arithmetic and copies ran while one was open for 8% of the time, Pallas kernels for 0%

commit v1 on v0

v1 whole, which is shorter than its diff:
```python
import jax
import jax.numpy as jnp
import numpy as np
from jax import lax
from jax.sharding import PartitionSpec as P

HD = 64


EPS_NORM = 1e-05
BETA = 0.5
LAMB_EPS = 1e-06
DECAY = 0.01
RATE = 0.5
NEG_FILL = -1e30


def rope_inverse(half_dim):
    exponent = np.arange(half_dim, dtype=np.float32) * np.float32(2.0 / (2 * half_dim))
    base_freq = np.float32(1.0) / np.power(np.float32(500000.0), exponent)
    wave_len = np.float32(2.0 * np.pi) / base_freq
    smooth = (np.float32(8192.0) / wave_len - np.float32(1.0)) / np.float32(3.0)
    middle = (np.float32(1.0) - smooth) * base_freq / np.float32(32.0) + smooth * base_freq
    scaled = np.where(
        wave_len < 2048.0,
        base_freq,
        np.where(wave_len > 8192.0, base_freq / np.float32(32.0), middle),
    )
    return scaled.astype(np.float32)


def doc_layout(lengths, position):
    doc_ends = jnp.cumsum(lengths, dtype=jnp.int32)
    starts_at = doc_ends - lengths
    segment = jnp.sum(
        (position[:, None] >= doc_ends[None, :]).astype(jnp.int32), axis=1, dtype=jnp.int32
    )
    onehot_doc = (
        segment[:, None] == jnp.arange(lengths.shape[0], dtype=jnp.int32)[None, :]
    ).astype(jnp.int32)
    doc_place = position - jnp.sum(onehot_doc * starts_at[None, :], axis=1, dtype=jnp.int32)
    return (segment, doc_place)


def rope_tables(doc_place, head_dim):
    inverse = jnp.asarray(rope_inverse(head_dim // 2))
    angles = doc_place.astype(jnp.float32)[:, None] * inverse[None, :]
    return (jnp.cos(angles), jnp.sin(angles))


def rotate(vectors, cosine, sine_part):
    half_dim = vectors.shape[-1] // 2
    front_half = vectors[..., :half_dim]
    back_half = vectors[..., half_dim:]
    cos_wide = cosine[:, None, :]
    sin_wide = sine_part[:, None, :]
    return jnp.concatenate(
        [
            front_half * cos_wide - back_half * sin_wide,
            back_half * cos_wide + front_half * sin_wide,
        ],
        axis=-1,
    )


def unrotate(gradient, cosine, sine_part):
    half_dim = gradient.shape[-1] // 2
    front_half = gradient[..., :half_dim]
    back_half = gradient[..., half_dim:]
    cos_wide = cosine[:, None, :]
    sin_wide = sine_part[:, None, :]
    return jnp.concatenate(
        [
            front_half * cos_wide + back_half * sin_wide,
            back_half * cos_wide - front_half * sin_wide,
        ],
        axis=-1,
    )


def rounded(value):
    return value.astype(jnp.bfloat16)


def widened(value):
    return value.astype(jnp.float32)


def dot_plain(left_side, right_side):
    return jnp.dot(left_side, right_side, preferred_element_type=jnp.float32)


def dot_rows(left_side, right_side):
    return lax.dot_general(
        left_side, right_side, (((1,), (1,)), ((), ())), preferred_element_type=jnp.float32
    )


def dot_cols(left_side, right_side):
    return lax.dot_general(
        left_side, right_side, (((0,), (0,)), ((), ())), preferred_element_type=jnp.float32
    )


def exchange(value, axis, mask):
    if isinstance(axis, tuple):
        size = 1
        for name in axis:
            size = size * lax.axis_size(name)
    else:
        size = lax.axis_size(axis)
    return lax.ppermute(value, axis, [(place, place ^ mask) for place in range(size)])


def gather_row(value):
    pair = jnp.concatenate([value, exchange(value, "y", 1)])
    return jnp.concatenate([pair, exchange(pair, "c", 1)])


def scatter_row(partial):
    half = partial.shape[0] // 2
    quarter = half // 2
    summed = widened(partial[:half]) + widened(exchange(partial[half:], "c", 1))
    return summed[:quarter] + widened(exchange(rounded(summed[quarter:]), "y", 1))


def all_sum(value):
    for axis in ("c", "y", "x", "z", "o"):
        mask = 1
        while mask < lax.axis_size(axis):
            value = value + exchange(value, axis, mask)
            mask = mask * 2
    return value


def lamb_moments(gradient, moment, second):
    new_moment = BETA * moment + (1.0 - BETA) * gradient
    new_second = BETA * second + (1.0 - BETA) * gradient * gradient
    return (new_moment, new_second, new_moment / (jnp.sqrt(new_second) + LAMB_EPS))


def square_sums(parts):
    pieces = []
    for part, stacked in zip(parts, (False, True, False, True, False)):
        if stacked:
            pieces.append(jnp.sum(part[0] * part[0]))
            pieces.append(jnp.sum(part[1] * part[1]))
        else:
            pieces.append(jnp.sum(part * part))
    return jnp.stack(pieces)


def scale_parts(parts, factors):
    return (
        parts[0] * factors[0],
        parts[1] * factors[1:3][:, None, None],
        parts[2] * factors[3],
        parts[3] * factors[4:6][:, None, None],
        parts[4] * factors[6],
    )


def per_device(
    hidden_in,
    out_grad,
    doc_lengths,
    norm_gains,
    w_query,
    w_keyval,
    w_out,
    w_gateup,
    w_down,
    moment_gains,
    moment_query,
    moment_keyval,
    moment_out,
    moment_gateup,
    moment_down,
    second_gains,
    second_query,
    second_keyval,
    second_out,
    second_gateup,
    second_down,
):
    tok = hidden_in.shape[1]
    width = hidden_in.shape[2]
    row_len = tok * 4
    n_o, n_z, n_x = lax.axis_size("o"), lax.axis_size("z"), lax.axis_size("x")
    n_parts = n_o * n_x
    depth = w_query.shape[0]
    part_depth = n_z * depth
    heads_wide = w_query.shape[1]
    kv_wide = w_keyval.shape[2]
    local_heads = heads_wide // HD
    local_kv = kv_wide // HD
    group_size = local_heads // local_kv
    ff_held = w_down.shape[0]
    ff_part = ff_held // n_z
    score_scale = HD ** (-0.5)
    my_part = lax.axis_index("o") * n_x + lax.axis_index("x")

    def to_parts(value):
        cut = value.reshape(tok, n_o, n_z, n_x, depth).transpose(1, 3, 0, 2, 4)
        cut = cut.reshape(n_parts, tok, part_depth)
        return jnp.concatenate(
            [
                lax.dynamic_index_in_dim(cut, my_part ^ place, 0, keepdims=False)
                for place in range(n_parts)
            ],
            axis=1,
        )

    def from_parts(value):
        cut = value.reshape(tok, n_parts, part_depth)
        cut = jnp.stack(
            [
                lax.dynamic_index_in_dim(cut, my_part ^ place, 1, keepdims=False)
                for place in range(n_parts)
            ]
        )
        cut = cut.reshape(n_o, n_x, tok, n_z, depth).transpose(2, 0, 3, 1, 4)
        return cut.reshape(tok, width)

    def gather_rows(value):
        return jnp.concatenate(
            [gather_row(exchange(value, "z", place) if place else value) for place in range(n_z)]
        )

    def scatter_rows(partials):
        total = None
        for place in range(n_z - 1, -1, -1):
            mine = scatter_row(partials[place])
            if place:
                mine = widened(exchange(rounded(mine), "z", place))
            total = mine if total is None else total + mine
        return total

    masters = (w_query, w_keyval, w_out, w_gateup, w_down)
    y_at, c_at = lax.axis_index("y"), lax.axis_index("c")
    token_blocks = [
        ((y_at ^ y_other) * 2 + (c_at ^ c_other)) * tok + jnp.arange(tok, dtype=jnp.int32)
        for c_other in range(2)
        for y_other in range(2)
    ]
    position = jnp.concatenate(token_blocks)
    segment, doc_place = doc_layout(doc_lengths[0], position)
    cosine, sine_part = rope_tables(doc_place, HD)

    attn_shard = rounded(jnp.concatenate([w_query, w_keyval[0], w_keyval[1], w_out.T], axis=1))
    attn_w = lax.all_gather(attn_shard, ("o", "z", "x"), axis=0, tiled=True)
    qkv_wide = heads_wide + 2 * kv_wide
    qkv_w, out_wt = attn_w[:, :qkv_wide], attn_w[:, qkv_wide:]

    gateup_send = rounded(w_gateup).reshape(2, depth, n_z, ff_part).transpose(2, 1, 0, 3)
    gateup_own = lax.all_to_all(
        gateup_send.reshape(n_z, depth, 2 * ff_part), "z", 0, 0, tiled=True
    ).reshape(part_depth, 2 * ff_part)
    down_own = lax.all_to_all(
        rounded(w_down).reshape(n_z, ff_part, depth), "z", 0, 0, tiled=True
    )
    gateup_w = jnp.concatenate(
        [
            exchange(gateup_own, ("o", "x"), place) if place else gateup_own
            for place in range(n_parts)
        ]
    )
    down_w = jnp.concatenate(
        [
            exchange(down_own, ("o", "x"), place) if place else down_own
            for place in range(n_parts)
        ]
    )
    down_w = down_w.transpose(1, 0, 2).reshape(ff_part, width)

    x_float = widened(hidden_in[0])
    gain_attn = norm_gains[0]
    gain_ffn = norm_gains[1]
    inv_one = lax.rsqrt(jnp.mean(x_float * x_float, axis=-1, keepdims=True) + EPS_NORM)
    normed_one = x_float * inv_one
    attn_input = gather_row(rounded(normed_one * gain_attn))
    qkv = dot_plain(attn_input, qkv_w)
    query_raw = qkv[:, :heads_wide].reshape(row_len, local_heads, HD)
    key_raw = qkv[:, heads_wide : heads_wide + kv_wide].reshape(row_len, local_kv, HD)
    values = rounded(qkv[:, heads_wide + kv_wide :]).reshape(row_len, local_kv, HD)
    queries = rounded(rotate(query_raw, cosine, sine_part)).reshape(
        row_len, local_kv, group_size, HD
    )
    key_rot = rounded(rotate(key_raw, cosine, sine_part))
    allowed = (segment[:, None] == segment[None, :]) & (position[None, :] <= position[:, None])
    scores = jnp.where(
        allowed[None, None],
        jnp.einsum("qkgd,tkd->kgqt", queries, key_rot, preferred_element_type=jnp.float32)
        * score_scale,
        NEG_FILL,
    )
    row_max = jnp.max(scores, axis=-1, keepdims=True)
    shifted = jnp.exp(scores - row_max)
    probabilities = shifted / jnp.sum(shifted, axis=-1, keepdims=True)
    prob_round = rounded(probabilities)
    context = rounded(
        jnp.einsum("kgqt,tkd->qkgd", prob_round, values, preferred_element_type=jnp.float32)
    ).reshape(row_len, heads_wide)
    mid_stream = x_float + scatter_row(rounded(dot_rows(context, out_wt)))
    inv_two = lax.rsqrt(jnp.mean(mid_stream * mid_stream, axis=-1, keepdims=True) + EPS_NORM)
    normed_two = mid_stream * inv_two

    ffn_input = gather_rows(to_parts(rounded(normed_two * gain_ffn)))
    grad_full = gather_rows(to_parts(out_grad[0]))
    gateup_pre = dot_plain(ffn_input, gateup_w)
    gate_pre, up_pre = gateup_pre[:, :ff_part], gateup_pre[:, ff_part:]
    sigmoid_gate = jax.nn.sigmoid(gate_pre)
    silu_gate = gate_pre * sigmoid_gate
    hidden_act = rounded(silu_gate * up_pre)
    ffn_out = scatter_rows(
        [
            rounded(dot_plain(hidden_act[place * row_len : (place + 1) * row_len], down_w))
            for place in range(n_z)
        ]
    )
    block_out = rounded(mid_stream + from_parts(ffn_out))[None]

    grad_hidden = dot_rows(grad_full, down_w)
    grad_gate = grad_hidden * up_pre * (sigmoid_gate * (1.0 + gate_pre * (1.0 - sigmoid_gate)))
    grad_up = grad_hidden * silu_gate
    grad_pair = jnp.concatenate([rounded(grad_gate), rounded(grad_up)], axis=1)
    grad_ffn_in = from_parts(
        scatter_rows(
            [
                rounded(dot_rows(grad_pair[place * row_len : (place + 1) * row_len], gateup_w))
                for place in range(n_z)
            ]
        )
    )
    grad_gateup_w = dot_cols(ffn_input, grad_pair).reshape(n_parts, n_z, depth, 2 * ff_part)
    grad_down_w = dot_cols(hidden_act, grad_full).reshape(ff_part, n_parts, n_z, depth)

    def to_owner(pieces):
        total = pieces[0]
        for place in range(1, n_parts):
            total = total + widened(exchange(rounded(pieces[place]), ("o", "x"), place))
        return widened(lax.all_to_all(rounded(total), "z", 0, 0, tiled=True))

    grad_gateup = (
        to_owner([grad_gateup_w[place] for place in range(n_parts)])
        .reshape(n_z, depth, 2, ff_part)
        .transpose(2, 1, 0, 3)
        .reshape(2, depth, ff_held)
    )
    grad_down = to_owner(
        [grad_down_w[:, place].transpose(1, 0, 2) for place in range(n_parts)]
    ).reshape(ff_held, depth)

    gain_grad_ffn = jnp.sum(grad_ffn_in * normed_two, axis=0)
    grad_normed_two = grad_ffn_in * gain_ffn
    grad_mid = widened(out_grad[0]) + inv_two * (
        grad_normed_two
        - normed_two * jnp.mean(grad_normed_two * normed_two, axis=-1, keepdims=True)
    )
    grad_mid_full = gather_row(rounded(grad_mid))
    grad_context = rounded(dot_plain(grad_mid_full, out_wt)).reshape(
        row_len, local_kv, group_size, HD
    )
    grad_out_wt = rounded(dot_cols(grad_mid_full, context))
    grad_out = widened(
        lax.psum_scatter(grad_out_wt, ("o", "z", "x"), scatter_dimension=0, tiled=True)
    ).T

    grad_probs = jnp.einsum(
        "qkgd,tkd->kgqt", grad_context, values, preferred_element_type=jnp.float32
    )
    inner_sum = jnp.sum(probabilities * grad_probs, axis=-1, keepdims=True)
    grad_scores = rounded(probabilities * (grad_probs - inner_sum) * score_scale)
    grad_queries = jnp.einsum(
        "kgqt,tkd->qkgd", grad_scores, key_rot, preferred_element_type=jnp.float32
    ).reshape(row_len, local_heads, HD)
    grad_keys = jnp.einsum(
        "kgqt,qkgd->tkd", grad_scores, queries, preferred_element_type=jnp.float32
    )
    grad_values = jnp.einsum(
        "kgqt,qkgd->tkd", prob_round, grad_context, preferred_element_type=jnp.float32
    )
    grad_qkv = jnp.concatenate(
        [
            rounded(unrotate(grad_queries, cosine, sine_part)).reshape(row_len, heads_wide),
            rounded(unrotate(grad_keys, cosine, sine_part)).reshape(row_len, kv_wide),
            rounded(grad_values).reshape(row_len, kv_wide),
        ],
        axis=1,
    )
    grad_qkv_w = widened(
        lax.psum_scatter(
            rounded(dot_cols(attn_input, grad_qkv)),
            ("o", "z", "x"),
            scatter_dimension=0,
            tiled=True,
        )
    )
    grad_query = grad_qkv_w[:, :heads_wide]
    grad_keyval = jnp.stack(
        [
            grad_qkv_w[:, heads_wide : heads_wide + kv_wide],
            grad_qkv_w[:, heads_wide + kv_wide :],
        ]
    )
    grad_attn_in = scatter_row(rounded(dot_rows(grad_qkv, qkv_w)))
    gain_grad_attn = jnp.sum(grad_attn_in * normed_one, axis=0)
    grad_normed_one = grad_attn_in * gain_attn
    input_grad = grad_mid + inv_one * (
        grad_normed_one
        - normed_one * jnp.mean(grad_normed_one * normed_one, axis=-1, keepdims=True)
    )

    grad_parts = (grad_query, grad_keyval, grad_out, grad_gateup, grad_down)
    moments = (moment_query, moment_keyval, moment_out, moment_gateup, moment_down)
    seconds = (second_query, second_keyval, second_out, second_gateup, second_down)
    results = [lamb_moments(grad_parts[slot], moments[slot], seconds[slot]) for slot in range(5)]
    new_moments = tuple((entry[0] for entry in results))
    new_seconds = tuple((entry[1] for entry in results))
    updates = tuple((results[slot][2] + DECAY * masters[slot] for slot in range(5)))
    packed = jnp.concatenate(
        [gain_grad_attn, gain_grad_ffn, jnp.pad(square_sums(masters), (0, 121))]
    ).reshape(-1, 128)
    packed = all_sum(packed)
    grad_gains = packed[:-1].reshape(2, width)
    weight_sq = packed[-1, :7]
    update_sq = all_sum(jnp.pad(square_sums(updates), (0, 121)).reshape(1, 128))[0, :7]
    gain_moment, gain_second, gain_direction = lamb_moments(grad_gains, moment_gains, second_gains)
    gain_update = gain_direction + DECAY * norm_gains
    weight_norms = jnp.concatenate(
        [jnp.sqrt(weight_sq), jnp.sqrt(jnp.sum(norm_gains * norm_gains, axis=1))]
    )
    update_norms = jnp.concatenate(
        [jnp.sqrt(update_sq), jnp.sqrt(jnp.sum(gain_update * gain_update, axis=1))]
    )
    trust_ratios = weight_norms / update_norms
    steps_taken = scale_parts(updates, trust_ratios[:7])
    new_parts = tuple((masters[slot] - RATE * steps_taken[slot] for slot in range(5)))
    new_gains = norm_gains - RATE * trust_ratios[7:9][:, None] * gain_update
    return (
        block_out,
        input_grad[None],
        grad_gains,
        grad_parts[0],
        grad_parts[1],
        grad_parts[2],
        grad_parts[3],
        grad_parts[4],
        new_gains,
        new_parts[0],
        new_parts[1],
        new_parts[2],
        new_parts[3],
        new_parts[4],
        gain_moment,
        new_moments[0],
        new_moments[1],
        new_moments[2],
        new_moments[3],
        new_moments[4],
        gain_second,
        new_seconds[0],
        new_seconds[1],
        new_seconds[2],
        new_seconds[3],
        new_seconds[4],
        weight_norms,
        update_norms,
        trust_ratios,
    )


def solution(mesh):
    n_dp, n_tensor = mesh.devices.shape
    split = jax.sharding.Mesh(
        mesh.devices.reshape(n_dp // 8, 4, 2, n_tensor // 2, 2), ("o", "z", "x", "y", "c")
    )
    dp, tensor = ("o", "z", "x"), ("y", "c")
    in_specs = (
        P(dp, tensor, None),
        P(dp, tensor, None),
        P(dp, None),
        P(),
        P(dp, tensor),
        P(None, dp, tensor),
        P(tensor, dp),
        P(None, dp, tensor),
        P(tensor, dp),
        P(),
        P(dp, tensor),
        P(None, dp, tensor),
        P(tensor, dp),
        P(None, dp, tensor),
        P(tensor, dp),
        P(),
        P(dp, tensor),
        P(None, dp, tensor),
        P(tensor, dp),
        P(None, dp, tensor),
        P(tensor, dp),
    )
    out_specs = (
        P(dp, tensor, None),
        P(dp, tensor, None),
        P(),
        P(dp, tensor),
        P(None, dp, tensor),
        P(tensor, dp),
        P(None, dp, tensor),
        P(tensor, dp),
        P(),
        P(dp, tensor),
        P(None, dp, tensor),
        P(tensor, dp),
        P(None, dp, tensor),
        P(tensor, dp),
        P(),
        P(dp, tensor),
        P(None, dp, tensor),
        P(tensor, dp),
        P(None, dp, tensor),
        P(tensor, dp),
        P(),
        P(dp, tensor),
        P(None, dp, tensor),
        P(tensor, dp),
        P(None, dp, tensor),
        P(tensor, dp),
        P(),
        P(),
        P(),
    )
    return jax.shard_map(
        per_device, mesh=split, in_specs=in_specs, out_specs=out_specs, check_vma=False
    )
```

time: 2040 us -> 871 us (0.43)
  waiting for transfers between devices: 1680 us -> 343 us
  starting transfers between devices: 1.81 us -> 95.1 us
  local copies, waits for them, and re-layouts: 60.5 us -> 152 us
  blocking collectives: 38.8 us -> 0 us
  other arithmetic: 81.6 us -> 118 us
    reduce_scatter x9 -> x2, waiting for transfers between devices: 1140 us -> 0.02 us  [the longest x1 0.02 us: per_device(): lax.psum_scatter(grad_out_wt, ('o', 'z', 'x'), scatter_dimension=0, tiled...]
    all_gather x9 -> x1, waiting for transfers between devices: 542 us -> 61.2 us  [per_device(): attn_w = lax.all_gather(attn_shard, ('o', 'z', 'x'), axis=0, tiled=True)]
    ppermute x0 -> x66, waiting for transfers between devices: none -> 282 us  [exchange(): lax.ppermute(value, axis, [(place, place ^ mask) for place in range(size)])]
    ppermute x0 -> x66, starting transfers between devices: none -> 67.4 us  [exchange(): lax.ppermute(value, axis, [(place, place ^ mask) for place in range(size)])]
    dot_general x17 -> x12, matrix products: 116 us -> 70.9 us  [the longest x7 28 us: dot_plain(): return jnp.dot(left_side, right_side, preferred_element_type=jnp.float32)]
    psum x1 -> x0, blocking collectives: 38.8 us -> none  [per_device(): lax.psum((gain_local, weight_sq_local), ('dp', 'tensor'))]
    reshape x0 -> x12, local copies, waits for them, and re-layouts: none -> 36.4 us  [the longest x3 19.7 us: per_device(): grad_gateup = to_owner([grad_gateup_w[place] for place in range(n_parts)]...]
    all_to_all x0 -> x4, starting transfers between devices: none -> 27.6 us  [the longest x2 17.9 us: to_owner(): return widened(lax.all_to_all(rounded(total), 'z', 0, 0, tiled=True))]
  transfers between devices with their start and end apart: 18 -> 73, of which waited for: 17 -> 19; matrix products, arithmetic and copies ran while one was open for 8% -> 34% of each run, Pallas kernels for 0% -> 0%
where the time goes in v1:
time: 871 us; the launch traced here: 860 us
  waiting for transfers between devices  343 us (39%)
  local copies, waits for them, and re-layouts  152 us (17%)
  matrix products  137 us (16%)
  other arithmetic  118 us (14%)
  starting transfers between devices  95.1 us (11%)
  between operations  15.5 us (2%)
    ppermute x66, waiting for transfers between devices, exchange(): lax.ppermute(value, axis, [(place, place ^ mask) for place in range(size)])  282 us
    unnamed x231, local copies, waits for them, and re-layouts  70 us
    ppermute x66, starting transfers between devices, exchange(): lax.ppermute(value, axis, [(place, place ^ mask) for place in range(size)])  67.4 us
    all_gather x1, waiting for transfers between devices, per_device(): attn_w = lax.all_gather(attn_shard, ('o', 'z', 'x'), axis=0, tiled=True)  61.2 us
    dot_general x7, matrix products, dot_rows(): lax.dot_general(left_side, right_side, (((1,), (1,)), ((), ())), preferre...  34.2 us
    dot_general x7, matrix products, dot_plain(): return jnp.dot(left_side, right_side, preferred_element_type=jnp.float32)  28 us
    dot_general x4, matrix products, dot_cols(): lax.dot_general(left_side, right_side, (((0,), (0,)), ((), ())), preferre...  26.1 us
    reshape x3, local copies, waits for them, and re-layouts, per_device(): grad_gateup = to_owner([grad_gateup_w[place] for place in range(n_parts)]...  19.7 us
  transfers between devices with their start and end apart: 73, of which 19 were waited for; matrix products, arithmetic and copies ran while one was open for 34% of the time, Pallas kernels for 0%

profile of v1, /device:TPU:0, one launch (start us, length us, event | category | flops | bytes accessed | tf_op | source)
XLA Modules:
  0.0 859.7 jit_solution(561263841514303418)
XLA Ops:
  23.7 5.2 all-to-all-start.1
  30.3 9.9 %collective-permute-done = bf16[128,2048]{1,0:T(8,128)(2,1)} collective-permute-done((bf16[128,2048]{1,0:T(8,128)(2,1)}, bf16[128,2048]{1,0:T(8,128)(2,1)}, u32[]{:S(2)}, u32[]{:S(2)}) %collective-permute-start) | collective-permute-done | bytes 524320 | tf_op jit(solution)/shard_map/ppermute | solution.py:112
  42.5 10.1 %collective-permute-done.30 = bf16[128,2048]{0,1:T(8,128)(2,1)S(1)} collective-permute-done((bf16[128,2048]{0,1:T(8,128)(2,1)}, bf16[128,2048]{0,1:T(8,128)(2,1)S(1)}, u32[]{:S(2)}, u32[]{:S(2)}) %collective-permute-start.30) | collective-permute-done | bytes 524320 | tf_op jit(solution)/shard_map/ppermute | solution.py:112
  53.0 4.6 copy.167
  60.7 16.3 %collective-permute-done.33 = bf16[128,2048]{0,1:T(8,128)(2,1)S(1)} collective-permute-done((bf16[128,2048]{0,1:T(8,128)(2,1)}, bf16[128,2048]{0,1:T(8,128)(2,1)S(1)}, u32[]{:S(2)}, u32[]{:S(2)}) %collective-permute-start.33) | collective-permute-done | bytes 524320 | tf_op jit(solution)/shard_map/ppermute | solution.py:112
  83.3 7.3 collective-permute-done.34
  91.8 61.2 %all-gather.2.cloned.1.call-done = bf16[2048,1280]{0,1:T(8,128)(2,1)} async-done(((bf16[256,1280]{0,1:T(8,128)(2,1)}), bf16[2048,1280]{0,1:T(8,128)(2,1)}) %all-gather.2.cloned.1.call-update) | async-done | bytes 5242896 | tf_op jit(solution)/shard_map/all_gather | solution.py:251
  153.0 4.4 fusion.16
  160.6 5.3 fusion.126
  165.9 4.2 fusion.37
  181.6 4.5 all-to-all-start
  197.5 8.5 collective-permute-done.3
  220.1 12.3 %collective-permute-done.6 = bf16[128,2048]{0,1:T(8,128)(2,1)} collective-permute-done((bf16[128,2048]{0,1:T(8,128)(2,1)}, bf16[128,2048]{0,1:T(8,128)(2,1)}, u32[]{:S(2)}, u32[]{:S(2)}) %collective-permute-start.6) | collective-permute-done | bytes 524320 | tf_op jit(solution)/shard_map/ppermute | solution.py:112
  235.2 34.2 %collective-permute-done.9 = bf16[128,2048]{0,1:T(8,128)(2,1)} collective-permute-done((bf16[128,2048]{0,1:T(8,128)(2,1)}, bf16[128,2048]{0,1:T(8,128)(2,1)}, u32[]{:S(2)}, u32[]{:S(2)}) %collective-permute-start.9) | collective-permute-done | bytes 524320 | tf_op jit(solution)/shard_map/ppermute | solution.py:112
  285.3 8.6 %collective-permute-done.13 = bf16[128,2048]{0,1:T(8,128)(2,1)S(1)} collective-permute-done((bf16[128,2048]{0,1:T(8,128)(2,1)}, bf16[128,2048]{0,1:T(8,128)(2,1)S(1)}, u32[]{:S(2)}, u32[]{:S(2)}) %collective-permute-start.13) | collective-permute-done | bytes 524320 | tf_op jit(solution)/shard_map/ppermute | solution.py:112
  311.4 14.5 %collective-permute-done.15 = bf16[1024,1024]{1,0:T(8,128)(2,1)S(1)} collective-permute-done((bf16[1024,1024]{1,0:T(8,128)(2,1)}, bf16[1024,1024]{1,0:T(8,128)(2,1)S(1)}, u32[]{:S(2)}, u32[]{:S(2)}) %collective-permute-start.15) | collective-permute-done | bytes 2097184 | tf_op jit(solution)/shard_map/ppermute | solution.py:112
  325.9 14.9 %fusion.114 = f32[2048,1024]{0,1:T(8,128)} fusion(bf16[2048,2048]{0,1:T(8,128)(2,1)} %constant_dynamic-update-slice_fusion, bf16[1024,1024]{1,0:T(8,128)(2,1)S(1)} %collective-permute-done.15, bf16[1024,1024]{1,0:T(8,128)(2,1)} %bitcast.31), kind=kOutput, calls=%fused_computation.311 | convolution fusion | flops 8598323200 | bytes 20971520 | tf_op jit(solution)/shard_map/dot_general | solution.py:90
  340.8 10.0 %multiply_convert_fusion = (bf16[2048,512]{0,1:T(8,128)(2,1)}, bf16[2048,512]{0,1:T(8,128)(2,1)}, bf16[2048,512]{0,1:T(8,128)(2,1)S(1)}) fusion(f32[2048,1024]{0,1:T(8,128)} %fusion.114, bf16[2048,2048]{0,1:T(8,128)(2,1)S(1)} %bitcast.273, bf16[512,2048]{0,1:T(8,128)(2,1)S(1)} %bitcast.241), kind=kOutput, calls=%fused_computation.29 | convolution fusion | flops 4310695936 | bytes 25165824 | tf_op jit(solution)/shard_map/dot_general | solution.py:94
  352.1 6.3 fusion.128
  358.4 6.0 reshape.381
  368.2 12.2 %fusion.7 = f32[2048,1024]{1,0:T(8,128)S(1)} fusion(bf16[2048,2048]{0,1:T(8,128)(2,1)} %constant_dynamic-update-slice_fusion, bf16[2048,512]{0,1:T(8,128)(2,1)S(1)} %copy-done.92, bf16[2048,512]{0,1:T(8,128)(2,1)} %get-tuple-element.214), kind=kOutput, calls=%fused_computation.22 | convolution fusion | flops 8598323200 | bytes 20971520 | tf_op jit(solution)/shard_map/dot_general | solution.py:100
  385.9 4.0 convolution_convert_fusion.1
  390.1 4.0 convolution_convert_fusion.2
  401.7 5.3 convolution_convert_fusion.4
  417.3 20.5 %collective-permute-done.46 = bf16[128,2048]{1,0:T(8,128)(2,1)S(1)} collective-permute-done((bf16[128,2048]{1,0:T(8,128)(2,1)S(1)}, bf16[128,2048]{1,0:T(8,128)(2,1)S(1)}, u32[]{:S(2)}, u32[]{:S(2)}) %collective-permute-start.46) | collective-permute-done | bytes 524320 | tf_op jit(solution)/shard_map/ppermute | solution.py:112
  438.0 11.0 %collective-permute-done.43 = bf16[128,2048]{1,0:T(8,128)(2,1)S(1)} collective-permute-done((bf16[128,2048]{1,0:T(8,128)(2,1)S(1)}, bf16[128,2048]{1,0:T(8,128)(2,1)S(1)}, u32[]{:S(2)}, u32[]{:S(2)}) %collective-permute-start.43) | collective-permute-done | bytes 524320 | tf_op jit(solution)/shard_map/ppermute | solution.py:112
  449.2 10.1 %collective-permute-done.40 = bf16[128,2048]{1,0:T(8,128)(2,1)S(1)} collective-permute-done((bf16[128,2048]{1,0:T(8,128)(2,1)S(1)}, bf16[128,2048]{1,0:T(8,128)(2,1)S(1)}, u32[]{:S(2)}, u32[]{:S(2)}) %collective-permute-start.40) | collective-permute-done | bytes 524320 | tf_op jit(solution)/shard_map/ppermute | solution.py:112
  469.0 14.7 %collective-permute-done.44 = bf16[128,2048]{1,0:T(8,128)(2,1)S(1)} collective-permute-done((bf16[128,2048]{1,0:T(8,128)(2,1)S(1)}, bf16[128,2048]{1,0:T(8,128)(2,1)S(1)}, u32[]{:S(2)}, u32[]{:S(2)}) %collective-permute-start.44) | collective-permute-done | bytes 524320 | tf_op jit(solution)/shard_map/ppermute | solution.py:112
  495.0 11.3 %collective-permute-done.50 = bf16[128,2048]{1,0:T(8,128)(2,1)S(1)} collective-permute-done((bf16[128,2048]{1,0:T(8,128)(2,1)S(1)}, bf16[128,2048]{1,0:T(8,128)(2,1)S(1)}, u32[]{:S(2)}, u32[]{:S(2)}) %collective-permute-start.50) | collective-permute-done | bytes 524320 | tf_op jit(solution)/shard_map/ppermute | solution.py:112
  527.3 13.5 %all-to-all-start.3 = ((bf16[4,512,256]{2,1,0:T(8,128)(2,1)}), bf16[4,512,256]{2,1,0:T(8,128)(2,1)}, u32[]{:S(2)}, u32[]{:S(2)}) async-start(bf16[4,512,256]{2,1,0:T(8,128)(2,1)} %fusion.20), calls=%async_computation.5 | async-start | bytes 2097152 | tf_op jit(solution)/shard_map/all_to_all | solution.py:342
  545.1 4.6 fusion.127
  549.7 13.9 %fusion.43 = f32[512,2,64]{0,2,1:T(8,128)S(1)} fusion(f32[2,512,512,4]{2,1,3,0:T(8,128)} %fusion.127, bf16[512,2,4,32]{0,3,2,1:T(8,128)(2,1)} %bitcast.262, bf16[512,2,4,32]{0,3,2,1:T(8,128)(2,1)} %bitcast.260, f32[2,4,512,512]{2,3,1,0:T(8,128)} %get-tuple-element.260, f32[2,4,512]{2,1,0:T(4,128)} %copy-done.96), kind=kOutput, calls=%fused_computation.103 | convolution fusion | flops 284168704 | bytes 17580032 | tf_op jit(solution)/shard_map/kgqt,qkgd->tkd/dot_general | solution.py:377
  563.7 15.2 %fusion.14 = f32[2,64,4,512]{3,1,2,0:T(8,128)} fusion(f32[2,512,512,4]{2,1,3,0:T(8,128)} %fusion.127, bf16[512,2,32]{0,2,1:T(8,128)(2,1)} %copy-done.71, bf16[512,2,32]{0,2,1:T(8,128)(2,1)} %copy-done.70, f32[2,4,512,512]{2,3,1,0:T(8,128)} %get-tuple-element.260, f32[2,4,512]{2,1,0:T(4,128)} %copy-done.96), kind=kOutput, calls=%fused_computation.40 | convolution fusion | flops 283382272 | bytes 17973248 | tf_op jit(solution)/shard_map/kgqt,tkd->qkgd/dot_general | solution.py:374
  580.3 4.9 fusion.44
  586.1 5.0 convolution_convert_fusion
  595.6 5.6 add_convert_fusion
  601.2 4.5 all-to-all-start.2
  629.1 88.8 %collective-permute-done.22 = bf16[128,2048]{1,0:T(8,128)(2,1)} collective-permute-done((bf16[128,2048]{1,0:T(8,128)(2,1)}, bf16[128,2048]{1,0:T(8,128)(2,1)}, u32[]{:S(2)}, u32[]{:S(2)}) %collective-permute-start.22) | collective-permute-done | bytes 524320 | tf_op jit(solution)/shard_map/ppermute | solution.py:112
  727.8 5.9 multiply_reduce_fusion
  738.4 6.6 reshape.397
  744.9 6.9 copy.208
  751.8 6.2 reshape.392
  758.0 9.6 %multiply_add_fusion.1 = (f32[2,256,2048]{2,1,0:T(8,128)S(1)}, f32[2,256,2048]{2,1,0:T(8,128)}, f32[2,256,2048]{2,1,0:T(8,128)}) fusion(f32[2,256,2048]{2,1,0:T(8,128)} %param.29, f32[2,256,2048]{2,1,0:T(8,128)} %reshape.392, f32[2,256,2048]{2,1,0:T(8,128)} %param.41, f32[2,256,2048]{2,1,0:T(8,128)} %param.35), kind=kLoop, calls=%fused_computation.27 | loop fusion | flops 10485760 | bytes 29360128 | tf_op jit(solution)/shard_map/add | solution.py:420
  782.3 4.5 stack.99
  786.8 4.6 stack.88
  802.9 10.7 %collective-permute-start.64 = (f32[1,128]{1,0:T(1,128)S(1)}, f32[1,128]{1,0:T(1,128)S(1)}, u32[]{:S(2)}, u32[]{:S(2)}) collective-permute-start(f32[1,128]{1,0:T(1,128)S(1)} %add.403), channel_id=1, source_target_pairs={{0,8},{8,0},{16,24},{24,16},{1,9},{9,1},{17,25},{25,17},{2,10},{10... | collective-permute-start | bytes 1544 | tf_op jit(solution)/shard_map/ppermute | solution.py:112
  815.1 4.0 fusion.52
  840.6 6.9 multiply_subtract_fusion
  (519 shorter events, 281.0 us)
Async XLA Ops:
  7.2 145.8 %all-gather.2.cloned.1.call-start = ((), (), s32[]{:S(2)}) async-start(), calls=%async_computation.6 | async-start | bytes 5898240 | tf_op jit(solution)/shard_map/all_gather | solution.py:251
  13.7 63.7 %collective-permute-start.28 = (bf16[128,2048]{0,1:T(8,128)(2,1)}, bf16[128,2048]{0,1:T(8,128)(2,1)S(1)}, u32[]{:S(2)}, u32[]{:S(2)}) collective-permute-start(bf16[128,2048]{0,1:T(8,128)(2,1)} %get-tuple-element.230), channel_id=1, source_target_pairs={{0,2},{2,0},{1,3},{3,1},{4,6},{6,4},{5,7},{7,5},{8,10},{10,8},{9,1... | collective-permute-start | bytes 1572872 | tf_op jit(solution)/shard_map/ppermute | solution.py:112
  16.7 35.9 %collective-permute-start.30 = (bf16[128,2048]{0,1:T(8,128)(2,1)}, bf16[128,2048]{0,1:T(8,128)(2,1)S(1)}, u32[]{:S(2)}, u32[]{:S(2)}) collective-permute-start(bf16[128,2048]{0,1:T(8,128)(2,1)} %get-tuple-element.230), channel_id=1, source_target_pairs={{0,8},{8,0},{16,24},{24,16},{1,9},{9,1},{17,25},{25,17},{2,10},{10... | collective-permute-start | bytes 1572872 | tf_op jit(solution)/shard_map/ppermute | solution.py:112
  18.3 58.7 %collective-permute-start.33 = (bf16[128,2048]{0,1:T(8,128)(2,1)}, bf16[128,2048]{0,1:T(8,128)(2,1)S(1)}, u32[]{:S(2)}, u32[]{:S(2)}) collective-permute-start(bf16[128,2048]{0,1:T(8,128)(2,1)} %get-tuple-element.230), channel_id=1, source_target_pairs={{0,16},{8,24},{16,0},{24,8},{1,17},{9,25},{17,1},{25,9},{2,18},{10... | collective-permute-start | bytes 1572872 | tf_op jit(solution)/shard_map/ppermute | solution.py:112
  20.9 57.7 %collective-permute-start.36 = (bf16[128,2048]{0,1:T(8,128)(2,1)}, bf16[128,2048]{0,1:T(8,128)(2,1)S(1)}, u32[]{:S(2)}, u32[]{:S(2)}) collective-permute-start(bf16[128,2048]{0,1:T(8,128)(2,1)} %get-tuple-element.230), channel_id=1, source_target_pairs={{0,24},{8,16},{16,8},{24,0},{1,25},{9,17},{17,9},{25,1},{2,26},{10... | collective-permute-start | bytes 1572872 | tf_op jit(solution)/shard_map/ppermute | solution.py:112
  23.7 157.9 %all-to-all-start.1 = ((bf16[4,512,256]{2,1,0:T(8,128)(2,1)}), bf16[4,512,256]{2,1,0:T(8,128)(2,1)}, u32[]{:S(2)}, u32[]{:S(2)}) async-start(bf16[4,512,256]{2,1,0:T(8,128)(2,1)} %bitcast.32), calls=%async_computation.1 | async-start | bytes 2097152 | tf_op jit(solution)/shard_map/all_to_all | solution.py:259
  42.5 49.3 %collective-permute-start.1 = (bf16[256,2048]{1,0:T(8,128)(2,1)}, bf16[256,2048]{1,0:T(8,128)(2,1)}, u32[]{:S(2)}, u32[]{:S(2)}) collective-permute-start(bf16[256,2048]{1,0:T(8,128)(2,1)} %pad_maximum_fusion.5), channel_id=1, source_target_pairs={{0,1},{1,0},{2,3},{3,2},{4,5},{5,4},{6,7},{7,6},{8,9},{9,8},{10,11... | collective-permute-start | bytes 3145736 | tf_op jit(solution)/shard_map/ppermute | solution.py:112
  52.6 28.4 %collective-permute-start.31 = (bf16[128,2048]{0,1:T(8,128)(2,1)S(1)}, bf16[128,2048]{0,1:T(8,128)(2,1)}, u32[]{:S(2)}, u32[]{:S(2)}) collective-permute-start(bf16[128,2048]{0,1:T(8,128)(2,1)S(1)} %collective-permute-done.30), channel_id=1, source_target_pairs={{0,2},{2,0},{1,3},{3,1},{4,6},{6,4},{5,7},{7,5},{8,10},{10,8},{9,1... | collective-permute-start | bytes 1572872 | tf_op jit(solution)/shard_map/ppermute | solution.py:112
  78.6 97.7 %collective-permute-start.29 = (bf16[256,2048]{0,1:T(8,128)(2,1)}, bf16[256,2048]{0,1:T(8,128)(2,1)}, u32[]{:S(2)}, u32[]{:S(2)}) collective-permute-start(bf16[256,2048]{0,1:T(8,128)(2,1)} %pad_maximum_fusion.10), channel_id=1, source_target_pairs={{0,1},{1,0},{2,3},{3,2},{4,5},{5,4},{6,7},{7,6},{8,9},{9,8},{10,11... | collective-permute-start | bytes 3145736 | tf_op jit(solution)/shard_map/ppermute | solution.py:112
  78.6 94.8 %collective-permute-start.37 = (bf16[128,2048]{0,1:T(8,128)(2,1)S(1)}, bf16[128,2048]{0,1:T(8,128)(2,1)}, u32[]{:S(2)}, u32[]{:S(2)}) collective-permute-start(bf16[128,2048]{0,1:T(8,128)(2,1)S(1)} %collective-permute-done.36), channel_id=1, source_target_pairs={{0,2},{2,0},{1,3},{3,1},{4,6},{6,4},{5,7},{7,5},{8,10},{10,8},{9,1... | collective-permute-start | bytes 1572872 | tf_op jit(solution)/shard_map/ppermute | solution.py:112
  83.1 104.7 %collective-permute-start.32 = (bf16[256,2048]{0,1:T(8,128)(2,1)}, bf16[256,2048]{0,1:T(8,128)(2,1)}, u32[]{:S(2)}, u32[]{:S(2)}) collective-permute-start(bf16[256,2048]{0,1:T(8,128)(2,1)} %pad_maximum_fusion.11), channel_id=1, source_target_pairs={{0,1},{1,0},{2,3},{3,2},{4,5},{5,4},{6,7},{7,6},{8,9},{9,8},{10,11... | collective-permute-start | bytes 3145736 | tf_op jit(solution)/shard_map/ppermute | solution.py:112
  91.8 103.4 %collective-permute-start.35 = (bf16[256,2048]{0,1:T(8,128)(2,1)}, bf16[256,2048]{0,1:T(8,128)(2,1)}, u32[]{:S(2)}, u32[]{:S(2)}) collective-permute-start(bf16[256,2048]{0,1:T(8,128)(2,1)} %pad_maximum_fusion.12), channel_id=1, source_target_pairs={{0,1},{1,0},{2,3},{3,2},{4,5},{5,4},{6,7},{7,6},{8,9},{9,8},{10,11... | collective-permute-start | bytes 3145736 | tf_op jit(solution)/shard_map/ppermute | solution.py:112
  176.3 41.0 %collective-permute-start.38 = (bf16[256,2048]{0,1:T(8,128)(2,1)}, bf16[256,2048]{0,1:T(8,128)(2,1)}, u32[]{:S(2)}, u32[]{:S(2)}) collective-permute-start(bf16[256,2048]{0,1:T(8,128)(2,1)} %pad_maximum_fusion.13), channel_id=1, source_target_pairs={{0,1},{1,0},{2,3},{3,2},{4,5},{5,4},{6,7},{7,6},{8,9},{9,8},{10,11... | collective-permute-start | bytes 3145736 | tf_op jit(solution)/shard_map/ppermute | solution.py:112
  181.6 93.5 %all-to-all-start = ((bf16[4,256,1024]{1,2,0:T(8,128)(2,1)}), bf16[4,256,1024]{1,2,0:T(8,128)(2,1)}, u32[]{:S(2)}, u32[]{:S(2)}) async-start(bf16[4,256,1024]{1,2,0:T(8,128)(2,1)} %bitcast.237), calls=%async_computation | async-start | bytes 4194304 | tf_op jit(solution)/shard_map/all_to_all | solution.py:256
  186.1 586.3 %reduce-scatter.5.cloned.1.call-start = ((), (), s32[]{:S(2)}) async-start(), calls=%async_computation.8 | async-start | bytes 2359296 | tf_op jit(solution)/shard_map/reduce_scatter | solution.py:366
  186.1 84.9 %collective-permute-start.16 = (bf16[4,512,256]{2,1,0:T(8,128)(2,1)}, bf16[4,512,256]{2,1,0:T(8,128)(2,1)}, u32[]{:S(2)}, u32[]{:S(2)}) collective-permute-start(bf16[4,512,256]{2,1,0:T(8,128)(2,1)} %all-to-all-done.1), channel_id=1, source_target_pairs={{0,4},{4,0},{1,5},{5,1},{2,6},{6,2},{3,7},{7,3},{8,12},{12,8},{9,1... | collective-permute-start | bytes 3145736 | tf_op jit(solution)/shard_map/ppermute | solution.py:112
  209.1 25.0 %collective-permute-start.4 = (bf16[128,2048]{0,1:T(8,128)(2,1)}, bf16[128,2048]{0,1:T(8,128)(2,1)S(1)}, u32[]{:S(2)}, u32[]{:S(2)}) collective-permute-start(bf16[128,2048]{0,1:T(8,128)(2,1)} %get-tuple-element.234), channel_id=1, source_target_pairs={{0,2},{2,0},{1,3},{3,1},{4,6},{6,4},{5,7},{7,5},{8,10},{10,8},{9,1... | collective-permute-start | bytes 1572872 | tf_op jit(solution)/shard_map/ppermute | solution.py:112
  210.5 21.9 %collective-permute-start.6 = (bf16[128,2048]{0,1:T(8,128)(2,1)}, bf16[128,2048]{0,1:T(8,128)(2,1)}, u32[]{:S(2)}, u32[]{:S(2)}) collective-permute-start(bf16[128,2048]{0,1:T(8,128)(2,1)} %get-tuple-element.234), channel_id=1, source_target_pairs={{0,8},{8,0},{16,24},{24,16},{1,9},{9,1},{17,25},{25,17},{2,10},{10... | collective-permute-start | bytes 1572872 | tf_op jit(solution)/shard_map/ppermute | solution.py:112
  213.0 56.4 %collective-permute-start.9 = (bf16[128,2048]{0,1:T(8,128)(2,1)}, bf16[128,2048]{0,1:T(8,128)(2,1)}, u32[]{:S(2)}, u32[]{:S(2)}) collective-permute-start(bf16[128,2048]{0,1:T(8,128)(2,1)} %get-tuple-element.234), channel_id=1, source_target_pairs={{0,16},{8,24},{16,0},{24,8},{1,17},{9,25},{17,1},{25,9},{2,18},{10... | collective-permute-start | bytes 1572872 | tf_op jit(solution)/shard_map/ppermute | solution.py:112
  217.3 63.3 %collective-permute-start.12 = (bf16[128,2048]{0,1:T(8,128)(2,1)}, bf16[128,2048]{0,1:T(8,128)(2,1)}, u32[]{:S(2)}, u32[]{:S(2)}) collective-permute-start(bf16[128,2048]{0,1:T(8,128)(2,1)} %get-tuple-element.234), channel_id=1, source_target_pairs={{0,24},{8,16},{16,8},{24,0},{1,25},{9,17},{17,9},{25,1},{2,26},{10... | collective-permute-start | bytes 1572872 | tf_op jit(solution)/shard_map/ppermute | solution.py:112
  232.4 49.6 %collective-permute-start.7 = (bf16[128,2048]{0,1:T(8,128)(2,1)}, bf16[128,2048]{0,1:T(8,128)(2,1)}, u32[]{:S(2)}, u32[]{:S(2)}) collective-permute-start(bf16[128,2048]{0,1:T(8,128)(2,1)} %collective-permute-done.6), channel_id=1, source_target_pairs={{0,2},{2,0},{1,3},{3,1},{4,6},{6,4},{5,7},{7,5},{8,10},{10,8},{9,1... | collective-permute-start | bytes 1572872 | tf_op jit(solution)/shard_map/ppermute | solution.py:112
  235.2 60.0 %collective-permute-start.5 = (bf16[256,2048]{0,1:T(8,128)(2,1)}, bf16[256,2048]{0,1:T(8,128)(2,1)}, u32[]{:S(2)}, u32[]{:S(2)}) collective-permute-start(bf16[256,2048]{0,1:T(8,128)(2,1)} %pad_maximum_fusion.6), channel_id=1, source_target_pairs={{0,1},{1,0},{2,3},{3,2},{4,5},{5,4},{6,7},{7,6},{8,9},{9,8},{10,11... | collective-permute-start | bytes 3145736 | tf_op jit(solution)/shard_map/ppermute | solution.py:112
  279.1 46.8 %collective-permute-start.15 = (bf16[1024,1024]{1,0:T(8,128)(2,1)}, bf16[1024,1024]{1,0:T(8,128)(2,1)S(1)}, u32[]{:S(2)}, u32[]{:S(2)}) collective-permute-start(bf16[1024,1024]{1,0:T(8,128)(2,1)} %bitcast.31), channel_id=1, source_target_pairs={{0,4},{4,0},{1,5},{5,1},{2,6},{6,2},{3,7},{7,3},{8,12},{12,8},{9,1... | collective-permute-start | bytes 6291464 | tf_op jit(solution)/shard_map/ppermute | solution.py:112
  408.2 84.1 %collective-permute-start.26 = (bf16[256,2048]{1,0:T(8,128)(2,1)}, bf16[256,2048]{1,0:T(8,128)(2,1)}, u32[]{:S(2)}, u32[]{:S(2)}) collective-permute-start(bf16[256,2048]{1,0:T(8,128)(2,1)} %slice.419), channel_id=1, source_target_pairs={{0,1},{1,0},{2,3},{3,2},{4,5},{5,4},{6,7},{7,6},{8,9},{9,8},{10,11... | collective-permute-start | bytes 3145736 | tf_op jit(solution)/shard_map/ppermute | solution.py:112
  411.7 56.8 %collective-permute-start.49 = (bf16[128,2048]{1,0:T(8,128)(2,1)S(1)}, bf16[128,2048]{1,0:T(8,128)(2,1)S(1)}, u32[]{:S(2)}, u32[]{:S(2)}) collective-permute-start(bf16[128,2048]{1,0:T(8,128)(2,1)S(1)} %slice.620), channel_id=1, source_target_pairs={{0,2},{2,0},{1,3},{3,1},{4,6},{6,4},{5,7},{7,5},{8,10},{10,8},{9,1... | collective-permute-start | bytes 1572872 | tf_op jit(solution)/shard_map/ppermute | solution.py:112
  412.6 25.2 %collective-permute-start.46 = (bf16[128,2048]{1,0:T(8,128)(2,1)S(1)}, bf16[128,2048]{1,0:T(8,128)(2,1)S(1)}, u32[]{:S(2)}, u32[]{:S(2)}) collective-permute-start(bf16[128,2048]{1,0:T(8,128)(2,1)S(1)} %slice.621), channel_id=1, source_target_pairs={{0,2},{2,0},{1,3},{3,1},{4,6},{6,4},{5,7},{7,5},{8,10},{10,8},{9,1... | collective-permute-start | bytes 1572872 | tf_op jit(solution)/shard_map/ppermute | solution.py:112
  414.7 34.3 %collective-permute-start.43 = (bf16[128,2048]{1,0:T(8,128)(2,1)S(1)}, bf16[128,2048]{1,0:T(8,128)(2,1)S(1)}, u32[]{:S(2)}, u32[]{:S(2)}) collective-permute-start(bf16[128,2048]{1,0:T(8,128)(2,1)S(1)} %slice.622), channel_id=1, source_target_pairs={{0,2},{2,0},{1,3},{3,1},{4,6},{6,4},{5,7},{7,5},{8,10},{10,8},{9,1... | collective-permute-start | bytes 1572872 | tf_op jit(solution)/shard_map/ppermute | solution.py:112
  415.6 43.7 %collective-permute-start.40 = (bf16[128,2048]{1,0:T(8,128)(2,1)S(1)}, bf16[128,2048]{1,0:T(8,128)(2,1)S(1)}, u32[]{:S(2)}, u32[]{:S(2)}) collective-permute-start(bf16[128,2048]{1,0:T(8,128)(2,1)S(1)} %slice.623), channel_id=1, source_target_pairs={{0,2},{2,0},{1,3},{3,1},{4,6},{6,4},{5,7},{7,5},{8,10},{10,8},{9,1... | collective-permute-start | bytes 1572872 | tf_op jit(solution)/shard_map/ppermute | solution.py:112
  437.9 30.6 %collective-permute-start.47 = (bf16[128,2048]{1,0:T(8,128)(2,1)S(1)}, bf16[128,2048]{1,0:T(8,128)(2,1)S(1)}, u32[]{:S(2)}, u32[]{:S(2)}) collective-permute-start(bf16[128,2048]{1,0:T(8,128)(2,1)S(1)} %fusion.65), channel_id=1, source_target_pairs={{0,8},{8,0},{16,24},{24,16},{1,9},{9,1},{17,25},{25,17},{2,10},{10... | collective-permute-start | bytes 1572872 | tf_op jit(solution)/shard_map/ppermute | solution.py:112
  449.2 34.5 %collective-permute-start.44 = (bf16[128,2048]{1,0:T(8,128)(2,1)S(1)}, bf16[128,2048]{1,0:T(8,128)(2,1)S(1)}, u32[]{:S(2)}, u32[]{:S(2)}) collective-permute-start(bf16[128,2048]{1,0:T(8,128)(2,1)S(1)} %fusion.66), channel_id=1, source_target_pairs={{0,16},{8,24},{16,0},{24,8},{1,17},{9,25},{17,1},{25,9},{2,18},{10... | collective-permute-start | bytes 1572872 | tf_op jit(solution)/shard_map/ppermute | solution.py:112
  459.5 24.2 %collective-permute-start.41 = (bf16[128,2048]{1,0:T(8,128)(2,1)S(1)}, bf16[128,2048]{1,0:T(8,128)(2,1)S(1)}, u32[]{:S(2)}, u32[]{:S(2)}) collective-permute-start(bf16[128,2048]{1,0:T(8,128)(2,1)S(1)} %fusion.67), channel_id=1, source_target_pairs={{0,24},{8,16},{16,8},{24,0},{1,25},{9,17},{17,9},{25,1},{2,26},{10... | collective-permute-start | bytes 1572872 | tf_op jit(solution)/shard_map/ppermute | solution.py:112
  468.5 38.6 %collective-permute-start.23 = (bf16[256,2048]{1,0:T(8,128)(2,1)}, bf16[256,2048]{1,0:T(8,128)(2,1)}, u32[]{:S(2)}, u32[]{:S(2)}) collective-permute-start(bf16[256,2048]{1,0:T(8,128)(2,1)} %slice.414), channel_id=1, source_target_pairs={{0,1},{1,0},{2,3},{3,2},{4,5},{5,4},{6,7},{7,6},{8,9},{9,8},{10,11... | collective-permute-start | bytes 3145736 | tf_op jit(solution)/shard_map/ppermute | solution.py:112
  468.5 41.4 %collective-permute-start.20 = (bf16[256,2048]{1,0:T(8,128)(2,1)}, bf16[256,2048]{1,0:T(8,128)(2,1)}, u32[]{:S(2)}, u32[]{:S(2)}) collective-permute-start(bf16[256,2048]{1,0:T(8,128)(2,1)} %slice.409), channel_id=1, source_target_pairs={{0,1},{1,0},{2,3},{3,2},{4,5},{5,4},{6,7},{7,6},{8,9},{9,8},{10,11... | collective-permute-start | bytes 3145736 | tf_op jit(solution)/shard_map/ppermute | solution.py:112
  483.6 34.9 %collective-permute-start.17 = (bf16[256,2048]{1,0:T(8,128)(2,1)}, bf16[256,2048]{1,0:T(8,128)(2,1)}, u32[]{:S(2)}, u32[]{:S(2)}) collective-permute-start(bf16[256,2048]{1,0:T(8,128)(2,1)} %slice.404), channel_id=1, source_target_pairs={{0,1},{1,0},{2,3},{3,2},{4,5},{5,4},{6,7},{7,6},{8,9},{9,8},{10,11... | collective-permute-start | bytes 3145736 | tf_op jit(solution)/shard_map/ppermute | solution.py:112
  483.6 40.0 %collective-permute-start.60 = (bf16[4,512,256]{2,1,0:T(8,128)(2,1)}, bf16[4,512,256]{2,1,0:T(8,128)(2,1)}, u32[]{:S(2)}, u32[]{:S(2)}) collective-permute-start(bf16[4,512,256]{2,1,0:T(8,128)(2,1)} %bitcast.233), channel_id=1, source_target_pairs={{0,4},{4,0},{1,5},{5,1},{2,6},{6,2},{3,7},{7,3},{8,12},{12,8},{9,1... | collective-permute-start | bytes 3145736 | tf_op jit(solution)/shard_map/ppermute | solution.py:112
  506.4 89.2 %collective-permute-start.59 = (bf16[4,256,1024]{2,1,0:T(8,128)(2,1)}, bf16[4,256,1024]{2,1,0:T(8,128)(2,1)}, u32[]{:S(2)}, u32[]{:S(2)}) collective-permute-start(bf16[4,256,1024]{2,1,0:T(8,128)(2,1)} %bitcast.80), channel_id=1, source_target_pairs={{0,4},{4,0},{1,5},{5,1},{2,6},{6,2},{3,7},{7,3},{8,12},{12,8},{9,1... | collective-permute-start | bytes 6291464 | tf_op jit(solution)/shard_map/ppermute | solution.py:112
  509.9 119.2 %collective-permute-start.27 = (bf16[128,2048]{1,0:T(8,128)(2,1)}, bf16[128,2048]{1,0:T(8,128)(2,1)}, u32[]{:S(2)}, u32[]{:S(2)}) collective-permute-start(bf16[128,2048]{1,0:T(8,128)(2,1)} %slice.624), channel_id=1, source_target_pairs={{0,2},{2,0},{1,3},{3,1},{4,6},{6,4},{5,7},{7,5},{8,10},{10,8},{9,1... | collective-permute-start | bytes 1572872 | tf_op jit(solution)/shard_map/ppermute | solution.py:112
  514.2 77.0 %collective-permute-start.24 = (bf16[128,2048]{1,0:T(8,128)(2,1)}, bf16[128,2048]{1,0:T(8,128)(2,1)}, u32[]{:S(2)}, u32[]{:S(2)}) collective-permute-start(bf16[128,2048]{1,0:T(8,128)(2,1)} %slice.625), channel_id=1, source_target_pairs={{0,2},{2,0},{1,3},{3,1},{4,6},{6,4},{5,7},{7,5},{8,10},{10,8},{9,1... | collective-permute-start | bytes 1572872 | tf_op jit(solution)/shard_map/ppermute | solution.py:112
  518.5 87.1 %collective-permute-start.21 = (bf16[128,2048]{1,0:T(8,128)(2,1)}, bf16[128,2048]{1,0:T(8,128)(2,1)}, u32[]{:S(2)}, u32[]{:S(2)}) collective-permute-start(bf16[128,2048]{1,0:T(8,128)(2,1)} %slice.626), channel_id=1, source_target_pairs={{0,2},{2,0},{1,3},{3,1},{4,6},{6,4},{5,7},{7,5},{8,10},{10,8},{9,1... | collective-permute-start | bytes 1572872 | tf_op jit(solution)/shard_map/ppermute | solution.py:112
  523.6 87.3 %collective-permute-start.18 = (bf16[128,2048]{1,0:T(8,128)(2,1)}, bf16[128,2048]{1,0:T(8,128)(2,1)}, u32[]{:S(2)}, u32[]{:S(2)}) collective-permute-start(bf16[128,2048]{1,0:T(8,128)(2,1)} %slice.627), channel_id=1, source_target_pairs={{0,2},{2,0},{1,3},{3,1},{4,6},{6,4},{5,7},{7,5},{8,10},{10,8},{9,1... | collective-permute-start | bytes 1572872 | tf_op jit(solution)/shard_map/ppermute | solution.py:112
  527.3 73.8 %all-to-all-start.3 = ((bf16[4,512,256]{2,1,0:T(8,128)(2,1)}), bf16[4,512,256]{2,1,0:T(8,128)(2,1)}, u32[]{:S(2)}, u32[]{:S(2)}) async-start(bf16[4,512,256]{2,1,0:T(8,128)(2,1)} %fusion.20), calls=%async_computation.5 | async-start | bytes 2097152 | tf_op jit(solution)/shard_map/all_to_all | solution.py:342
  540.8 235.0 %reduce-scatter.3.cloned.1.call-start = ((), (), s32[]{:S(2)}) async-start(), calls=%async_computation.7 | async-start | bytes 3538944 | tf_op jit(solution)/shard_map/reduce_scatter | solution.py:392
  593.5 35.6 %collective-permute-start.25 = (bf16[128,2048]{1,0:T(8,128)(2,1)}, bf16[128,2048]{1,0:T(8,128)(2,1)}, u32[]{:S(2)}, u32[]{:S(2)}) collective-permute-start(bf16[128,2048]{1,0:T(8,128)(2,1)} %fusion.69), channel_id=1, source_target_pairs={{0,8},{8,0},{16,24},{24,16},{1,9},{9,1},{17,25},{25,17},{2,10},{10... | collective-permute-start | bytes 1572872 | tf_op jit(solution)/shard_map/ppermute | solution.py:112
  601.2 137.2 %all-to-all-start.2 = ((bf16[4,256,1024]{2,1,0:T(8,128)(2,1)}), bf16[4,256,1024]{2,1,0:T(8,128)(2,1)}, u32[]{:S(2)}, u32[]{:S(2)}) async-start(bf16[4,256,1024]{2,1,0:T(8,128)(2,1)} %add_convert_fusion), calls=%async_computation.4 | async-start | bytes 4194304 | tf_op jit(solution)/shard_map/all_to_all | solution.py:342
  608.1 109.8 %collective-permute-start.22 = (bf16[128,2048]{1,0:T(8,128)(2,1)}, bf16[128,2048]{1,0:T(8,128)(2,1)}, u32[]{:S(2)}, u32[]{:S(2)}) collective-permute-start(bf16[128,2048]{1,0:T(8,128)(2,1)} %fusion.70), channel_id=1, source_target_pairs={{0,16},{8,24},{16,0},{24,8},{1,17},{9,25},{17,1},{25,9},{2,18},{10... | collective-permute-start | bytes 1572872 | tf_op jit(solution)/shard_map/ppermute | solution.py:112
  612.9 105.0 %collective-permute-start.19 = (bf16[128,2048]{1,0:T(8,128)(2,1)}, bf16[128,2048]{1,0:T(8,128)(2,1)}, u32[]{:S(2)}, u32[]{:S(2)}) collective-permute-start(bf16[128,2048]{1,0:T(8,128)(2,1)} %fusion.71), channel_id=1, source_target_pairs={{0,24},{8,16},{16,8},{24,0},{1,25},{9,17},{17,9},{25,1},{2,26},{10... | collective-permute-start | bytes 1572872 | tf_op jit(solution)/shard_map/ppermute | solution.py:112
  629.0 104.7 %collective-permute-start.52 = (bf16[256,2048]{1,0:T(8,128)(2,1)}, bf16[256,2048]{1,0:T(8,128)(2,1)}, u32[]{:S(2)}, u32[]{:S(2)}) collective-permute-start(bf16[256,2048]{1,0:T(8,128)(2,1)} %slice.451), channel_id=1, source_target_pairs={{0,1},{1,0},{2,3},{3,2},{4,5},{5,4},{6,7},{7,6},{8,9},{9,8},{10,11... | collective-permute-start | bytes 3145736 | tf_op jit(solution)/shard_map/ppermute | solution.py:112
  737.5 32.3 %collective-permute-start.53 = (bf16[128,2048]{1,0:T(8,128)(2,1)}, bf16[128,2048]{1,0:T(8,128)(2,1)}, u32[]{:S(2)}, u32[]{:S(2)}) collective-permute-start(bf16[128,2048]{1,0:T(8,128)(2,1)} %slice.619), channel_id=1, source_target_pairs={{0,2},{2,0},{1,3},{3,1},{4,6},{6,4},{5,7},{7,5},{8,10},{10,8},{9,1... | collective-permute-start | bytes 1572872 | tf_op jit(solution)/shard_map/ppermute | solution.py:112
  (126 other events, 1602.3 us)
Sparse Core Ops, SparseCore 0:
  12.3 140.6 all-gather.1
  518.6 99.0 reduce-scatter.4
  621.4 132.6 reduce-scatter.2

commit v2 on v1

v2 whole, which is shorter than its diff:
```python
import jax
import jax.numpy as jnp
import numpy as np
from jax import lax
from jax.experimental import pallas as pl
from jax.experimental.pallas import tpu as pltpu
from jax.sharding import PartitionSpec as P

HD = 64


EPS_NORM = 1e-05
BETA = 0.5
LAMB_EPS = 1e-06
DECAY = 0.01
RATE = 0.5
NEG_FILL = -1e30


def rope_inverse(half_dim):
    exponent = np.arange(half_dim, dtype=np.float32) * np.float32(2.0 / (2 * half_dim))
    base_freq = np.float32(1.0) / np.power(np.float32(500000.0), exponent)
    wave_len = np.float32(2.0 * np.pi) / base_freq
    smooth = (np.float32(8192.0) / wave_len - np.float32(1.0)) / np.float32(3.0)
    middle = (np.float32(1.0) - smooth) * base_freq / np.float32(32.0) + smooth * base_freq
    scaled = np.where(
        wave_len < 2048.0,
        base_freq,
        np.where(wave_len > 8192.0, base_freq / np.float32(32.0), middle),
    )
    return scaled.astype(np.float32)


def doc_layout(lengths, position):
    doc_ends = jnp.cumsum(lengths, dtype=jnp.int32)
    starts_at = doc_ends - lengths
    segment = jnp.sum(
        (position[:, None] >= doc_ends[None, :]).astype(jnp.int32), axis=1, dtype=jnp.int32
    )
    onehot_doc = (
        segment[:, None] == jnp.arange(lengths.shape[0], dtype=jnp.int32)[None, :]
    ).astype(jnp.int32)
    doc_place = position - jnp.sum(onehot_doc * starts_at[None, :], axis=1, dtype=jnp.int32)
    return (segment, doc_place)


def rope_tables(doc_place, head_dim):
    inverse = jnp.asarray(rope_inverse(head_dim // 2))
    angles = doc_place.astype(jnp.float32)[:, None] * inverse[None, :]
    return (jnp.cos(angles), jnp.sin(angles))


def rounded(value):
    return value.astype(jnp.bfloat16)


def widened(value):
    return value.astype(jnp.float32)


def dot_plain(left_side, right_side):
    return lax.dot_general(
        left_side, right_side, (((1,), (0,)), ((), ())), preferred_element_type=jnp.float32
    )


def dot_rows(left_side, right_side):
    return lax.dot_general(
        left_side, right_side, (((1,), (1,)), ((), ())), preferred_element_type=jnp.float32
    )


def dot_cols(left_side, right_side):
    return lax.dot_general(
        left_side, right_side, (((0,), (0,)), ((), ())), preferred_element_type=jnp.float32
    )


def exchange(value, axis, mask, what="swap"):
    names = axis if isinstance(axis, tuple) else (axis,)
    size = 1
    for name in names:
        size = size * lax.axis_size(name)
    with jax.named_scope(what):
        return lax.ppermute(value, axis, [(place, place ^ mask) for place in range(size)])


def resplit(value, what):
    with jax.named_scope(what):
        return lax.all_to_all(value, "z", 0, 0, tiled=True)


def after(value, *others):
    return lax.optimization_barrier((value,) + others)[0]


def gather_row(value, what):
    across = exchange(value, "y", 1, what + "_y")
    return gather_core(value, across, what)


def gather_core(value, across, what, *waits):
    pair = jnp.concatenate([value, after(across, *waits)])
    return (value, across, exchange(pair, "c", 1, what + "_c"))


class RowSum:
    def __init__(self, keep, send, what):
        self.keep, self.what = keep, what
        self.tokens = keep.shape[0] // 2
        self.received = exchange(send, "c", 1, what + "_c")

    def pass_on(self, *waits):
        tokens = self.tokens
        received = after(self.received, *waits)
        passed = rounded(widened(self.keep[tokens:]) + widened(received[tokens:]))
        self.across = exchange(passed, "y", 1, self.what + "_y")

    def total(self):
        tokens = self.tokens
        return (
            widened(self.keep[:tokens])
            + widened(self.received[:tokens])
            + widened(self.across)
        )


def scatter_row(keep, send, what):
    row = RowSum(keep, send, what)
    row.pass_on()
    return row.total()


def all_sum(value):
    for axis in ("c", "x", "y", "z", "o"):
        mask = 1
        while mask < lax.axis_size(axis):
            value = value + exchange(value, axis, mask)
            mask = mask * 2
    return value


HBM = pl.BlockSpec(memory_space=pl.ANY)
VMEM = pl.BlockSpec(memory_space=pltpu.VMEM)
SMEM = pl.BlockSpec(memory_space=pltpu.SMEM)


def start_copies(pairs, sems, first=0):
    copies = [
        pltpu.make_async_copy(source, target, sems.at[first + place])
        for place, (source, target) in enumerate(pairs)
    ]
    for copy in copies:
        copy.start()
    return copies


def row_copies(pieces, target):
    pairs, first = [], 0
    for piece in pieces:
        pairs.append((piece, target.at[pl.ds(first, piece.shape[0]), :]))
        first += piece.shape[0]
    return pairs


def block_rows_of(index, place, depth):
    return pl.ds(pl.multiple_of(index[place] * depth, depth), depth)


def lane_iota(rows):
    return lax.broadcasted_iota(jnp.int32, (rows, 128), 1)


def partner(value):
    lane = lane_iota(value.shape[0])
    return jnp.where(lane % HD < HD // 2, pltpu.roll(value, 128 - HD // 2, 1), pltpu.roll(value, HD // 2, 1))


def head_lanes(value, head, kv):
    lane = lane_iota(value.shape[0])
    moved = value if head % 2 == kv else pltpu.roll(value, HD, 1)
    keep = lane < HD if kv == 0 else lane >= HD
    return jnp.where(keep, moved, 0.0)


def pair_slab(even, odd, kv):
    lane = lane_iota(even.shape[0])
    if kv == 0:
        odd = pltpu.roll(odd, HD, 1)
    else:
        even = pltpu.roll(even, HD, 1)
    return jnp.where(lane < HD, even, odd)


CHUNK = 256


def attend_body(n_blocks, heads, group, *refs):
    index, a_own, a_across, a_core = refs[:4]
    weights = refs[4 : 4 + n_blocks]
    cosine, sine, bias = refs[4 + n_blocks : 7 + n_blocks]
    a_all, q_out, kv_out, ctx_out, lse_out = refs[7 + n_blocks : 12 + n_blocks]
    held, sems = refs[12 + n_blocks :]
    depth = weights[0].shape[0]
    copies = start_copies(row_copies((a_own, a_across, a_core), a_all), sems)
    copies += start_copies(
        [
            (weights[i].at[:, : held.shape[1]], held.at[block_rows_of(index, i, depth), :])
            for i in range(n_blocks)
        ],
        sems,
        3,
    )
    for copy in copies:
        copy.wait()
    rows_all = a_all.shape[0]
    n_slabs = heads // 2

    @pl.loop(0, rows_all // CHUNK)
    def _(at):
        rows = pl.ds(pl.multiple_of(at * CHUNK, CHUNK), CHUNK)
        raw = dot_plain(a_all[rows, :], held[...])
        cos, sin = cosine[rows, :], sine[rows, :]
        for slab in range(n_slabs + 1):
            part = raw[:, slab * 128 : (slab + 1) * 128]
            part = part * cos + partner(part) * sin
            if slab < n_slabs:
                for head in (2 * slab, 2 * slab + 1):
                    q_out[head, rows, :] = rounded(head_lanes(part, head, head // group))
            else:
                kv_out[0, rows, :] = rounded(part)
        kv_out[1, rows, :] = rounded(raw[:, (n_slabs + 1) * 128 : (n_slabs + 2) * 128])

    @pl.loop(0, rows_all // CHUNK)
    def _(at):
        rows = pl.ds(pl.multiple_of(at * CHUNK, CHUNK), CHUNK)
        keys, values = kv_out[0], kv_out[1]
        lane = lane_iota(CHUNK)
        logs = jnp.zeros((CHUNK, 128), jnp.float32)
        for slab in range(n_slabs):
            outs = []
            for head in (2 * slab, 2 * slab + 1):
                scores = dot_rows(q_out[head, rows, :], keys) * HD ** (-0.5) + bias[rows, :]
                most = jnp.max(scores, axis=-1, keepdims=True)
                shifted = jnp.exp(scores - most)
                total = jnp.sum(shifted, axis=-1, keepdims=True)
                outs.append(dot_plain(rounded(shifted / total), values))
                logs = jnp.where(lane == head, most + jnp.log(total), logs)
            ctx_out[rows, slab * 128 : (slab + 1) * 128] = rounded(
                pair_slab(outs[0], outs[1], 2 * slab // group)
            )
        lse_out[rows, :] = logs


def attend_back_body(n_blocks, heads, group, *refs):
    index, d_all = refs[:2]
    weights = refs[2 : 2 + n_blocks]
    queries, keyvals, bias, logs, cosine, sine = refs[2 + n_blocks : 8 + n_blocks]
    out = refs[8 + n_blocks]
    held, d_heads, key_sum, value_sum, sems = refs[9 + n_blocks :]
    depth, wide = weights[0].shape[0], held.shape[1]
    first = weights[0].shape[1] - wide
    copies = start_copies(
        [
            (weights[i].at[:, pl.ds(first, wide)], held.at[block_rows_of(index, i, depth), :])
            for i in range(n_blocks)
        ],
        sems,
    )
    for copy in copies:
        copy.wait()
    rows_all = d_all.shape[0]
    n_slabs = heads // 2
    key_sum[...] = jnp.zeros_like(key_sum)
    value_sum[...] = jnp.zeros_like(value_sum)

    @pl.loop(0, rows_all // CHUNK)
    def _(at):
        rows = pl.ds(pl.multiple_of(at * CHUNK, CHUNK), CHUNK)
        d_ctx = dot_plain(d_all[rows, :], held[...])
        for slab in range(n_slabs):
            part = d_ctx[:, slab * 128 : (slab + 1) * 128]
            for head in (2 * slab, 2 * slab + 1):
                d_heads[head, :, :] = rounded(head_lanes(part, head, head // group))
        keys, values = keyvals[0], keyvals[1]
        lane = lane_iota(CHUNK)
        cos, sin = cosine[rows, :], sine[rows, :]
        log_rows = logs[rows, :]
        for slab in range(n_slabs):
            kv = 2 * slab // group
            outs = []
            for head in (2 * slab, 2 * slab + 1):
                query, d_head = queries[head, rows, :], d_heads[head]
                log_total = jnp.sum(jnp.where(lane == head, log_rows, 0.0), axis=-1, keepdims=True)
                scores = dot_rows(query, keys) * HD ** (-0.5) + bias[rows, :]
                probs = jnp.exp(scores - log_total)
                d_probs = dot_rows(d_head, values)
                inner = jnp.sum(probs * d_probs, axis=-1, keepdims=True)
                d_scores = rounded(probs * (d_probs - inner) * HD ** (-0.5))
                key_sum[...] += dot_cols(d_scores, query)
                value_sum[...] += dot_cols(rounded(probs), d_head)
                outs.append(dot_plain(d_scores, keys))
            part = pair_slab(outs[0], outs[1], kv)
            out[rows, slab * 128 : (slab + 1) * 128] = rounded(part * cos - partner(part) * sin)

    key_grad = key_sum[...]
    key_grad = key_grad * cosine[...] - partner(key_grad) * sine[...]
    out[:, n_slabs * 128 : (n_slabs + 1) * 128] = rounded(key_grad)
    out[:, (n_slabs + 1) * 128 : (n_slabs + 2) * 128] = rounded(value_sum[...])


def rows_out_body(n_blocks, first, *refs):
    index, left = refs[:2]
    weights = refs[2 : 2 + n_blocks]
    keep, send, held, sems = refs[2 + n_blocks :]
    depth, wide = weights[0].shape[0], held.shape[1]
    copies = start_copies(
        [
            (weights[i].at[:, pl.ds(first, wide)], held.at[block_rows_of(index, i, depth), :])
            for i in range(n_blocks)
        ],
        sems,
    )
    for copy in copies:
        copy.wait()
    half = left.shape[0] // 2
    send[...] = rounded(dot_rows(left[half:, :], held[...]))
    keep[...] = rounded(dot_rows(left[:half, :], held[...]))


def natural_rows(scalars, pieces, which, target):
    tokens = pieces[0].shape[0] // 2
    pairs = []
    for at in range(4):
        place = pl.ds(pl.multiple_of(scalars[3 + at] * tokens, tokens), tokens)
        piece = pieces[min(at, 2)]
        first = (which + 2 * (at - 2 if at > 2 else 0)) * tokens
        pairs.append((piece.at[pl.ds(first, tokens), :], target.at[place, :]))
    return pairs


def ffn_body(n_parts, n_z, n_alias, scalars, *refs):
    pieces = refs[:3]
    gateup = refs[3 : 3 + n_parts]
    down = refs[3 + n_parts : 3 + 2 * n_parts]
    refs = refs[3 + 2 * n_parts + n_alias :]
    b_rows, d_rows, hid, grad_pair, keep, send, wide, deep, sems = refs
    part = down[0].shape[2]
    copies = start_copies(natural_rows(scalars, pieces, 0, b_rows), sems)
    copies += start_weights(scalars, 7, gateup, (), wide, None, sems, 4)
    later = start_copies(natural_rows(scalars, pieces, 1, d_rows), sems, len(copies))
    later += start_weights(scalars, 7, (), down, None, deep, sems, len(copies) + 4)
    for copy in copies:
        copy.wait()
    pre = dot_plain(b_rows[...], wide[...])
    for copy in later:
        copy.wait()
    d_hid = dot_plain(d_rows[...], deep[...])
    gate_pre, up_pre = pre[:, :part], pre[:, part:]
    sigma = jax.nn.sigmoid(gate_pre)
    silu = gate_pre * sigma
    hid[...] = rounded(silu * up_pre)
    d_gate = d_hid * up_pre * (sigma * (1.0 + gate_pre * (1.0 - sigma)))
    grad_pair[:, :part] = rounded(d_gate)
    grad_pair[:, part:] = rounded(d_hid * silu)
    grad_in = rounded(dot_rows(grad_pair[...], wide[...]))
    lay_out(grad_in, scalars, keep, send)


def start_weights(index, first, gateup, down, wide, deep, sems, first_sem=0):
    pairs = []
    for i, piece in enumerate(gateup):
        n_z, _, depth, part = piece.shape
        for z in range(n_z):
            block = block_rows_of(index, first + i * n_z + z, depth)
            for half in range(2):
                pairs.append((piece.at[z, half], wide.at[block, pl.ds(half * part, part)]))
    for i, piece in enumerate(down):
        n_z, depth, _ = piece.shape
        for z in range(n_z):
            pairs.append((piece.at[z], deep.at[block_rows_of(index, first + i * n_z + z, depth), :]))
    return start_copies(pairs, sems, first_sem)


def cost(flops, nbytes):
    return pl.CostEstimate(flops=flops, bytes_accessed=nbytes, transcendentals=0)


def bf16_of(*shape):
    return jax.ShapeDtypeStruct(shape, jnp.bfloat16)


def attend(index, pieces, weights, cosine, sine, bias, heads, group):
    rows, width = cosine.shape[0], pieces[0].shape[1]
    n_blocks, wide = len(weights), (heads + 4) * HD
    return pl.pallas_call(
        lambda *refs: attend_body(n_blocks, heads, group, *refs),
        out_shape=(
            bf16_of(rows, width),
            bf16_of(heads, rows, 128),
            bf16_of(2, rows, 128),
            bf16_of(rows, heads * HD),
            jax.ShapeDtypeStruct((rows, 128), jnp.float32),
        ),
        in_specs=[SMEM] + [HBM] * (3 + n_blocks) + [VMEM] * 3,
        out_specs=(VMEM,) * 5,
        scratch_shapes=[
            pltpu.VMEM((width, wide), jnp.bfloat16),
            pltpu.SemaphoreType.DMA((3 + n_blocks,)),
        ],
        cost_estimate=cost(2 * rows * width * wide + 4 * heads * rows * rows * 128, 8 << 20),
        name="attend",
    )(index, *pieces, *weights, cosine, sine, bias)


def attend_back(index, grad_rows, weights, queries, keyvals, bias, logs, cosine, sine, heads, group):
    rows, width = grad_rows.shape
    n_blocks, wide = len(weights), heads * HD
    return pl.pallas_call(
        lambda *refs: attend_back_body(n_blocks, heads, group, *refs),
        out_shape=bf16_of(rows, heads * HD + 256),
        in_specs=[SMEM, VMEM] + [HBM] * n_blocks + [VMEM] * 6,
        out_specs=VMEM,
        scratch_shapes=[
            pltpu.VMEM((width, wide), jnp.bfloat16),
            pltpu.VMEM((heads, CHUNK, 128), jnp.bfloat16),
            pltpu.VMEM((rows, 128), jnp.float32),
            pltpu.VMEM((rows, 128), jnp.float32),
            pltpu.SemaphoreType.DMA((n_blocks,)),
        ],
        cost_estimate=cost(2 * rows * width * wide + 10 * heads * rows * rows * 128, 8 << 20),
        name="attend_back",
    )(index, grad_rows, *weights, queries, keyvals, bias, logs, cosine, sine)


def rows_out(index, left, weights, first, name):
    rows, wide = left.shape
    n_blocks = len(weights)
    width = n_blocks * weights[0].shape[0]
    return pl.pallas_call(
        lambda *refs: rows_out_body(n_blocks, first, *refs),
        out_shape=(bf16_of(rows // 2, width),) * 2,
        in_specs=[SMEM, VMEM] + [HBM] * n_blocks,
        out_specs=(VMEM,) * 2,
        scratch_shapes=[
            pltpu.VMEM((width, wide), jnp.bfloat16),
            pltpu.SemaphoreType.DMA((n_blocks,)),
        ],
        cost_estimate=cost(2 * rows * width * wide, 6 << 20),
        name=name,
    )(index, left, *weights)


def ffn_rows(scalars, pieces, gateup, down, total, earlier):
    row_len, width = 2 * pieces[0].shape[0], pieces[0].shape[1]
    n_parts, n_z, part = len(gateup), gateup[0].shape[0], gateup[0].shape[3]
    n_alias = len(earlier)

    def block(wide):
        return pl.BlockSpec((row_len, wide), lambda i, scalars: (scalars[0], 0))

    def whole(wide):
        return pl.BlockSpec((row_len // 2, wide), lambda i, scalars: (0, 0))

    return pl.pallas_call(
        lambda *refs: ffn_body(n_parts, n_z, n_alias, *refs),
        grid_spec=pltpu.PrefetchScalarGridSpec(
            num_scalar_prefetch=1,
            grid=(1,),
            in_specs=[HBM] * (3 + 2 * n_parts + n_alias),
            out_specs=(block(width), block(width), block(part), block(2 * part), whole(width), whole(width)),
            scratch_shapes=[
                pltpu.VMEM((width, 2 * part), jnp.bfloat16),
                pltpu.VMEM((width, part), jnp.bfloat16),
                pltpu.SemaphoreType.DMA((8 + 3 * n_parts * n_z,)),
            ],
        ),
        out_shape=(
            bf16_of(total, width),
            bf16_of(total, width),
            bf16_of(total, part),
            bf16_of(total, 2 * part),
            bf16_of(row_len // 2, width),
            bf16_of(row_len // 2, width),
        ),
        input_output_aliases={4 + 2 * n_parts + at: at for at in range(n_alias)},
        cost_estimate=cost(row_len * width, 1 << 20),
        name="ffn_rows",
    )(scalars, *pieces, *gateup, *down, *earlier)


def lay_out(value, scalars, keep, send, lead=()):
    tokens = value.shape[0] // 4
    for place in range(4):
        piece = value[place * tokens : (place + 1) * tokens, :]
        target = pl.ds(pl.multiple_of(((place // 2) ^ scalars[1]) * tokens, tokens), tokens)

        @pl.when(scalars[2] == place % 2)
        def _():
            keep[(*lead, target, slice(None))] = piece

        @pl.when(scalars[2] != place % 2)
        def _():
            send[(*lead, target, slice(None))] = piece


def out_rows_body(n_parts, scalars, left, *refs):
    down = refs[:n_parts]
    keep, send, deep, sems = refs[n_parts:]

    @pl.when(pl.program_id(0) == 0)
    def _():
        for copy in start_weights(scalars, 7, (), down, None, deep, sems):
            copy.wait()

    lay_out(rounded(dot_rows(left[...], deep[...])), scalars, keep, send, (0,))


def out_rows(scalars, left, down, row_len):
    rows, part = left.shape
    n_parts, n_z, depth = len(down), down[0].shape[0], down[0].shape[1]
    width, n_rows = n_parts * n_z * depth, rows // row_len
    block = pl.BlockSpec((1, row_len // 2, width), lambda i, scalars: (i, 0, 0))
    return pl.pallas_call(
        lambda *refs: out_rows_body(n_parts, *refs),
        grid_spec=pltpu.PrefetchScalarGridSpec(
            num_scalar_prefetch=1,
            grid=(n_rows,),
            in_specs=[pl.BlockSpec((row_len, part), lambda i, scalars: (i, 0))] + [HBM] * n_parts,
            out_specs=(block, block),
            scratch_shapes=[
                pltpu.VMEM((width, part), jnp.bfloat16),
                pltpu.SemaphoreType.DMA((n_parts * n_z,)),
            ],
        ),
        out_shape=(bf16_of(n_rows, row_len // 2, width),) * 2,
        cost_estimate=cost(rows * width, 1 << 20),
        name="out_rows",
    )(scalars, left, *down)


def lamb_update(gradient, moment, second, weight):
    new_moment = BETA * moment + (1.0 - BETA) * gradient
    new_second = BETA * second + (1.0 - BETA) * gradient * gradient
    update = new_moment / (jnp.sqrt(new_second) + LAMB_EPS) + DECAY * weight
    return (new_moment, new_second, update)


def tile_sum(value):
    rows, wide = value.shape
    step = min(wide, 128)
    total = value[:, :step]
    for at in range(1, wide // step):
        total = total + value[:, at * step : (at + 1) * step]
    return jnp.sum(total.reshape(rows // 8, 8, step), axis=0)


def lamb_step(gradient, refs, place):
    moment, second, weight, grad_out, moment_out, second_out = refs
    new_moment, new_second, update = lamb_update(
        gradient, moment[place], second[place], weight[place]
    )
    grad_out[place] = gradient
    moment_out[place] = new_moment
    second_out[place] = new_second
    return tile_sum(update * update), tile_sum(weight[place] * weight[place])


def lamb_gateup_body(grads, *refs):
    sums = refs[6]
    update_sq, weight_sq = lamb_step(widened(grads[0]), refs[:6], 0)

    @pl.when(pl.program_id(1) == 0)
    def _():
        sums[...] = jnp.zeros_like(sums)

    sums[0, 0] += update_sq
    sums[0, 1] += weight_sq


def lamb_gateup(grads, moment, second, weight):
    two, depth, held = weight.shape
    n_z, part = grads.shape[0], held // grads.shape[0]
    block = pl.BlockSpec((1, depth, part), lambda half, z: (half, 0, z))
    whole = jax.ShapeDtypeStruct(weight.shape, jnp.float32)
    return pl.pallas_call(
        lamb_gateup_body,
        grid=(two, n_z),
        in_specs=[pl.BlockSpec((1, depth, part), lambda half, z: (z, 0, half))] + [block] * 3,
        out_specs=(block,) * 3 + (pl.BlockSpec((1, 2, 8, 128), lambda half, z: (half, 0, 0, 0)),),
        out_shape=(whole,) * 3 + (jax.ShapeDtypeStruct((two, 2, 8, 128), jnp.float32),),
        cost_estimate=cost(20 * weight.size, 26 * weight.size),
        name="lamb_gateup",
    )(grads, moment, second, weight)


def lamb_turned_body(n_sum, grads, *refs):
    sums = refs[6]
    gradient = widened(grads[0])
    for at in range(1, n_sum):
        gradient = gradient + widened(grads[at])
    update_sq, weight_sq = lamb_step(gradient.T, refs[:6], ...)

    @pl.when(pl.program_id(0) == 0)
    def _():
        sums[...] = jnp.zeros_like(sums)

    step = update_sq.shape[1]
    sums[0, :, :step] += update_sq
    sums[1, :, :step] += weight_sq


def lamb_turned(grads, moment, second, weight, n_sum, name):
    rows, depth = grads.shape[2], grads.shape[1]
    block = pl.BlockSpec((rows, depth), lambda i: (i, 0))
    whole = jax.ShapeDtypeStruct(weight.shape, jnp.float32)
    return pl.pallas_call(
        lambda *refs: lamb_turned_body(n_sum, *refs),
        grid=(weight.shape[0] // rows,),
        in_specs=[pl.BlockSpec((n_sum, depth, rows), lambda i: (i, 0, 0))] + [block] * 3,
        out_specs=(block,) * 3 + (pl.BlockSpec((2, 8, 128), lambda i: (0, 0, 0)),),
        out_shape=(whole,) * 3 + (jax.ShapeDtypeStruct((2, 8, 128), jnp.float32),),
        cost_estimate=cost(20 * weight.size, 26 * weight.size),
        name=name,
    )(grads, moment, second, weight)


def lamb_qkv_body(grads, *refs):
    query, keyval, sums = refs[0:3] + refs[6:9], refs[3:6] + refs[9:12], refs[12]
    gradient = widened(grads[0])
    for at in range(1, grads.shape[0]):
        gradient = gradient + widened(grads[at])
    wide, narrow = query[0].shape[1], keyval[0].shape[2]
    sums[0, 0], sums[0, 1] = lamb_step(gradient[:, :wide], query, ...)
    for at in range(2):
        first = wide + at * narrow
        sums[1 + at, 0], sums[1 + at, 1] = lamb_step(
            gradient[:, first : first + narrow], keyval, at
        )


def lamb_qkv(grads, query, keyval):
    shapes = [jax.ShapeDtypeStruct(part[0].shape, jnp.float32) for part in (query, keyval)]
    return pl.pallas_call(
        lamb_qkv_body,
        in_specs=[VMEM] * 7,
        out_specs=(VMEM,) * 7,
        out_shape=(shapes[0],) * 3
        + (shapes[1],) * 3
        + (jax.ShapeDtypeStruct((3, 2, 8, 128), jnp.float32),),
        cost_estimate=cost(4 << 20, 6 << 20),
        name="lamb_qkv",
    )(grads, *query, *keyval)


def lamb_moments(gradient, moment, second):
    new_moment = BETA * moment + (1.0 - BETA) * gradient
    new_second = BETA * second + (1.0 - BETA) * gradient * gradient
    return (new_moment, new_second, new_moment / (jnp.sqrt(new_second) + LAMB_EPS))


def per_device(
    hidden_in,
    out_grad,
    doc_lengths,
    norm_gains,
    w_query,
    w_keyval,
    w_out,
    w_gateup,
    w_down,
    moment_gains,
    moment_query,
    moment_keyval,
    moment_out,
    moment_gateup,
    moment_down,
    second_gains,
    second_query,
    second_keyval,
    second_out,
    second_gateup,
    second_down,
):
    tok = hidden_in.shape[1]
    width = hidden_in.shape[2]
    row_len = tok * 4
    n_o, n_z, n_x = lax.axis_size("o"), lax.axis_size("z"), lax.axis_size("x")
    n_parts = n_o * n_x
    depth = w_query.shape[0]
    heads_wide = w_query.shape[1]
    kv_wide = w_keyval.shape[2]
    local_heads = heads_wide // HD
    group_size = heads_wide // kv_wide
    ff_held = w_down.shape[0]
    ff_part = ff_held // n_z
    my_part = lax.axis_index("o") * n_x + lax.axis_index("x")
    my_z = lax.axis_index("z")

    part_of = my_part ^ jnp.arange(n_parts, dtype=jnp.int32)[:, None]
    z_of = jnp.arange(n_z, dtype=jnp.int32)[None, :]

    def block_of(part, z):
        return (((part // n_x) * n_z + z) * n_x + part % n_x).reshape(-1)

    y_at, c_at = lax.axis_index("y"), lax.axis_index("c")
    attn_index = block_of(part_of, my_z ^ z_of)
    ffn_index = block_of(part_of, z_of)

    token_block = [
        (y_at ^ y_other) * 2 + (c_at ^ c_other) for c_other in range(2) for y_other in range(2)
    ]

    def row_scalars(place):
        return jnp.concatenate([jnp.stack([my_z ^ place, y_at, c_at] + token_block), ffn_index])

    parts = range(1, n_parts)

    def to_parts(piece, what):
        return [exchange(piece, ("o", "x"), place, what) for place in parts]

    def in_order(column, across):
        return list(column) + [across[z][place - 1] for place in parts for z in range(n_z)]

    position = jnp.concatenate(
        [block * tok + jnp.arange(tok, dtype=jnp.int32) for block in token_block]
    )

    x_float = widened(hidden_in[0])
    gain_attn = norm_gains[0]
    gain_ffn = norm_gains[1]
    inv_one = lax.rsqrt(jnp.mean(x_float * x_float, axis=-1, keepdims=True) + EPS_NORM)
    normed_one = x_float * inv_one
    qkv_own = rounded(jnp.concatenate([w_query, w_keyval[0], w_keyval[1]], axis=1))
    qkv_near = exchange(qkv_own, "z", 1, "wqkv_z1")
    qkv_far = exchange(qkv_own, "z", 2, "wqkv_z2")
    qkv_x0 = to_parts(qkv_own, "wqkv_x0")
    phase_a = (qkv_near, qkv_far, *qkv_x0)
    qkv_last = exchange(after(qkv_far, *phase_a), "z", 1, "wqkv_z3")
    qkv_x1 = to_parts(after(qkv_near, *phase_a), "wqkv_x1")
    qkv_x2 = to_parts(after(qkv_far, *phase_a), "wqkv_x2")
    attn_own = after(rounded(normed_one * gain_attn), *phase_a)
    attn_across = exchange(attn_own, "y", 1, "a_y")
    phase_b = (qkv_last, *qkv_x1, *qkv_x2, attn_across)
    out_own = after(rounded(w_out.T), *phase_b)
    out_near = exchange(out_own, "z", 1, "wout_z1")
    out_far = exchange(out_own, "z", 2, "wout_z2")
    out_x0 = to_parts(out_own, "wout_x0")
    qkv_x3 = to_parts(after(qkv_last, *phase_b), "wqkv_x3")
    attn_pair = jnp.concatenate([attn_own, after(attn_across, *phase_b)])
    attn_pieces = (attn_own, attn_across, exchange(attn_pair, "c", 1, "a_c"))
    phase_c = (out_near, out_far, *out_x0, *qkv_x3)
    out_last = exchange(after(out_far, *phase_c), "z", 1, "wout_z3")
    out_x1 = to_parts(after(out_near, *phase_c), "wout_x1")
    out_x2 = to_parts(after(out_far, *phase_c), "wout_x2")
    out_x3 = to_parts(out_last, "wout_x3")
    qkv_w = in_order(
        (qkv_own, qkv_near, qkv_far, qkv_last), (qkv_x0, qkv_x1, qkv_x2, qkv_x3)
    )
    out_w = in_order(
        (out_own, out_near, out_far, out_last), (out_x0, out_x1, out_x2, out_x3)
    )
    gateup_send = rounded(w_gateup).reshape(2, depth, n_z, ff_part).transpose(2, 0, 1, 3)
    gateup_own = resplit(after(gateup_send, out_last), "wgu_z")
    segment, doc_place = doc_layout(doc_lengths[0], position)
    cosine, sine_part = rope_tables(doc_place, HD)
    cosine = jnp.concatenate([cosine] * 4, axis=1)
    sine_part = jnp.concatenate([-sine_part, sine_part] * 2, axis=1)
    bias = jnp.where(
        (segment[:, None] == segment[None, :]) & (position[None, :] <= position[:, None]),
        jnp.float32(0.0),
        jnp.float32(NEG_FILL),
    )
    attn_input, queries, keyvals, context, logs = attend(
        after(attn_index, out_last), attn_pieces, qkv_w, cosine, sine_part, bias, local_heads, group_size
    )
    mid_stream = x_float + scatter_row(
        *rows_out(attn_index, context, out_w, 0, "mid_rows"), "mid"
    )
    inv_two = lax.rsqrt(jnp.mean(mid_stream * mid_stream, axis=-1, keepdims=True) + EPS_NORM)
    normed_two = mid_stream * inv_two

    pair_own = jnp.concatenate(
        [rounded(normed_two * gain_ffn), after(out_grad[0], gateup_own)]
    )
    pair_far = exchange(pair_own, "z", 2, "bd_z2")
    pair_near = exchange(pair_own, "z", 1, "bd_z1")
    pair_rows = {0: gather_row(pair_own, "bd0")}
    down_turned = rounded(w_down).reshape(n_z, ff_part, depth).transpose(0, 2, 1)
    down_send = after(down_turned, pair_own)
    down_own = resplit(down_send, "wd_z")
    gateup_w = [gateup_own] + [
        exchange(gateup_own, ("o", "x"), place, "wgu_x") for place in range(1, n_parts)
    ]
    down_w = [down_own] + [
        exchange(after(down_own, gateup_w[-1]), ("o", "x"), place, "wd_x")
        for place in range(1, n_parts)
    ]

    pair_last = exchange(
        after(pair_far, pair_near), "z", 1, "bd_z3"
    )
    pair_rows[1] = gather_row(after(pair_near, pair_rows[0][1]), "bd1")
    held, rows = (), {}

    def ffn_row(place, *waits):
        *outs, keep, send = ffn_rows(
            after(row_scalars(place), *waits),
            pair_rows[place],
            gateup_w,
            down_w,
            n_z * row_len,
            held,
        )
        rows[place] = RowSum(keep, send, "db" + str(place))
        return tuple(outs), send

    held, sent = ffn_row(0, pair_near, pair_far)
    far_across = exchange(after(pair_far, sent), "y", 1, "bd2_y")
    held, sent1 = ffn_row(1, pair_last)
    pair_rows[2] = gather_core(pair_far, far_across, "bd2", sent1)
    last_across = exchange(after(pair_last, sent), "y", 1, "bd3_y")
    held, sent2 = ffn_row(2)
    pair_rows[3] = gather_core(pair_last, last_across, "bd3", sent2)
    for place in (1, 0, 2):
        rows[place].pass_on(last_across)
    held, sent = ffn_row(3, rows[1].received)
    rows[3].pass_on()
    ffn_input, grad_full, hidden_act, grad_pair = held

    def parts_of(weight_grad):
        cut = weight_grad.reshape(n_o, n_z, n_x, depth, weight_grad.shape[1])
        return [
            lax.dynamic_index_in_dim(
                lax.dynamic_index_in_dim(cut, (my_part ^ place) // n_x, 0, keepdims=False),
                (my_part ^ place) % n_x,
                1,
                keepdims=False,
            )
            for place in range(n_parts)
        ]

    def part_moves(pieces, what, *waits):
        return [pieces[0]] + [
            exchange(after(pieces[place], *waits), ("o", "x"), place, what + "_x")
            for place in range(1, n_parts)
        ]

    def part_sum(pieces, *waits):
        total = widened(after(pieces[0], *waits))
        for piece in pieces[1:]:
            total = total + widened(piece)
        return rounded(total)

    down_pieces = parts_of(
        rounded(dot_cols(grad_full, after(hidden_act, rows[3].received)))
    )
    gateup_pieces = parts_of(
        rounded(dot_cols(ffn_input, after(grad_pair, down_pieces[-1])))
    )
    down_moves = part_moves(down_pieces, "gdown")
    out_keep, out_send = out_rows(
        row_scalars(0), after(hidden_act, gateup_pieces[-1]), down_w, row_len
    )
    gateup_moves = part_moves(gateup_pieces, "ggu")
    near_sum = exchange(rounded(rows[1].total()), "z", 1, "db1_z")
    last_sum = exchange(after(rounded(rows[3].total()), near_sum), "z", 1, "db3_z")
    far_sum = exchange(
        after(rounded(rows[2].total() + widened(last_sum)), *down_moves[1:]), "z", 2, "db2_z"
    )
    grad_ffn_in = rows[0].total() + widened(near_sum) + widened(far_sum)
    grad_ffn_in = after(grad_ffn_in, out_send, *down_moves[1:])

    gain_grad_ffn = jnp.sum(grad_ffn_in * normed_two, axis=0)
    grad_normed_two = grad_ffn_in * gain_ffn
    grad_mid = widened(out_grad[0]) + inv_two * (
        grad_normed_two
        - normed_two * jnp.mean(grad_normed_two * normed_two, axis=-1, keepdims=True)
    )
    def ratios_of(totals):
        norms = jnp.sqrt(jnp.sum(totals.reshape(-1, 2, 1024), axis=2))
        return norms[:, 1], norms[:, 0], norms[:, 1] / norms[:, 0]

    def stepped(weight, entry, ratio):
        update = entry[1] / (jnp.sqrt(entry[2]) + LAMB_EPS) + DECAY * weight
        return weight - RATE * (update * ratio)

    grad_mid_send = rounded(grad_mid)
    grad_mid_rows = gather_row(grad_mid_send, "dmid")
    down_grads = resplit(part_sum(down_moves), "gdown_z")
    grad_mid_full = after(jnp.concatenate(grad_mid_rows), down_grads, *gateup_moves[1:])
    out_received = exchange(out_send, "c", 1, "out_c")
    out_passed = rounded(
        widened(out_keep[:, tok:]) + widened(out_received[:, tok:])
    )
    out_across = exchange(out_passed, "y", 1, "out_y")
    grad_qkv = attend_back(
        attn_index,
        after(grad_mid_full, out_passed),
        out_w,
        queries,
        keyvals,
        bias,
        logs,
        cosine,
        sine_part,
        local_heads,
        group_size,
    )
    qkv_pieces = parts_of(
        rounded(dot_cols(attn_input, grad_qkv))
    )
    qkv_moves = part_moves(qkv_pieces, "gqkv")
    out_pieces = parts_of(
        rounded(dot_cols(after(grad_mid_full, *qkv_moves), context))
    )
    out_moves = part_moves(out_pieces, "gout")
    gateup_grads = resplit(after(part_sum(gateup_moves), down_grads), "ggu_z")
    out_total = rounded(
        widened(out_keep[:, :tok]) + widened(out_received[:, :tok]) + widened(out_across)
    )
    *down_new, down_sq = lamb_turned(
        after(down_grads, qkv_pieces[-1]), moment_down, second_down, w_down, 1, "lamb_down"
    )
    ffn_out = resplit(after(out_total, gateup_grads, down_sq, qkv_pieces[-1]), "out_z")
    *gateup_new, gateup_sq = lamb_gateup(gateup_grads, moment_gateup, second_gateup, w_gateup)
    out_grads = resplit(after(part_sum(out_moves), ffn_out, gateup_sq), "gout_z")
    qkv_total = part_sum(qkv_moves)
    block_out = rounded(mid_stream + jnp.sum(widened(ffn_out), axis=0))[None]
    grad_attn_in = scatter_row(*rows_out(attn_index, grad_qkv, qkv_w, 0, "grad_rows"), "da")
    gain_grad_attn = jnp.sum(grad_attn_in * normed_one, axis=0)
    grad_normed_one = grad_attn_in * gain_attn
    input_grad = grad_mid + inv_one * (
        grad_normed_one
        - normed_one * jnp.mean(grad_normed_one * normed_one, axis=-1, keepdims=True)
    )
    gain_rows = 2 * width // 128
    packed = all_sum(
        jnp.concatenate(
            [gain_grad_attn.reshape(-1, 128), gain_grad_ffn.reshape(-1, 128)]
            + [gateup_sq.reshape(-1, 128), down_sq.reshape(-1, 128)]
        )
    )
    qkv_grads = resplit(after(qkv_total, out_grads), "gqkv_z")
    ffn_norms = ratios_of(packed[gain_rows:])
    new_gateup = stepped(w_gateup, gateup_new, ffn_norms[2][:2][:, None, None])
    new_down = stepped(w_down, down_new, ffn_norms[2][2])
    grad_gains = packed[:gain_rows].reshape(2, width)
    gain_moment, gain_second, gain_direction = lamb_moments(grad_gains, moment_gains, second_gains)
    gain_update = gain_direction + DECAY * norm_gains
    gain_norms = (
        jnp.sqrt(jnp.sum(norm_gains * norm_gains, axis=1)),
        jnp.sqrt(jnp.sum(gain_update * gain_update, axis=1)),
    )
    gain_norms = gain_norms + (gain_norms[0] / gain_norms[1],)
    new_gains = norm_gains - RATE * gain_norms[2][:, None] * gain_update

    *out_new, out_sq = lamb_turned(out_grads, moment_out, second_out, w_out, n_z, "lamb_out")
    *qkv_new, qkv_sq = lamb_qkv(
        after(qkv_grads, new_gateup, new_down, new_gains, out_sq, block_out, input_grad),
        (moment_query, second_query, w_query),
        (moment_keyval, second_keyval, w_keyval),
    )
    attn_sq = all_sum(jnp.concatenate([qkv_sq, out_sq[None]]).reshape(-1, 128))
    attn_norms = ratios_of(attn_sq)
    new_query = stepped(w_query, qkv_new[:3], attn_norms[2][0])
    new_keyval = stepped(w_keyval, qkv_new[3:], attn_norms[2][1:3][:, None, None])
    new_out = stepped(w_out, out_new, attn_norms[2][3])
    results = (qkv_new[:3], qkv_new[3:], out_new, gateup_new, down_new)
    grad_parts = tuple((entry[0] for entry in results))
    new_moments = tuple((entry[1] for entry in results))
    new_seconds = tuple((entry[2] for entry in results))
    new_parts = (new_query, new_keyval, new_out, new_gateup, new_down)
    weight_norms, update_norms, trust_ratios = (
        jnp.concatenate([attn_norms[at], ffn_norms[at], gain_norms[at]]) for at in range(3)
    )
    return (
        block_out,
        input_grad[None],
        grad_gains,
        grad_parts[0],
        grad_parts[1],
        grad_parts[2],
        grad_parts[3],
        grad_parts[4],
        new_gains,
        new_parts[0],
        new_parts[1],
        new_parts[2],
        new_parts[3],
        new_parts[4],
        gain_moment,
        new_moments[0],
        new_moments[1],
        new_moments[2],
        new_moments[3],
        new_moments[4],
        gain_second,
        new_seconds[0],
        new_seconds[1],
        new_seconds[2],
        new_seconds[3],
        new_seconds[4],
        weight_norms,
        update_norms,
        trust_ratios,
    )


def solution(mesh):
    n_dp, n_tensor = mesh.devices.shape
    split = jax.sharding.Mesh(
        mesh.devices.reshape(n_dp // 8, 4, 2, n_tensor // 2, 2), ("o", "z", "x", "y", "c")
    )
    dp, tensor = ("o", "z", "x"), ("y", "c")
    in_specs = (
        P(dp, tensor, None),
        P(dp, tensor, None),
        P(dp, None),
        P(),
        P(dp, tensor),
        P(None, dp, tensor),
        P(tensor, dp),
        P(None, dp, tensor),
        P(tensor, dp),
        P(),
        P(dp, tensor),
        P(None, dp, tensor),
        P(tensor, dp),
        P(None, dp, tensor),
        P(tensor, dp),
        P(),
        P(dp, tensor),
        P(None, dp, tensor),
        P(tensor, dp),
        P(None, dp, tensor),
        P(tensor, dp),
    )
    out_specs = (
        P(dp, tensor, None),
        P(dp, tensor, None),
        P(),
        P(dp, tensor),
        P(None, dp, tensor),
        P(tensor, dp),
        P(None, dp, tensor),
        P(tensor, dp),
        P(),
        P(dp, tensor),
        P(None, dp, tensor),
        P(tensor, dp),
        P(None, dp, tensor),
        P(tensor, dp),
        P(),
        P(dp, tensor),
        P(None, dp, tensor),
        P(tensor, dp),
        P(None, dp, tensor),
        P(tensor, dp),
        P(),
        P(dp, tensor),
        P(None, dp, tensor),
        P(tensor, dp),
        P(None, dp, tensor),
        P(tensor, dp),
        P(),
        P(),
        P(),
    )
    return jax.shard_map(
        per_device, mesh=split, in_specs=in_specs, out_specs=out_specs, check_vma=False
    )
```

time: 871 us -> 671 us (0.77)
  Pallas kernels: 0 us -> 133 us
  local copies, waits for them, and re-layouts: 152 us -> 29.2 us
  matrix products: 137 us -> 25 us
  waiting for transfers between devices: 343 us -> 292 us
  other arithmetic: 118 us -> 98.1 us
  starting transfers between devices: 95.1 us -> 81.3 us
  between operations: 15.5 us -> 2.01 us
    pallas_call x0 -> x13, Pallas kernels: none -> 133 us  [the longest x4 53.7 us: ffn_rows(): pl.pallas_call(lambda *refs: ffn_body(n_parts, n_z, n_alias, *refs), grid...]
    dot_general x19 -> x0, matrix products: 105 us -> none  [the longest x7 34.2 us: dot_rows(): lax.dot_general(left_side, right_side, (((1,), (1,)), ((), ())), preferre...]
    all_gather x1 -> x0, waiting for transfers between devices: 61.2 us -> none  [per_device(): attn_w = lax.all_gather(attn_shard, ('o', 'z', 'x'), axis=0, tiled=True)]
    unnamed x231 -> x150, local copies, waits for them, and re-layouts: 70 us -> 13.7 us
    reshape x12 -> x5, local copies, waits for them, and re-layouts: 36.4 us -> 4.68 us  [the longest x1 2.36 us: per_device(): rounded(w_gateup).reshape(2, depth, n_z, ff_part).transpose(2, 0, 1, 3)]
    all_to_all x4 -> x7, waiting for transfers between devices: 0.01 us -> 30.1 us  [resplit(): return lax.all_to_all(value, 'z', 0, 0, tiled=True)]
    convert_element_type x12 -> x19, other arithmetic: 17.7 us -> 40.1 us  [rounded(): return value.astype(jnp.bfloat16)]
    add x16 -> x5, other arithmetic: 26.3 us -> 5.08 us  [the longest x1 2.89 us: per_device(): grad_mid + inv_one * (grad_normed_one - normed_one * jnp.mean(grad_normed...]
  transfers between devices with their start and end apart: 73 -> 69, of which waited for: 19 -> 38; matrix products, arithmetic and copies ran while one was open for 34% -> 19% of each run, Pallas kernels for 0% -> 20%
where the time goes in v2:
time: 671 us; the launch traced here: 661 us
  waiting for transfers between devices  292 us (44%)
  Pallas kernels  133 us (20%)
  other arithmetic  98.1 us (15%)
  starting transfers between devices  81.3 us (12%)
  local copies, waits for them, and re-layouts  29.2 us (4%)
  matrix products  25 us (4%)
    ppermute x62, waiting for transfers between devices, exchange(): lax.ppermute(value, axis, [(place, place ^ mask) for place in range(size)])  262 us
    pallas_call x4, Pallas kernels, ffn_rows(): pl.pallas_call(lambda *refs: ffn_body(n_parts, n_z, n_alias, *refs), grid...  53.7 us
    ppermute x62, starting transfers between devices, exchange(): lax.ppermute(value, axis, [(place, place ^ mask) for place in range(size)])  53.1 us
    convert_element_type x19, other arithmetic, rounded(): return value.astype(jnp.bfloat16)  40.1 us
    all_to_all x7, waiting for transfers between devices, resplit(): return lax.all_to_all(value, 'z', 0, 0, tiled=True)  30.1 us
    all_to_all x7, starting transfers between devices, resplit(): return lax.all_to_all(value, 'z', 0, 0, tiled=True)  28.1 us
    dot_general x4, matrix products, dot_cols(): lax.dot_general(left_side, right_side, (((0,), (0,)), ((), ())), preferre...  25 us
    sub x5, other arithmetic, stepped(): return weight - RATE * (update * ratio)  19.2 us
  transfers between devices with their start and end apart: 69, of which 38 were waited for; matrix products, arithmetic and copies ran while one was open for 19% of the time, Pallas kernels for 20%

profile of v2, /device:TPU:0, one launch (start us, length us, event | category | flops | bytes accessed | tf_op | source)
XLA Modules:
  0.0 661.2 jit_solution(5515650243756538414)
XLA Ops:
  10.8 4.3 collective-permute-done.2.refs_8_.refs_6_
  15.0 9.8 %collective-permute-done.1.refs_5_.refs_3_ = bf16[256,768]{1,0:T(8,128)(2,1)S(1)} collective-permute-done((bf16[256,768]{1,0:T(8,128)(2,1)S(1)}, bf16[256,768]{1,0:T(8,128)(2,1)S(1)}, u32[]{:S(2)}, u32[]{:S(2)}) %collective-permute-start.1) | collective-permute-done | bytes 393248 | tf_op jit(solution)/shard_map/wqkv_z1/ppermute | solution.py:85
  31.7 9.5 %collective-permute-done.5.refs_10_.refs_8_ = bf16[256,768]{1,0:T(8,128)(2,1)} collective-permute-done((bf16[256,768]{1,0:T(8,128)(2,1)}, bf16[256,768]{1,0:T(8,128)(2,1)}, u32[]{:S(2)}, u32[]{:S(2)}) %collective-permute-start.5) | collective-permute-done | bytes 393248 | tf_op jit(solution)/shard_map/wqkv_x2/ppermute | solution.py:85
  41.2 4.2 collective-permute-done.4.refs_9_.refs_7_
  55.7 4.5 collective-permute-done.8.refs_3_
  83.9 14.7 %attend.1 = (bf16[512,2048]{1,0:T(8,128)(2,1)}, bf16[8,512,128]{2,1,0:T(8,128)(2,1)}, bf16[2,512,128]{2,1,0:T(8,128)(2,1)}, bf16[512,512]{1,0:T(8,128)(2,1)}, f32[512,128]{1,0:T(8,128)}) custom-call(s32[8]{0:T(128)} %add.363.refs_0_, bf16[128,2048]{1,0:T(8,128)(2,1)} %copy-done.32, bf16[128,2048]{1,0:T(8,128)(2,1)} %copy-done.47, ...), custom_call_target="tpu_custom_call" | custom-call | flops 2684354560 | bytes 8388608 | tf_op jit(solution)/shard_map/attend/pallas_call | solution.py:396
  99.4 4.9 mid_rows.1
  109.0 13.5 %collective-permute-done.17 = bf16[128,2048]{1,0:T(8,128)(2,1)S(1)} collective-permute-done((bf16[128,2048]{1,0:T(8,128)(2,1)S(1)}, bf16[128,2048]{1,0:T(8,128)(2,1)S(1)}, u32[]{:S(2)}, u32[]{:S(2)}) %collective-permute-start.17) | collective-permute-done | bytes 524320 | tf_op jit(solution)/shard_map/mid_y/ppermute | solution.py:85
  125.1 5.6 all-to-all-done.refs_4_
  141.0 15.1 %collective-permute-done.21.refs_2_ = bf16[256,2048]{1,0:T(8,128)(2,1)} collective-permute-done((bf16[256,2048]{1,0:T(8,128)(2,1)}, bf16[256,2048]{1,0:T(8,128)(2,1)}, u32[]{:S(2)}, u32[]{:S(2)}) %collective-permute-start.21) | collective-permute-done | bytes 1048608 | tf_op jit(solution)/shard_map/bd0_y/ppermute | solution.py:85
  156.1 13.7 %collective-permute-done.19.refs_1_ = bf16[256,2048]{1,0:T(8,128)(2,1)} collective-permute-done((bf16[256,2048]{1,0:T(8,128)(2,1)}, bf16[256,2048]{1,0:T(8,128)(2,1)}, u32[]{:S(2)}, u32[]{:S(2)}) %collective-permute-start.19) | collective-permute-done | bytes 1048608 | tf_op jit(solution)/shard_map/bd_z1/ppermute | solution.py:85
  174.5 16.2 %collective-permute-done.22.refs_2_ = bf16[256,2048]{1,0:T(8,128)(2,1)S(1)} collective-permute-done((bf16[256,2048]{1,0:T(8,128)(2,1)}, bf16[256,2048]{1,0:T(8,128)(2,1)S(1)}, u32[]{:S(2)}, u32[]{:S(2)}) %collective-permute-start.22) | collective-permute-done | bytes 1048608 | tf_op jit(solution)/shard_map/bd1_y/ppermute | solution.py:85
  197.0 25.7 %collective-permute-done.18.refs_1_ = bf16[256,2048]{1,0:T(8,128)(2,1)} collective-permute-done((bf16[256,2048]{1,0:T(8,128)(2,1)}, bf16[256,2048]{1,0:T(8,128)(2,1)}, u32[]{:S(2)}, u32[]{:S(2)}) %collective-permute-start.18) | collective-permute-done | bytes 1048608 | tf_op jit(solution)/shard_map/bd_z2/ppermute | solution.py:85
  223.7 13.2 %ffn_rows.4 = (bf16[2048,2048]{1,0:T(8,128)(2,1)}, bf16[2048,2048]{1,0:T(8,128)(2,1)}, bf16[2048,512]{1,0:T(8,128)(2,1)}, bf16[2048,1024]{1,0:T(8,128)(2,1)}, bf...) custom-call(s32[15]{0:T(128)} %concatenate.75.refs_0_, bf16[256,2048]{1,0:T(8,128)(2,1)} %pad_maximum_fusion.6.refs_1_, ...), custom_call_target="tpu_custom_call" | custom-call | flops 1048576 | bytes 1048576 | tf_op jit(solution)/shard_map/ffn_rows/pallas_call | solution.py:465
  238.2 9.9 %collective-permute-done.20.refs_1_ = bf16[256,2048]{1,0:T(8,128)(2,1)S(1)} collective-permute-done((bf16[256,2048]{1,0:T(8,128)(2,1)}, bf16[256,2048]{1,0:T(8,128)(2,1)S(1)}, u32[]{:S(2)}, u32[]{:S(2)}) %collective-permute-start.20) | collective-permute-done | bytes 1048608 | tf_op jit(solution)/shard_map/bd_z3/ppermute | solution.py:85
  248.0 13.5 %ffn_rows.5 = (bf16[2048,2048]{1,0:T(8,128)(2,1)}, bf16[2048,2048]{1,0:T(8,128)(2,1)}, bf16[2048,512]{1,0:T(8,128)(2,1)}, bf16[2048,1024]{1,0:T(8,128)(2,1)}, bf...) custom-call(s32[15]{0:T(128)} %concatenate.77.refs_0_, ...), custom_call_target="tpu_custom_call", output_to_operand_aliasing={{0}: (8, {}), {1}: (9, {}), {2}: (10, {}), {3}: (11, {})} | custom-call | flops 1048576 | bytes 1048576 | tf_op jit(solution)/shard_map/ffn_rows/pallas_call | solution.py:465
  270.0 13.3 %ffn_rows.6 = (bf16[2048,2048]{1,0:T(8,128)(2,1)}, bf16[2048,2048]{1,0:T(8,128)(2,1)}, bf16[2048,512]{1,0:T(8,128)(2,1)}, bf16[2048,1024]{1,0:T(8,128)(2,1)}, bf...) custom-call(s32[15]{0:T(128)} %concatenate.81.refs_0_, ...), custom_call_target="tpu_custom_call", output_to_operand_aliasing={{0}: (8, {}), {1}: (9, {}), {2}: (10, {}), {3}: (11, {})} | custom-call | flops 1048576 | bytes 1048576 | tf_op jit(solution)/shard_map/ffn_rows/pallas_call | solution.py:465
  283.3 7.8 %collective-permute-done.28.refs_2_ = bf16[256,2048]{1,0:T(8,128)(2,1)S(1)} collective-permute-done((bf16[256,2048]{1,0:T(8,128)(2,1)S(1)}, bf16[256,2048]{1,0:T(8,128)(2,1)S(1)}, u32[]{:S(2)}, u32[]{:S(2)}) %collective-permute-start.28) | collective-permute-done | bytes 1048608 | tf_op jit(solution)/shard_map/bd3_y/ppermute | solution.py:85
  293.2 5.1 collective-permute-done.27
  302.0 13.7 %ffn_rows.7 = (bf16[2048,2048]{1,0:T(8,128)(2,1)}, bf16[2048,2048]{1,0:T(8,128)(2,1)}, bf16[2048,512]{1,0:T(8,128)(2,1)}, bf16[2048,1024]{1,0:T(8,128)(2,1)}, bf...) custom-call(s32[15]{0:T(128)} %concatenate.76.refs_0_, ...), custom_call_target="tpu_custom_call", output_to_operand_aliasing={{0}: (8, {}), {1}: (9, {}), {2}: (10, {}), {3}: (11, {})} | custom-call | flops 1048576 | bytes 1048576 | tf_op jit(solution)/shard_map/ffn_rows/pallas_call | solution.py:465
  324.3 8.9 %convolution_convert_fusion.3 = bf16[2048,512]{1,0:T(8,128)(2,1)S(1)} fusion(bf16[2048,2048]{1,0:T(8,128)(2,1)} %get-tuple-element.166, bf16[2048,512]{1,0:T(8,128)(2,1)S(1)} %copy-done.3), kind=kOutput, calls=%fused_computation.9 | convolution fusion | flops 4296015872 | bytes 12582912 | tf_op jit(solution)/shard_map/dot_general | solution.py:74
  335.9 9.6 %convolution_convert_fusion = bf16[2048,1024]{1,0:T(8,128)(2,1)S(1)} fusion(bf16[2048,2048]{1,0:T(8,128)(2,1)S(1)} %bitcast.105, bf16[2048,1024]{1,0:T(8,128)(2,1)S(1)} %copy-done.1), kind=kOutput, calls=%fused_computation.5 | convolution fusion | flops 8592031744 | bytes 16777216 | tf_op jit(solution)/shard_map/dot_general | solution.py:74
  349.0 10.9 %out_rows.1 = (bf16[4,256,2048]{2,1,0:T(8,128)(2,1)}, bf16[4,256,2048]{2,1,0:T(8,128)(2,1)}) custom-call(s32[15]{0:T(128)} %concatenate.75.refs_0_, bf16[2048,512]{1,0:T(8,128)(2,1)} %get-tuple-element.170.refs_1_, bf16[4,256,512]{2,1,0:T(8,128)(2,1)} %copy-done.2, bf16[4,256,512]{2,1,0:T(8,128)(2,1)} %copy-done.4), custom_call_target="tpu_custom_call" | custom-call | flops 4194304 | bytes 1048576 | tf_op jit(solution)/shard_map/out_rows/pallas_call | solution.py:524
  365.5 10.6 %collective-permute-done.44 = bf16[128,2048]{1,0:T(8,128)(2,1)S(1)} collective-permute-done((bf16[128,2048]{1,0:T(8,128)(2,1)S(1)}, bf16[128,2048]{1,0:T(8,128)(2,1)S(1)}, u32[]{:S(2)}, u32[]{:S(2)}) %collective-permute-start.44) | collective-permute-done | bytes 524320 | tf_op jit(solution)/shard_map/db3_z/ppermute | solution.py:85
  381.2 4.2 all-to-all-start.2
  385.5 30.0 %collective-permute-done.45 = bf16[128,2048]{1,0:T(8,128)(2,1)} collective-permute-done((bf16[128,2048]{1,0:T(8,128)(2,1)}, bf16[128,2048]{1,0:T(8,128)(2,1)}, u32[]{:S(2)}, u32[]{:S(2)}) %collective-permute-start.45) | collective-permute-done | bytes 524320 | tf_op jit(solution)/shard_map/db2_z/ppermute | solution.py:85
  419.9 6.0 collective-permute-done.35
  437.3 4.5 add_convert_fusion.2
  445.9 16.6 %attend_back.1.refs_1_ = bf16[512,768]{1,0:T(8,128)(2,1)} custom-call(s32[8]{0:T(128)} %add.363.refs_0_, bf16[512,2048]{1,0:T(8,128)(2,1)} %pad_maximum_fusion.4.refs_1_, bf16[256,512]{1,0:T(8,128)(2,1)} %bitcast.121, bf16[256,512]{1,0:T(8,128)(2,1)} %collective-permute-done.8.refs_3_, bf16[256,512]{1,0:T(8,128)(2,1)} %collective-permute-done.7.refs_4_, ...), custom_call_target="tpu_custom_call" | custom-call | flops 3758096384 | bytes 8388608 | tf_op jit(solution)/shard_map/attend_back/pallas_call | solution.py:419
  468.1 5.8 grad_rows.1
  474.5 6.7 %lamb_down.1 = (f32[2048,256]{1,0:T(8,128)}, f32[2048,256]{1,0:T(8,128)}, f32[2048,256]{1,0:T(8,128)}, f32[2,8,128]{2,1,0:T(8,128)}) custom-call(bf16[4,256,512]{2,1,0:T(8,128)(2,1)} %all-to-all-done.2.refs_0_, f32[2048,256]{1,0:T(8,128)} %refs_1_.4, f32[2048,256]{1,0:T(8,128)} %refs_2_.4, f32[2048,256]{1,0:T(8,128)} %refs_3_.3), custom_call_target="tpu_custom_call" | custom-call | flops 10485760 | bytes 13631488 | tf_op jit(solution)/shard_map/lamb_down/pallas_call | solution.py:617
  481.2 9.0 %collective-permute-done.34 = bf16[4,128,2048]{2,1,0:T(8,128)(2,1)} collective-permute-done((bf16[4,128,2048]{2,1,0:T(8,128)(2,1)}, bf16[4,128,2048]{2,1,0:T(8,128)(2,1)}, u32[]{:S(2)}, u32[]{:S(2)}) %collective-permute-start.34) | collective-permute-done | bytes 2097184 | tf_op jit(solution)/shard_map/out_y/ppermute | solution.py:85
  490.2 5.6 add_convert_fusion.1
  497.1 5.0 all-to-all-start.4
  505.6 5.5 collective-permute-done.55
  515.6 12.9 %lamb_gateup.1 = (f32[2,256,2048]{2,1,0:T(8,128)}, f32[2,256,2048]{2,1,0:T(8,128)}, f32[2,256,2048]{2,1,0:T(8,128)}, f32[2,2,8,128]{3,2,1,0:T(8,128)}) custom-call(bf16[4,256,1024]{2,1,0:T(8,128)(2,1)} %copy-done.14, f32[2,256,2048]{2,1,0:T(8,128)} %refs_0_.2, f32[2,256,2048]{2,1,0:T(8,128)} %refs_1_.5, f32[2,256,2048]{2,1,0:T(8,128)} %refs_2_.5), custom_call_target="tpu_custom_call" | custom-call | flops 20971520 | bytes 27262976 | tf_op jit(solution)/shard_map/lamb_gateup/pallas_call | solution.py:586
  533.4 7.5 %collective-permute-done.51 = f32[80,128]{1,0:T(8,128)S(1)} collective-permute-done((f32[80,128]{1,0:T(8,128)S(1)}, f32[80,128]{1,0:T(8,128)S(1)}, u32[]{:S(2)}, u32[]{:S(2)}) %collective-permute-start.51) | collective-permute-done | bytes 40992 | tf_op jit(solution)/shard_map/swap/ppermute | solution.py:85
  544.1 6.1 all-to-all-done.4
  550.2 4.2 all-to-all-start.5
  559.9 11.9 %collective-permute-done.53 = f32[80,128]{1,0:T(8,128)S(1)} collective-permute-done((f32[80,128]{1,0:T(8,128)S(1)}, f32[80,128]{1,0:T(8,128)S(1)}, u32[]{:S(2)}, u32[]{:S(2)}) %collective-permute-start.53) | collective-permute-done | bytes 40992 | tf_op jit(solution)/shard_map/swap/ppermute | solution.py:85
  571.8 4.6 collective-permute-start.54
  576.5 4.9 collective-permute-done.54
  583.7 5.2 multiply_subtract_fusion.1
  593.2 8.9 %multiply_subtract_fusion = f32[2,256,2048]{2,1,0:T(8,128)} fusion(f32[2,256,2048]{2,1,0:T(8,128)} %refs_2_.5, f32[2,256,2048]{2,1,0:T(8,128)} %get-tuple-element.112, f32[2,256,2048]{2,1,0:T(8,128)} %get-tuple-element.118, f32[2]{0:T(128)S(1)} %bitcast.139), kind=kLoop, calls=%fused_computation | loop fusion | flops 7340032 | bytes 16777224 | tf_op jit(solution)/shard_map/sub | solution.py:886
  610.6 18.4 %all-to-all-done.6.grads = bf16[4,256,768]{2,1,0:T(8,128)(2,1)S(1)} async-done(((bf16[4,256,768]{2,1,0:T(8,128)(2,1)}), bf16[4,256,768]{2,1,0:T(8,128)(2,1)S(1)}, u32[]{:S(2)}, u32[]{:S(2)}) %all-to-all-start.6) | async-done | bytes 1572896 | tf_op jit(solution)/shard_map/gqkv_z/all_to_all | solution.py:90
  630.2 4.0 lamb_qkv.1
  644.2 3.9 collective-permute-done.60
  648.1 4.9 collective-permute-done.61
  (367 shorter events, 204.6 us)
Async XLA Ops:
  5.9 18.9 %collective-permute-start.1 = (bf16[256,768]{1,0:T(8,128)(2,1)S(1)}, bf16[256,768]{1,0:T(8,128)(2,1)S(1)}, u32[]{:S(2)}, u32[]{:S(2)}) collective-permute-start(bf16[256,768]{1,0:T(8,128)(2,1)S(1)} %pad_maximum_fusion.8.refs_4_.refs_2_), channel_id=1, source_target_pairs={{0,8},{8,0},{16,24},{24,16},{1,9},{9,1},{17,25},{25,17},{2,10},{10... | collective-permute-start | bytes 1179656 | tf_op jit(solution)/shard_map/wqkv_z1/ppermute | solution.py:85
  7.5 19.8 %collective-permute-start = (bf16[256,768]{1,0:T(8,128)(2,1)S(1)}, bf16[256,768]{1,0:T(8,128)(2,1)}, u32[]{:S(2)}, u32[]{:S(2)}) collective-permute-start(bf16[256,768]{1,0:T(8,128)(2,1)S(1)} %pad_maximum_fusion.8.refs_4_.refs_2_), channel_id=1, source_target_pairs={{0,16},{8,24},{16,0},{24,8},{1,17},{9,25},{17,1},{25,9},{2,18},{10... | collective-permute-start | bytes 1179656 | tf_op jit(solution)/shard_map/wqkv_z2/ppermute | solution.py:85
  27.3 18.1 %collective-permute-start.6 = (bf16[128,2048]{1,0:T(8,128)(2,1)S(1)}, bf16[128,2048]{1,0:T(8,128)(2,1)S(1)}, u32[]{:S(2)}, u32[]{:S(2)}) collective-permute-start(bf16[128,2048]{1,0:T(8,128)(2,1)S(1)} %fusion.4.refs_1_), channel_id=1, source_target_pairs={{0,2},{2,0},{1,3},{3,1},{4,6},{6,4},{5,7},{7,5},{8,10},{10,8},{9,1... | collective-permute-start | bytes 1572872 | tf_op jit(solution)/shard_map/a_y/ppermute | solution.py:85
  29.9 15.5 %collective-permute-start.4 = (bf16[256,768]{1,0:T(8,128)(2,1)}, bf16[256,768]{1,0:T(8,128)(2,1)}, u32[]{:S(2)}, u32[]{:S(2)}) collective-permute-start(bf16[256,768]{1,0:T(8,128)(2,1)} %copy-done.67), channel_id=1, source_target_pairs={{0,4},{4,0},{1,5},{5,1},{2,6},{6,2},{3,7},{7,3},{8,12},{12,8},{9,1... | collective-permute-start | bytes 1179656 | tf_op jit(solution)/shard_map/wqkv_x1/ppermute | solution.py:85
  46.5 37.3 %collective-permute-start.12 = (bf16[256,2048]{1,0:T(8,128)(2,1)}, bf16[256,2048]{1,0:T(8,128)(2,1)}, u32[]{:S(2)}, u32[]{:S(2)}) collective-permute-start(bf16[256,2048]{1,0:T(8,128)(2,1)} %pad_maximum_fusion.5), channel_id=1, source_target_pairs={{0,1},{1,0},{2,3},{3,2},{4,5},{5,4},{6,7},{7,6},{8,9},{9,8},{10,11... | collective-permute-start | bytes 3145736 | tf_op jit(solution)/shard_map/a_c/ppermute | solution.py:85
  49.1 14.8 %collective-permute-start.7 = (bf16[256,512]{1,0:T(8,128)(2,1)S(1)}, bf16[256,512]{1,0:T(8,128)(2,1)}, u32[]{:S(2)}, u32[]{:S(2)}) collective-permute-start(bf16[256,512]{1,0:T(8,128)(2,1)S(1)} %bitcast.119), channel_id=1, source_target_pairs={{0,16},{8,24},{16,0},{24,8},{1,17},{9,25},{17,1},{25,9},{2,18},{10... | collective-permute-start | bytes 786440 | tf_op jit(solution)/shard_map/wout_z2/ppermute | solution.py:85
  68.0 30.5 %collective-permute-start.14 = (bf16[256,512]{1,0:T(8,128)(2,1)}, bf16[256,512]{1,0:T(8,128)(2,1)S(1)}, u32[]{:S(2)}, u32[]{:S(2)}) collective-permute-start(bf16[256,512]{1,0:T(8,128)(2,1)} %collective-permute-done.7.refs_4_), channel_id=1, source_target_pairs={{0,4},{4,0},{1,5},{5,1},{2,6},{6,2},{3,7},{7,3},{8,12},{12,8},{9,1... | collective-permute-start | bytes 786440 | tf_op jit(solution)/shard_map/wout_x2/ppermute | solution.py:85
  68.6 30.0 %collective-permute-start.13 = (bf16[256,512]{1,0:T(8,128)(2,1)}, bf16[256,512]{1,0:T(8,128)(2,1)S(1)}, u32[]{:S(2)}, u32[]{:S(2)}) collective-permute-start(bf16[256,512]{1,0:T(8,128)(2,1)} %collective-permute-done.8.refs_3_), channel_id=1, source_target_pairs={{0,4},{4,0},{1,5},{5,1},{2,6},{6,2},{3,7},{7,3},{8,12},{12,8},{9,1... | collective-permute-start | bytes 786440 | tf_op jit(solution)/shard_map/wout_x1/ppermute | solution.py:85
  72.2 26.4 %collective-permute-start.15 = (bf16[256,512]{1,0:T(8,128)(2,1)}, bf16[256,512]{1,0:T(8,128)(2,1)}, u32[]{:S(2)}, u32[]{:S(2)}) collective-permute-start(bf16[256,512]{1,0:T(8,128)(2,1)} %collective-permute-done.11.refs_5_), channel_id=1, source_target_pairs={{0,4},{4,0},{1,5},{5,1},{2,6},{6,2},{3,7},{7,3},{8,12},{12,8},{9,1... | collective-permute-start | bytes 786440 | tf_op jit(solution)/shard_map/wout_x3/ppermute | solution.py:85
  80.3 50.4 %all-to-all-start = ((bf16[4,2,256,512]{3,2,1,0:T(8,128)(2,1)}), bf16[4,2,256,512]{3,2,1,0:T(8,128)(2,1)S(1)}, u32[]{:S(2)}, u32[]{:S(2)}) async-start(bf16[4,2,256,512]{3,2,1,0:T(8,128)(2,1)} %bitcast.107), calls=%async_computation | async-start | bytes 4194304 | tf_op jit(solution)/shard_map/wgu_z/all_to_all | solution.py:90
  108.4 14.0 %collective-permute-start.17 = (bf16[128,2048]{1,0:T(8,128)(2,1)S(1)}, bf16[128,2048]{1,0:T(8,128)(2,1)S(1)}, u32[]{:S(2)}, u32[]{:S(2)}) collective-permute-start(bf16[128,2048]{1,0:T(8,128)(2,1)S(1)} %add_convert_fusion.15), channel_id=1, source_target_pairs={{0,2},{2,0},{1,3},{3,1},{4,6},{6,4},{5,7},{7,5},{8,10},{10,8},{9,1... | collective-permute-start | bytes 1572872 | tf_op jit(solution)/shard_map/mid_y/ppermute | solution.py:85
  131.7 24.4 %collective-permute-start.21 = (bf16[256,2048]{1,0:T(8,128)(2,1)}, bf16[256,2048]{1,0:T(8,128)(2,1)}, u32[]{:S(2)}, u32[]{:S(2)}) collective-permute-start(bf16[256,2048]{1,0:T(8,128)(2,1)} %pad_maximum_fusion.6.refs_1_), channel_id=1, source_target_pairs={{0,2},{2,0},{1,3},{3,1},{4,6},{6,4},{5,7},{7,5},{8,10},{10,8},{9,1... | collective-permute-start | bytes 3145736 | tf_op jit(solution)/shard_map/bd0_y/ppermute | solution.py:85
  132.2 37.6 %collective-permute-start.19 = (bf16[256,2048]{1,0:T(8,128)(2,1)}, bf16[256,2048]{1,0:T(8,128)(2,1)}, u32[]{:S(2)}, u32[]{:S(2)}) collective-permute-start(bf16[256,2048]{1,0:T(8,128)(2,1)} %pad_maximum_fusion.6.refs_1_), channel_id=1, source_target_pairs={{0,8},{8,0},{16,24},{24,16},{1,9},{9,1},{17,25},{25,17},{2,10},{10... | collective-permute-start | bytes 3145736 | tf_op jit(solution)/shard_map/bd_z1/ppermute | solution.py:85
  132.2 62.3 %collective-permute-start.24 = (bf16[4,2,256,512]{3,2,1,0:T(8,128)(2,1)S(1)}, bf16[4,2,256,512]{3,2,1,0:T(8,128)(2,1)}, u32[]{:S(2)}, u32[]{:S(2)}) collective-permute-start(bf16[4,2,256,512]{3,2,1,0:T(8,128)(2,1)S(1)} %all-to-all-done.refs_4_), channel_id=1, source_target_pairs={{0,4},{4,0},{1,5},{5,1},{2,6},{6,2},{3,7},{7,3},{8,12},{12,8},{9,1... | collective-permute-start | bytes 6291464 | tf_op jit(solution)/shard_map/wgu_x/ppermute | solution.py:85
  137.3 57.2 %all-to-all-start.1 = ((bf16[4,256,512]{2,1,0:T(8,128)(2,1)}), bf16[4,256,512]{2,1,0:T(8,128)(2,1)S(1)}, u32[]{:S(2)}, u32[]{:S(2)}) async-start(bf16[4,256,512]{2,1,0:T(8,128)(2,1)} %bitcast.112), calls=%async_computation.1 | async-start | bytes 2097152 | tf_op jit(solution)/shard_map/wd_z/all_to_all | solution.py:90
  169.9 20.9 %collective-permute-start.22 = (bf16[256,2048]{1,0:T(8,128)(2,1)}, bf16[256,2048]{1,0:T(8,128)(2,1)S(1)}, u32[]{:S(2)}, u32[]{:S(2)}) collective-permute-start(bf16[256,2048]{1,0:T(8,128)(2,1)} %collective-permute-done.19.refs_1_), channel_id=1, source_target_pairs={{0,2},{2,0},{1,3},{3,1},{4,6},{6,4},{5,7},{7,5},{8,10},{10,8},{9,1... | collective-permute-start | bytes 3145736 | tf_op jit(solution)/shard_map/bd1_y/ppermute | solution.py:85
  174.5 48.3 %collective-permute-start.26 = (bf16[512,2048]{1,0:T(8,128)(2,1)}, bf16[512,2048]{1,0:T(8,128)(2,1)}, u32[]{:S(2)}, u32[]{:S(2)}) collective-permute-start(bf16[512,2048]{1,0:T(8,128)(2,1)} %pad_maximum_fusion.1), channel_id=1, source_target_pairs={{0,1},{1,0},{2,3},{3,2},{4,5},{5,4},{6,7},{7,6},{8,9},{9,8},{10,11... | collective-permute-start | bytes 6291464 | tf_op jit(solution)/shard_map/bd0_c/ppermute | solution.py:85
  174.5 48.2 %collective-permute-start.18 = (bf16[256,2048]{1,0:T(8,128)(2,1)}, bf16[256,2048]{1,0:T(8,128)(2,1)}, u32[]{:S(2)}, u32[]{:S(2)}) collective-permute-start(bf16[256,2048]{1,0:T(8,128)(2,1)} %pad_maximum_fusion.6.refs_1_), channel_id=1, source_target_pairs={{0,16},{8,24},{16,0},{24,8},{1,17},{9,25},{17,1},{25,9},{2,18},{10... | collective-permute-start | bytes 3145736 | tf_op jit(solution)/shard_map/bd_z2/ppermute | solution.py:85
  194.5 28.2 %collective-permute-start.25 = (bf16[4,256,512]{2,1,0:T(8,128)(2,1)S(1)}, bf16[4,256,512]{2,1,0:T(8,128)(2,1)S(1)}, u32[]{:S(2)}, u32[]{:S(2)}) collective-permute-start(bf16[4,256,512]{2,1,0:T(8,128)(2,1)S(1)} %all-to-all-done.1.refs_6_.refs_2_), channel_id=1, source_target_pairs={{0,4},{4,0},{1,5},{5,1},{2,6},{6,2},{3,7},{7,3},{8,12},{12,8},{9,1... | collective-permute-start | bytes 3145736 | tf_op jit(solution)/shard_map/wd_x/ppermute | solution.py:85
  196.3 51.8 %collective-permute-start.23 = (bf16[512,2048]{1,0:T(8,128)(2,1)}, bf16[512,2048]{1,0:T(8,128)(2,1)}, u32[]{:S(2)}, u32[]{:S(2)}) collective-permute-start(bf16[512,2048]{1,0:T(8,128)(2,1)} %pad_maximum_fusion), channel_id=1, source_target_pairs={{0,1},{1,0},{2,3},{3,2},{4,5},{5,4},{6,7},{7,6},{8,9},{9,8},{10,11... | collective-permute-start | bytes 6291464 | tf_op jit(solution)/shard_map/bd1_c/ppermute | solution.py:85
  222.7 25.3 %collective-permute-start.20 = (bf16[256,2048]{1,0:T(8,128)(2,1)}, bf16[256,2048]{1,0:T(8,128)(2,1)S(1)}, u32[]{:S(2)}, u32[]{:S(2)}) collective-permute-start(bf16[256,2048]{1,0:T(8,128)(2,1)} %collective-permute-done.18.refs_1_), channel_id=1, source_target_pairs={{0,8},{8,0},{16,24},{24,16},{1,9},{9,1},{17,25},{25,17},{2,10},{10... | collective-permute-start | bytes 3145736 | tf_op jit(solution)/shard_map/bd_z3/ppermute | solution.py:85
  237.0 25.4 %collective-permute-start.29 = (bf16[256,2048]{1,0:T(8,128)(2,1)}, bf16[256,2048]{1,0:T(8,128)(2,1)S(1)}, u32[]{:S(2)}, u32[]{:S(2)}) collective-permute-start(bf16[256,2048]{1,0:T(8,128)(2,1)} %collective-permute-done.18.refs_1_), channel_id=1, source_target_pairs={{0,2},{2,0},{1,3},{3,1},{4,6},{6,4},{5,7},{7,5},{8,10},{10,8},{9,1... | collective-permute-start | bytes 3145736 | tf_op jit(solution)/shard_map/bd2_y/ppermute | solution.py:85
  265.5 25.6 %collective-permute-start.28 = (bf16[256,2048]{1,0:T(8,128)(2,1)S(1)}, bf16[256,2048]{1,0:T(8,128)(2,1)S(1)}, u32[]{:S(2)}, u32[]{:S(2)}) collective-permute-start(bf16[256,2048]{1,0:T(8,128)(2,1)S(1)} %collective-permute-done.20.refs_1_), channel_id=1, source_target_pairs={{0,2},{2,0},{1,3},{3,1},{4,6},{6,4},{5,7},{7,5},{8,10},{10,8},{9,1... | collective-permute-start | bytes 3145736 | tf_op jit(solution)/shard_map/bd3_y/ppermute | solution.py:85
  298.4 22.1 %collective-permute-start.41 = (bf16[256,2048]{1,0:T(8,128)(2,1)}, bf16[256,2048]{1,0:T(8,128)(2,1)}, u32[]{:S(2)}, u32[]{:S(2)}) collective-permute-start(bf16[256,2048]{1,0:T(8,128)(2,1)} %get-tuple-element.157), channel_id=1, source_target_pairs={{0,1},{1,0},{2,3},{3,2},{4,5},{5,4},{6,7},{7,6},{8,9},{9,8},{10,11... | collective-permute-start | bytes 3145736 | tf_op jit(solution)/shard_map/db2_c/ppermute | solution.py:85
  299.5 16.8 %collective-permute-start.39 = (bf16[128,2048]{1,0:T(8,128)(2,1)}, bf16[128,2048]{1,0:T(8,128)(2,1)}, u32[]{:S(2)}, u32[]{:S(2)}) collective-permute-start(bf16[128,2048]{1,0:T(8,128)(2,1)} %add_convert_fusion.13), channel_id=1, source_target_pairs={{0,2},{2,0},{1,3},{3,1},{4,6},{6,4},{5,7},{7,5},{8,10},{10,8},{9,1... | collective-permute-start | bytes 1572872 | tf_op jit(solution)/shard_map/db1_y/ppermute | solution.py:85
  315.8 46.3 %collective-permute-start.37 = (bf16[256,2048]{1,0:T(8,128)(2,1)}, bf16[256,2048]{1,0:T(8,128)(2,1)}, u32[]{:S(2)}, u32[]{:S(2)}) collective-permute-start(bf16[256,2048]{1,0:T(8,128)(2,1)} %get-tuple-element.149), channel_id=1, source_target_pairs={{0,1},{1,0},{2,3},{3,2},{4,5},{5,4},{6,7},{7,6},{8,9},{9,8},{10,11... | collective-permute-start | bytes 3145736 | tf_op jit(solution)/shard_map/db0_c/ppermute | solution.py:85
  318.7 43.1 %collective-permute-start.40 = (bf16[128,2048]{1,0:T(8,128)(2,1)}, bf16[128,2048]{1,0:T(8,128)(2,1)}, u32[]{:S(2)}, u32[]{:S(2)}) collective-permute-start(bf16[128,2048]{1,0:T(8,128)(2,1)} %add_convert_fusion.12), channel_id=1, source_target_pairs={{0,8},{8,0},{16,24},{24,16},{1,9},{9,1},{17,25},{25,17},{2,10},{10... | collective-permute-start | bytes 1572872 | tf_op jit(solution)/shard_map/db1_z/ppermute | solution.py:85
  322.7 42.8 %collective-permute-start.42 = (bf16[128,2048]{1,0:T(8,128)(2,1)}, bf16[128,2048]{1,0:T(8,128)(2,1)}, u32[]{:S(2)}, u32[]{:S(2)}) collective-permute-start(bf16[128,2048]{1,0:T(8,128)(2,1)} %add_convert_fusion.11), channel_id=1, source_target_pairs={{0,2},{2,0},{1,3},{3,1},{4,6},{6,4},{5,7},{7,5},{8,10},{10,8},{9,1... | collective-permute-start | bytes 1572872 | tf_op jit(solution)/shard_map/db2_y/ppermute | solution.py:85
  335.2 24.8 %collective-permute-start.43 = (bf16[128,2048]{1,0:T(8,128)(2,1)}, bf16[128,2048]{1,0:T(8,128)(2,1)}, u32[]{:S(2)}, u32[]{:S(2)}) collective-permute-start(bf16[128,2048]{1,0:T(8,128)(2,1)} %add_convert_fusion.10), channel_id=1, source_target_pairs={{0,2},{2,0},{1,3},{3,1},{4,6},{6,4},{5,7},{7,5},{8,10},{10,8},{9,1... | collective-permute-start | bytes 1572872 | tf_op jit(solution)/shard_map/db3_y/ppermute | solution.py:85
  347.3 31.1 %collective-permute-start.36 = (bf16[4,256,512]{2,1,0:T(8,128)(2,1)}, bf16[4,256,512]{2,1,0:T(8,128)(2,1)}, u32[]{:S(2)}, u32[]{:S(2)}) collective-permute-start(bf16[4,256,512]{2,1,0:T(8,128)(2,1)} %get-tuple-element.238), channel_id=1, source_target_pairs={{0,4},{4,0},{1,5},{5,1},{2,6},{6,2},{3,7},{7,3},{8,12},{12,8},{9,1... | collective-permute-start | bytes 3145736 | tf_op jit(solution)/shard_map/gdown_x/ppermute | solution.py:85
  360.0 77.3 %collective-permute-start.33 = (bf16[4,256,2048]{2,1,0:T(8,128)(2,1)}, bf16[4,256,2048]{2,1,0:T(8,128)(2,1)}, u32[]{:S(2)}, u32[]{:S(2)}) collective-permute-start(bf16[4,256,2048]{2,1,0:T(8,128)(2,1)} %get-tuple-element.172), channel_id=1, source_target_pairs={{0,1},{1,0},{2,3},{3,2},{4,5},{5,4},{6,7},{7,6},{8,9},{9,8},{10,11... | collective-permute-start | bytes 12582920 | tf_op jit(solution)/shard_map/out_c/ppermute | solution.py:85
  361.8 14.3 %collective-permute-start.44 = (bf16[128,2048]{1,0:T(8,128)(2,1)S(1)}, bf16[128,2048]{1,0:T(8,128)(2,1)S(1)}, u32[]{:S(2)}, u32[]{:S(2)}) collective-permute-start(bf16[128,2048]{1,0:T(8,128)(2,1)S(1)} %add_convert_fusion.9), channel_id=1, source_target_pairs={{0,8},{8,0},{16,24},{24,16},{1,9},{9,1},{17,25},{25,17},{2,10},{10... | collective-permute-start | bytes 1572872 | tf_op jit(solution)/shard_map/db3_z/ppermute | solution.py:85
  364.1 21.3 %collective-permute-start.38 = (bf16[128,2048]{1,0:T(8,128)(2,1)}, bf16[128,2048]{1,0:T(8,128)(2,1)}, u32[]{:S(2)}, u32[]{:S(2)}) collective-permute-start(bf16[128,2048]{1,0:T(8,128)(2,1)} %add_convert_fusion.14), channel_id=1, source_target_pairs={{0,2},{2,0},{1,3},{3,1},{4,6},{6,4},{5,7},{7,5},{8,10},{10,8},{9,1... | collective-permute-start | bytes 1572872 | tf_op jit(solution)/shard_map/db0_y/ppermute | solution.py:85
  378.4 37.0 %collective-permute-start.45 = (bf16[128,2048]{1,0:T(8,128)(2,1)}, bf16[128,2048]{1,0:T(8,128)(2,1)}, u32[]{:S(2)}, u32[]{:S(2)}) collective-permute-start(bf16[128,2048]{1,0:T(8,128)(2,1)} %add_convert_fusion.8), channel_id=1, source_target_pairs={{0,16},{8,24},{16,0},{24,8},{1,17},{9,25},{17,1},{25,9},{2,18},{10... | collective-permute-start | bytes 1572872 | tf_op jit(solution)/shard_map/db2_z/ppermute | solution.py:85
  378.4 47.5 %collective-permute-start.35 = (bf16[4,256,1024]{2,1,0:T(8,128)(2,1)}, bf16[4,256,1024]{2,1,0:T(8,128)(2,1)}, u32[]{:S(2)}, u32[]{:S(2)}) collective-permute-start(bf16[4,256,1024]{2,1,0:T(8,128)(2,1)} %get-tuple-element.232), channel_id=1, source_target_pairs={{0,4},{4,0},{1,5},{5,1},{2,6},{6,2},{3,7},{7,3},{8,12},{12,8},{9,1... | collective-permute-start | bytes 6291464 | tf_op jit(solution)/shard_map/ggu_x/ppermute | solution.py:85
  381.2 52.3 %all-to-all-start.2 = ((bf16[4,256,512]{2,1,0:T(8,128)(2,1)}), bf16[4,256,512]{2,1,0:T(8,128)(2,1)}, u32[]{:S(2)}, u32[]{:S(2)}) async-start(bf16[4,256,512]{2,1,0:T(8,128)(2,1)} %add_convert_fusion.5), calls=%async_computation.2 | async-start | bytes 2097152 | tf_op jit(solution)/shard_map/gdown_z/all_to_all | solution.py:90
  418.6 13.8 %collective-permute-start.46 = (bf16[128,2048]{1,0:T(8,128)(2,1)S(1)}, bf16[128,2048]{1,0:T(8,128)(2,1)S(1)}, u32[]{:S(2)}, u32[]{:S(2)}) collective-permute-start(bf16[128,2048]{1,0:T(8,128)(2,1)S(1)} %fusion.17), channel_id=1, source_target_pairs={{0,2},{2,0},{1,3},{3,1},{4,6},{6,4},{5,7},{7,5},{8,10},{10,8},{9,1... | collective-permute-start | bytes 1572872 | tf_op jit(solution)/shard_map/dmid_y/ppermute | solution.py:85
  433.5 62.3 %all-to-all-start.3 = ((bf16[4,256,1024]{2,1,0:T(8,128)(2,1)}), bf16[4,256,1024]{2,1,0:T(8,128)(2,1)S(1)}, u32[]{:S(2)}, u32[]{:S(2)}) async-start(bf16[4,256,1024]{2,1,0:T(8,128)(2,1)} %add_convert_fusion), calls=%async_computation.3 | async-start | bytes 4194304 | tf_op jit(solution)/shard_map/ggu_z/all_to_all | solution.py:90
  441.8 48.3 %collective-permute-start.34 = (bf16[4,128,2048]{2,1,0:T(8,128)(2,1)}, bf16[4,128,2048]{2,1,0:T(8,128)(2,1)}, u32[]{:S(2)}, u32[]{:S(2)}) collective-permute-start(bf16[4,128,2048]{2,1,0:T(8,128)(2,1)} %add_convert_fusion.2), channel_id=1, source_target_pairs={{0,2},{2,0},{1,3},{3,1},{4,6},{6,4},{5,7},{7,5},{8,10},{10,8},{9,1... | collective-permute-start | bytes 6291464 | tf_op jit(solution)/shard_map/out_y/ppermute | solution.py:85
  473.9 28.2 %collective-permute-start.48 = (bf16[256,2048]{1,0:T(8,128)(2,1)}, bf16[256,2048]{1,0:T(8,128)(2,1)}, u32[]{:S(2)}, u32[]{:S(2)}) collective-permute-start(bf16[256,2048]{1,0:T(8,128)(2,1)} %get-tuple-element.194), channel_id=1, source_target_pairs={{0,1},{1,0},{2,3},{3,2},{4,5},{5,4},{6,7},{7,6},{8,9},{9,8},{10,11... | collective-permute-start | bytes 3145736 | tf_op jit(solution)/shard_map/da_c/ppermute | solution.py:85
  474.2 36.9 %collective-permute-start.55 = (bf16[4,256,768]{2,1,0:T(8,128)(2,1)}, bf16[4,256,768]{2,1,0:T(8,128)(2,1)}, u32[]{:S(2)}, u32[]{:S(2)}) collective-permute-start(bf16[4,256,768]{2,1,0:T(8,128)(2,1)} %get-tuple-element.234), channel_id=1, source_target_pairs={{0,4},{4,0},{1,5},{5,1},{2,6},{6,2},{3,7},{7,3},{8,12},{12,8},{9,1... | collective-permute-start | bytes 4718600 | tf_op jit(solution)/shard_map/gqkv_x/ppermute | solution.py:85
  497.1 53.1 %all-to-all-start.4 = ((bf16[4,128,2048]{2,1,0:T(8,128)(2,1)}), bf16[4,128,2048]{2,1,0:T(8,128)(2,1)}, u32[]{:S(2)}, u32[]{:S(2)}) async-start(bf16[4,128,2048]{2,1,0:T(8,128)(2,1)} %add_convert_fusion.1), calls=%async_computation.4 | async-start | bytes 4194304 | tf_op jit(solution)/shard_map/out_z/all_to_all | solution.py:90
  504.2 24.2 %collective-permute-start.49 = (bf16[128,2048]{1,0:T(8,128)(2,1)}, bf16[128,2048]{1,0:T(8,128)(2,1)S(1)}, u32[]{:S(2)}, u32[]{:S(2)}) collective-permute-start(bf16[128,2048]{1,0:T(8,128)(2,1)} %add_convert_fusion.6), channel_id=1, source_target_pairs={{0,2},{2,0},{1,3},{3,1},{4,6},{6,4},{5,7},{7,5},{8,10},{10,8},{9,1... | collective-permute-start | bytes 1572872 | tf_op jit(solution)/shard_map/da_y/ppermute | solution.py:85
  515.3 26.3 %collective-permute-start.56 = (bf16[4,256,512]{2,1,0:T(8,128)(2,1)}, bf16[4,256,512]{2,1,0:T(8,128)(2,1)}, u32[]{:S(2)}, u32[]{:S(2)}) collective-permute-start(bf16[4,256,512]{2,1,0:T(8,128)(2,1)} %get-tuple-element.236), channel_id=1, source_target_pairs={{0,4},{4,0},{1,5},{5,1},{2,6},{6,2},{3,7},{7,3},{8,12},{12,8},{9,1... | collective-permute-start | bytes 3145736 | tf_op jit(solution)/shard_map/gout_x/ppermute | solution.py:85
  540.9 13.5 %collective-permute-start.52 = (f32[80,128]{1,0:T(8,128)S(1)}, f32[80,128]{1,0:T(8,128)S(1)}, u32[]{:S(2)}, u32[]{:S(2)}) collective-permute-start(f32[80,128]{1,0:T(8,128)S(1)} %add.417), channel_id=1, source_target_pairs={{0,2},{2,0},{1,3},{3,1},{4,6},{6,4},{5,7},{7,5},{8,10},{10,8},{9,1... | collective-permute-start | bytes 122888 | tf_op jit(solution)/shard_map/swap/ppermute | solution.py:85
  550.2 38.8 %all-to-all-start.5 = ((bf16[4,256,512]{2,1,0:T(8,128)(2,1)}), bf16[4,256,512]{2,1,0:T(8,128)(2,1)}, u32[]{:S(2)}, u32[]{:S(2)}) async-start(bf16[4,256,512]{2,1,0:T(8,128)(2,1)} %add_convert_fusion.4), calls=%async_computation.5 | async-start | bytes 2097152 | tf_op jit(solution)/shard_map/gout_z/all_to_all | solution.py:90
  554.5 17.3 %collective-permute-start.53 = (f32[80,128]{1,0:T(8,128)S(1)}, f32[80,128]{1,0:T(8,128)S(1)}, u32[]{:S(2)}, u32[]{:S(2)}) collective-permute-start(f32[80,128]{1,0:T(8,128)S(1)} %add.418), channel_id=1, source_target_pairs={{0,8},{8,0},{16,24},{24,16},{1,9},{9,1},{17,25},{25,17},{2,10},{10... | collective-permute-start | bytes 122888 | tf_op jit(solution)/shard_map/swap/ppermute | solution.py:85
  588.9 40.1 %all-to-all-start.6 = ((bf16[4,256,768]{2,1,0:T(8,128)(2,1)}), bf16[4,256,768]{2,1,0:T(8,128)(2,1)S(1)}, u32[]{:S(2)}, u32[]{:S(2)}) async-start(bf16[4,256,768]{2,1,0:T(8,128)(2,1)} %add_convert_fusion.3), calls=%async_computation.6 | async-start | bytes 3145728 | tf_op jit(solution)/shard_map/gqkv_z/all_to_all | solution.py:90
  (95 other events, 1254.4 us)

commit v3 on v2

--- a/solution.py
+++ b/solution.py
@@ -76,18 +76,183 @@
     )
 
 
-def exchange(value, axis, mask, what="swap"):
+class At:
+    (
+        wqkv_z1,
+        wqkv_z2,
+        wqkv_x0,
+        wqkv_z3,
+        wqkv_x1,
+        wqkv_x2,
+        pack,
+        tables,
+        cosine,
+        sine,
+        wout_z1,
+        wout_z2,
+        wout_x0,
+        wqkv_x3,
+        a_y,
+        a_c,
+        wout_z3,
+        wout_x1,
+        wout_x2,
+        wout_x3,
+        wgu_z,
+        attend,
+        mid_c,
+        mid_add,
+        mid_y,
+        pair,
+        bd_z2,
+        bd_z1,
+        wgu_x,
+        wd_z,
+        wd_x,
+        bd_z3,
+        bd0_y,
+        bd0_c,
+        bd1_y,
+        bd1_c,
+        bd2_y,
+        bd2_c,
+        bd3_y,
+        bd3_c,
+        ffn0,
+        ffn1,
+        ffn2,
+        ffn3,
+        db0_c,
+        db0_add,
+        db0_y,
+        db1_c,
+        db1_add,
+        db1_y,
+        db2_c,
+        db2_add,
+        db2_y,
+        db3_c,
+        db3_add,
+        db3_y,
+        db1_z,
+        db3_z,
+        db2_z,
+        gdown,
+        gdown_x,
+        gdown_own,
+        ggu,
+        ggu_x,
+        ggu_own,
+        gqkv,
+        gqkv_x,
+        gqkv_own,
+        gout,
+        gout_x,
+        gout_own,
+        out_rows,
+        gdown_z,
+        out_c,
+        out_add,
+        ffnin,
+        dmid_y,
+        dmid_c,
+        out_y,
+        ggu_z,
+        dmid,
+        attend_back,
+        lamb_down,
+        grad_rows,
+        da_c,
+        da_add,
+        da_y,
+        out_z,
+        lamb_gateup,
+        gout_z,
+        input_grad,
+        gqkv_z,
+        block_out,
+        sums,
+        new_gateup,
+        new_down,
+        new_gains,
+        lamb_out,
+        lamb_qkv,
+        swap,
+    ) = range(100)
+
+
+GATES = {
+    At.wqkv_z3: (At.wqkv_z1, At.wqkv_x0),
+    At.wqkv_x1: (At.wqkv_z2, At.wqkv_x0),
+    At.wqkv_x2: (At.wqkv_x0, At.wqkv_z2),
+    At.a_y: (At.wqkv_z2, At.wqkv_x0),
+    At.wout_z1: (At.wqkv_z3, At.wqkv_x1, At.wqkv_x2, At.a_y, At.pack, At.tables, At.cosine, At.sine),
+    At.wout_z2: (At.wqkv_z3, At.wqkv_x1, At.wqkv_x2, At.a_y, At.pack, At.tables, At.cosine, At.sine),
+    At.wout_x0: (At.wqkv_z3, At.wqkv_x1, At.wqkv_x2, At.a_y, At.pack, At.tables, At.cosine, At.sine),
+    At.wqkv_x3: (At.wqkv_z3, At.wqkv_x1, At.wqkv_x2, At.a_y, At.pack, At.tables, At.cosine, At.sine),
+    At.a_c: (At.wqkv_z3, At.wqkv_x1, At.wqkv_x2, At.a_y, At.pack, At.tables, At.cosine, At.sine),
+    At.wout_z3: (At.wout_z2, At.wout_x0, At.wqkv_x3),
+    At.wout_x1: (At.wout_z1, At.wout_z2, At.wout_x0, At.wqkv_x3, At.wqkv_x1),
+    At.wout_x2: (At.wout_z1, At.wout_z2, At.wout_x0, At.wqkv_x3),
+    At.wgu_z: (At.wout_z3, At.pack),
+    At.pair: (At.wgu_z,),
+    At.wd_x: (At.wgu_x,),
+    At.bd_z3: (At.wout_z3,),
+    At.bd1_y: (At.bd0_y,),
+    At.ffn0: (At.bd_z1,),
+    At.bd2_y: (At.bd_z1,),
+    At.ffn1: (At.bd_z3,),
+    At.bd2_c: (At.ffn1, At.wgu_x),
+    At.bd3_y: (At.ffn0,),
+    At.db1_add: (At.bd3_y, At.db2_c, At.ffn2, At.db0_c),
+    At.db2_add: (At.bd3_y,),
+    At.gdown: (At.db3_c,),
+    At.ggu: (At.gdown,),
+    At.gdown_own: (At.out_rows, At.db0_y),
+    At.ggu_own: (At.gdown_x,),
+    At.db3_z: (At.db1_z,),
+    At.db2_z: (At.gdown_x,),
+    At.ffnin: (At.out_rows, At.gdown_x),
+    At.dmid: (At.ggu_x,),
+    At.attend_back: (At.out_add,),
+    At.gout: (At.gqkv_x,),
+    At.out_z: (At.lamb_down, At.gqkv),
+    At.gout_z: (At.out_z,),
+    At.gqkv_z: (At.gout_z,),
+    At.lamb_down: (At.gqkv,),
+    At.gqkv_own: (At.gqkv, At.gout),
+    At.gout_own: (At.gout,),
+    At.lamb_qkv: (At.new_gateup, At.new_down, At.new_gains, At.lamb_out, At.block_out, At.input_grad),
+    At.sums: (At.gqkv_own,),
+    At.grad_rows: (At.out_c,),
+    At.bd_z1: (At.wout_x0, At.pair),
+    At.out_add: (At.gdown_z,),
+    At.ffn2: (At.bd3_y,),
+}
+MADE = {}
+
+
+def note(what, value):
+    MADE[what] = value
+    return value
+
+
+def hold(what, value):
+    waits = [MADE[name] for name in GATES.get(what, ()) if name in MADE]
+    return after(value, *waits) if waits else value
+
+
+def exchange(value, axis, mask, what=At.swap):
     names = axis if isinstance(axis, tuple) else (axis,)
     size = 1
     for name in names:
         size = size * lax.axis_size(name)
-    with jax.named_scope(what):
-        return lax.ppermute(value, axis, [(place, place ^ mask) for place in range(size)])
+    pairs = [(place, place ^ mask) for place in range(size)]
+    return note(what, lax.ppermute(hold(what, value), axis, pairs))
 
 
 def resplit(value, what):
-    with jax.named_scope(what):
-        return lax.all_to_all(value, "z", 0, 0, tiled=True)
+    return note(what, lax.all_to_all(hold(what, value), "z", 0, 0, tiled=True))
 
 
 def after(value, *others):
@@ -95,26 +260,26 @@
 
 
 def gather_row(value, what):
-    across = exchange(value, "y", 1, what + "_y")
+    across = exchange(value, "y", 1, what)
     return gather_core(value, across, what)
 
 
 def gather_core(value, across, what, *waits):
     pair = jnp.concatenate([value, after(across, *waits)])
-    return (value, across, exchange(pair, "c", 1, what + "_c"))
+    return (value, across, exchange(pair, "c", 1, what + 1))
 
 
 class RowSum:
     def __init__(self, keep, send, what):
         self.keep, self.what = keep, what
         self.tokens = keep.shape[0] // 2
-        self.received = exchange(send, "c", 1, what + "_c")
-
-    def pass_on(self, *waits):
+        self.received = exchange(send, "c", 1, what)
+
+    def pass_on(self):
         tokens = self.tokens
-        received = after(self.received, *waits)
+        received = hold(self.what + 1, self.received)
         passed = rounded(widened(self.keep[tokens:]) + widened(received[tokens:]))
-        self.across = exchange(passed, "y", 1, self.what + "_y")
+        self.across = exchange(passed, "y", 1, self.what + 2)
 
     def total(self):
         tokens = self.tokens
@@ -344,7 +509,10 @@
     gateup = refs[3 : 3 + n_parts]
     down = refs[3 + n_parts : 3 + 2 * n_parts]
     refs = refs[3 + 2 * n_parts + n_alias :]
-    b_rows, d_rows, hid, grad_pair, keep, send, wide, deep, sems = refs
+    b_all, d_all, hid, grad_pair, keep, send, b_rows, d_rows, wide, deep, sems = refs
+    first = pl.multiple_of(scalars[0] * b_rows.shape[0], b_rows.shape[0])
+    own_rows = pl.ds(first, b_rows.shape[0])
+    last = sems.shape[0] - 2
     part = down[0].shape[2]
     copies = start_copies(natural_rows(scalars, pieces, 0, b_rows), sems)
     copies += start_weights(scalars, 7, gateup, (), wide, None, sems, 4)
@@ -352,9 +520,11 @@
     later += start_weights(scalars, 7, (), down, None, deep, sems, len(copies) + 4)
     for copy in copies:
         copy.wait()
+    kept = start_copies([(b_rows, b_all.at[own_rows, :])], sems, last)
     pre = dot_plain(b_rows[...], wide[...])
     for copy in later:
         copy.wait()
+    kept += start_copies([(d_rows, d_all.at[own_rows, :])], sems, last + 1)
     d_hid = dot_plain(d_rows[...], deep[...])
     gate_pre, up_pre = pre[:, :part], pre[:, part:]
     sigma = jax.nn.sigmoid(gate_pre)
@@ -365,6 +535,8 @@
     grad_pair[:, part:] = rounded(d_hid * silu)
     grad_in = rounded(dot_rows(grad_pair[...], wide[...]))
     lay_out(grad_in, scalars, keep, send)
+    for copy in kept:
+        copy.wait()
 
 
 def start_weights(index, first, gateup, down, wide, deep, sems, first_sem=0):
@@ -468,11 +640,13 @@
             num_scalar_prefetch=1,
             grid=(1,),
             in_specs=[HBM] * (3 + 2 * n_parts + n_alias),
-            out_specs=(block(width), block(width), block(part), block(2 * part), whole(width), whole(width)),
+            out_specs=(HBM, HBM, block(part), block(2 * part), whole(width), whole(width)),
             scratch_shapes=[
+                pltpu.VMEM((row_len, width), jnp.bfloat16),
+                pltpu.VMEM((row_len, width), jnp.bfloat16),
                 pltpu.VMEM((width, 2 * part), jnp.bfloat16),
                 pltpu.VMEM((width, part), jnp.bfloat16),
-                pltpu.SemaphoreType.DMA((8 + 3 * n_parts * n_z,)),
+                pltpu.SemaphoreType.DMA((10 + 3 * n_parts * n_z,)),
             ],
         ),
         out_shape=(
@@ -487,6 +661,32 @@
         cost_estimate=cost(row_len * width, 1 << 20),
         name="ffn_rows",
     )(scalars, *pieces, *gateup, *down, *earlier)
+
+
+def weight_grad_body(index, left, right, out):
+    out[0] = rounded(dot_cols(left[...], right[...]))
+
+
+def weight_grad(index, part, left, right, depth, count):
+    rows, wide = right.shape
+    if depth % 128:
+        blocks = rounded(dot_cols(left, right)).reshape(-1, depth, wide)
+        return blocks[index[part * count : (part + 1) * count]]
+    return pl.pallas_call(
+        weight_grad_body,
+        grid_spec=pltpu.PrefetchScalarGridSpec(
+            num_scalar_prefetch=1,
+            grid=(count,),
+            in_specs=[
+                pl.BlockSpec((rows, depth), lambda i, index: (0, index[part * count + i])),
+                pl.BlockSpec((rows, wide), lambda i, index: (0, 0)),
+            ],
+            out_specs=pl.BlockSpec((1, depth, wide), lambda i, index: (i, 0, 0)),
+        ),
+        out_shape=bf16_of(count, depth, wide),
+        cost_estimate=cost(rows * wide, 1 << 20),
+        name="weight_grad",
+    )(index, left, right)
 
 
 def lay_out(value, scalars, keep, send, lead=()):
@@ -657,6 +857,38 @@
     new_moment = BETA * moment + (1.0 - BETA) * gradient
     new_second = BETA * second + (1.0 - BETA) * gradient * gradient
     return (new_moment, new_second, new_moment / (jnp.sqrt(new_second) + LAMB_EPS))
+
+
+def attn_step_body(sums, *refs):
+    query, keyval, out = refs[0:3] + (refs[9],), refs[3:6] + (refs[10],), refs[6:9] + (refs[11],)
+    norms = refs[12]
+    lane = lane_iota(8)
+    row = lax.broadcasted_iota(jnp.int32, (8, 128), 0)
+    kept = jnp.zeros((8, 128), jnp.float32)
+    targets = ((query, ...), (keyval, 0), (keyval, 1), (out, ...))
+    for at, ((weight, moment, second, new), place) in enumerate(targets):
+        update_norm, weight_norm = (
+            jnp.sqrt(jnp.sum(jnp.sum(sums[at, which], axis=0, keepdims=True), axis=1, keepdims=True))
+            for which in range(2)
+        )
+        ratio = weight_norm / update_norm
+        for which, value in enumerate((weight_norm, update_norm, ratio)):
+            kept = jnp.where((row == which) & (lane == at), value, kept)
+        update = moment[place] / (jnp.sqrt(second[place]) + LAMB_EPS) + DECAY * weight[place]
+        new[place] = weight[place] - RATE * (update * ratio)
+    norms[...] = kept
+
+
+def attn_step(sums, query, keyval, out):
+    shapes = [jax.ShapeDtypeStruct(part[0].shape, jnp.float32) for part in (query, keyval, out)]
+    return pl.pallas_call(
+        attn_step_body,
+        in_specs=[VMEM] * 10,
+        out_specs=(VMEM,) * 4,
+        out_shape=(*shapes, jax.ShapeDtypeStruct((8, 128), jnp.float32)),
+        cost_estimate=cost(4 << 20, 6 << 20),
+        name="attn_step",
+    )(sums, *query, *keyval, *out)
 
 
 def per_device(
@@ -682,6 +914,7 @@
     second_gateup,
     second_down,
 ):
+    MADE.clear()
     tok = hidden_in.shape[1]
     width = hidden_in.shape[2]
     row_len = tok * 4
@@ -732,36 +965,16 @@
     inv_one = lax.rsqrt(jnp.mean(x_float * x_float, axis=-1, keepdims=True) + EPS_NORM)
     normed_one = x_float * inv_one
     qkv_own = rounded(jnp.concatenate([w_query, w_keyval[0], w_keyval[1]], axis=1))
-    qkv_near = exchange(qkv_own, "z", 1, "wqkv_z1")
-    qkv_far = exchange(qkv_own, "z", 2, "wqkv_z2")
-    qkv_x0 = to_parts(qkv_own, "wqkv_x0")
-    phase_a = (qkv_near, qkv_far, *qkv_x0)
-    qkv_last = exchange(after(qkv_far, *phase_a), "z", 1, "wqkv_z3")
-    qkv_x1 = to_parts(after(qkv_near, *phase_a), "wqkv_x1")
-    qkv_x2 = to_parts(after(qkv_far, *phase_a), "wqkv_x2")
-    attn_own = after(rounded(normed_one * gain_attn), *phase_a)
-    attn_across = exchange(attn_own, "y", 1, "a_y")
-    phase_b = (qkv_last, *qkv_x1, *qkv_x2, attn_across)
-    out_own = after(rounded(w_out.T), *phase_b)
-    out_near = exchange(out_own, "z", 1, "wout_z1")
-    out_far = exchange(out_own, "z", 2, "wout_z2")
-    out_x0 = to_parts(out_own, "wout_x0")
-    qkv_x3 = to_parts(after(qkv_last, *phase_b), "wqkv_x3")
-    attn_pair = jnp.concatenate([attn_own, after(attn_across, *phase_b)])
-    attn_pieces = (attn_own, attn_across, exchange(attn_pair, "c", 1, "a_c"))
-    phase_c = (out_near, out_far, *out_x0, *qkv_x3)
-    out_last = exchange(after(out_far, *phase_c), "z", 1, "wout_z3")
-    out_x1 = to_parts(after(out_near, *phase_c), "wout_x1")
-    out_x2 = to_parts(after(out_far, *phase_c), "wout_x2")
-    out_x3 = to_parts(out_last, "wout_x3")
-    qkv_w = in_order(
-        (qkv_own, qkv_near, qkv_far, qkv_last), (qkv_x0, qkv_x1, qkv_x2, qkv_x3)
-    )
-    out_w = in_order(
-        (out_own, out_near, out_far, out_last), (out_x0, out_x1, out_x2, out_x3)
-    )
+    qkv_near = exchange(qkv_own, "z", 1, At.wqkv_z1)
+    qkv_far = exchange(qkv_own, "z", 2, At.wqkv_z2)
+    qkv_x0 = to_parts(qkv_own, At.wqkv_x0)
+    qkv_last = exchange(qkv_far, "z", 1, At.wqkv_z3)
+    qkv_x1 = to_parts(qkv_near, At.wqkv_x1)
+    qkv_x2 = to_parts(qkv_far, At.wqkv_x2)
+    attn_own = rounded(normed_one * gain_attn)
+    attn_across = exchange(attn_own, "y", 1, At.a_y)
     gateup_send = rounded(w_gateup).reshape(2, depth, n_z, ff_part).transpose(2, 0, 1, 3)
-    gateup_own = resplit(after(gateup_send, out_last), "wgu_z")
+    note(At.pack, gateup_send)
     segment, doc_place = doc_layout(doc_lengths[0], position)
     cosine, sine_part = rope_tables(doc_place, HD)
     cosine = jnp.concatenate([cosine] * 4, axis=1)
@@ -771,105 +984,112 @@
         jnp.float32(0.0),
         jnp.float32(NEG_FILL),
     )
+    note(At.tables, bias)
+    note(At.cosine, cosine)
+    note(At.sine, sine_part)
+    out_own = rounded(w_out.T)
+    out_near = exchange(out_own, "z", 1, At.wout_z1)
+    out_far = exchange(out_own, "z", 2, At.wout_z2)
+    out_x0 = to_parts(out_own, At.wout_x0)
+    qkv_x3 = to_parts(qkv_last, At.wqkv_x3)
+    attn_pieces = gather_core(attn_own, attn_across, At.a_y)
+    out_last = exchange(out_far, "z", 1, At.wout_z3)
+    out_x1 = to_parts(out_near, At.wout_x1)
+    out_x2 = to_parts(out_far, At.wout_x2)
+    out_x3 = to_parts(out_last, At.wout_x3)
+    qkv_w = in_order(
+        (qkv_own, qkv_near, qkv_far, qkv_last), (qkv_x0, qkv_x1, qkv_x2, qkv_x3)
+    )
+    out_w = in_order(
+        (out_own, out_near, out_far, out_last), (out_x0, out_x1, out_x2, out_x3)
+    )
+    gateup_own = resplit(gateup_send, At.wgu_z)
     attn_input, queries, keyvals, context, logs = attend(
-        after(attn_index, out_last), attn_pieces, qkv_w, cosine, sine_part, bias, local_heads, group_size
+        hold(At.attend, attn_index), attn_pieces, qkv_w, cosine, sine_part, bias, local_heads, group_size
     )
     mid_stream = x_float + scatter_row(
-        *rows_out(attn_index, context, out_w, 0, "mid_rows"), "mid"
+        *rows_out(attn_index, context, out_w, 0, "mid_rows"), At.mid_c
     )
     inv_two = lax.rsqrt(jnp.mean(mid_stream * mid_stream, axis=-1, keepdims=True) + EPS_NORM)
     normed_two = mid_stream * inv_two
 
     pair_own = jnp.concatenate(
-        [rounded(normed_two * gain_ffn), after(out_grad[0], gateup_own)]
-    )
-    pair_far = exchange(pair_own, "z", 2, "bd_z2")
-    pair_near = exchange(pair_own, "z", 1, "bd_z1")
-    pair_rows = {0: gather_row(pair_own, "bd0")}
+        [rounded(normed_two * gain_ffn), hold(At.pair, out_grad[0])]
+    )
+    note(At.pair, pair_own)
+    pair_far = exchange(pair_own, "z", 2, At.bd_z2)
+    pair_near = exchange(pair_own, "z", 1, At.bd_z1)
+    pair_across = exchange(pair_own, "y", 1, At.bd0_y)
+    gateup_w = [gateup_own] + to_parts(gateup_own, At.wgu_x)
     down_turned = rounded(w_down).reshape(n_z, ff_part, depth).transpose(0, 2, 1)
-    down_send = after(down_turned, pair_own)
-    down_own = resplit(down_send, "wd_z")
-    gateup_w = [gateup_own] + [
-        exchange(gateup_own, ("o", "x"), place, "wgu_x") for place in range(1, n_parts)
-    ]
-    down_w = [down_own] + [
-        exchange(after(down_own, gateup_w[-1]), ("o", "x"), place, "wd_x")
-        for place in range(1, n_parts)
-    ]
-
-    pair_last = exchange(
-        after(pair_far, pair_near), "z", 1, "bd_z3"
-    )
-    pair_rows[1] = gather_row(after(pair_near, pair_rows[0][1]), "bd1")
+    down_own = resplit(down_turned, At.wd_z)
+    down_w = [down_own] + to_parts(down_own, At.wd_x)
+    pair_last = exchange(pair_far, "z", 1, At.bd_z3)
+    near_across = exchange(pair_near, "y", 1, At.bd1_y)
+    pair_rows = {0: gather_core(pair_own, pair_across, At.bd0_y)}
+    pair_rows[1] = gather_core(pair_near, near_across, At.bd1_y)
     held, rows = (), {}
 
-    def ffn_row(place, *waits):
+    def ffn_row(place):
         *outs, keep, send = ffn_rows(
-            after(row_scalars(place), *waits),
+            hold(At.ffn0 + place, row_scalars(place)),
             pair_rows[place],
             gateup_w,
             down_w,
             n_z * row_len,
             held,
         )
-        rows[place] = RowSum(keep, send, "db" + str(place))
-        return tuple(outs), send
-
-    held, sent = ffn_row(0, pair_near, pair_far)
-    far_across = exchange(after(pair_far, sent), "y", 1, "bd2_y")
-    held, sent1 = ffn_row(1, pair_last)
-    pair_rows[2] = gather_core(pair_far, far_across, "bd2", sent1)
-    last_across = exchange(after(pair_last, sent), "y", 1, "bd3_y")
-    held, sent2 = ffn_row(2)
-    pair_rows[3] = gather_core(pair_last, last_across, "bd3", sent2)
+        note(At.ffn0 + place, send)
+        rows[place] = RowSum(keep, send, At.db0_c + 3 * place)
+        return tuple(outs)
+
+    held = ffn_row(0)
+    far_across = exchange(pair_far, "y", 1, At.bd2_y)
+    held = ffn_row(1)
+    pair_rows[2] = gather_core(pair_far, far_across, At.bd2_y)
+    last_across = exchange(pair_last, "y", 1, At.bd3_y)
+    held = ffn_row(2)
+    pair_rows[3] = gather_core(pair_last, last_across, At.bd3_y)
     for place in (1, 0, 2):
-        rows[place].pass_on(last_across)
-    held, sent = ffn_row(3, rows[1].received)
+        rows[place].pass_on()
+    held = ffn_row(3)
     rows[3].pass_on()
     ffn_input, grad_full, hidden_act, grad_pair = held
 
-    def parts_of(weight_grad):
-        cut = weight_grad.reshape(n_o, n_z, n_x, depth, weight_grad.shape[1])
+    def others(left, right, what):
+        index = hold(what, ffn_index)
+        made = [weight_grad(index, place, left, right, depth, n_z) for place in parts]
+        note(what, made[-1])
         return [
-            lax.dynamic_index_in_dim(
-                lax.dynamic_index_in_dim(cut, (my_part ^ place) // n_x, 0, keepdims=False),
-                (my_part ^ place) % n_x,
-                1,
-                keepdims=False,
-            )
-            for place in range(n_parts)
+            exchange(piece, ("o", "x"), place, what + 1) for place, piece in zip(parts, made)
         ]
 
-    def part_moves(pieces, what, *waits):
-        return [pieces[0]] + [
-            exchange(after(pieces[place], *waits), ("o", "x"), place, what + "_x")
-            for place in range(1, n_parts)
-        ]
-
-    def part_sum(pieces, *waits):
-        total = widened(after(pieces[0], *waits))
-        for piece in pieces[1:]:
+    def with_own(left, right, moved, what):
+        index = hold(what + 2, ffn_index)
+        own = note(what + 2, weight_grad(index, 0, left, right, depth, n_z))
+        total = widened(own)
+        for piece in moved:
             total = total + widened(piece)
         return rounded(total)
 
-    down_pieces = parts_of(
-        rounded(dot_cols(grad_full, after(hidden_act, rows[3].received)))
-    )
-    gateup_pieces = parts_of(
-        rounded(dot_cols(ffn_input, after(grad_pair, down_pieces[-1])))
-    )
-    down_moves = part_moves(down_pieces, "gdown")
+    near_sum = exchange(rounded(rows[1].total()), "z", 1, At.db1_z)
+    down_moves = others(grad_full, hidden_act, At.gdown)
+    gateup_moves = others(ffn_input, grad_pair, At.ggu)
+    last_sum = exchange(rounded(rows[3].total()), "z", 1, At.db3_z)
+    far_sum = exchange(rounded(rows[2].total() + widened(last_sum)), "z", 2, At.db2_z)
     out_keep, out_send = out_rows(
-        row_scalars(0), after(hidden_act, gateup_pieces[-1]), down_w, row_len
-    )
-    gateup_moves = part_moves(gateup_pieces, "ggu")
-    near_sum = exchange(rounded(rows[1].total()), "z", 1, "db1_z")
-    last_sum = exchange(after(rounded(rows[3].total()), near_sum), "z", 1, "db3_z")
-    far_sum = exchange(
-        after(rounded(rows[2].total() + widened(last_sum)), *down_moves[1:]), "z", 2, "db2_z"
-    )
+        hold(At.out_rows, row_scalars(0)), hidden_act, down_w, row_len
+    )
+    note(At.out_rows, out_send)
+    down_total = with_own(grad_full, hidden_act, down_moves, At.gdown)
+    down_grads = resplit(down_total, At.gdown_z)
+    out_received = exchange(out_send, "c", 1, At.out_c)
+    out_passed = rounded(
+        widened(out_keep[:, tok:]) + widened(hold(At.out_add, out_received)[:, tok:])
+    )
+    note(At.out_add, out_passed)
     grad_ffn_in = rows[0].total() + widened(near_sum) + widened(far_sum)
-    grad_ffn_in = after(grad_ffn_in, out_send, *down_moves[1:])
+    grad_ffn_in = hold(At.ffnin, grad_ffn_in)
 
     gain_grad_ffn = jnp.sum(grad_ffn_in * normed_two, axis=0)
     grad_normed_two = grad_ffn_in * gain_ffn
@@ -877,26 +1097,14 @@
         grad_normed_two
         - normed_two * jnp.mean(grad_normed_two * normed_two, axis=-1, keepdims=True)
     )
-    def ratios_of(totals):
-        norms = jnp.sqrt(jnp.sum(totals.reshape(-1, 2, 1024), axis=2))
-        return norms[:, 1], norms[:, 0], norms[:, 1] / norms[:, 0]
-
-    def stepped(weight, entry, ratio):
-        update = entry[1] / (jnp.sqrt(entry[2]) + LAMB_EPS) + DECAY * weight
-        return weight - RATE * (update * ratio)
-
-    grad_mid_send = rounded(grad_mid)
-    grad_mid_rows = gather_row(grad_mid_send, "dmid")
-    down_grads = resplit(part_sum(down_moves), "gdown_z")
-    grad_mid_full = after(jnp.concatenate(grad_mid_rows), down_grads, *gateup_moves[1:])
-    out_received = exchange(out_send, "c", 1, "out_c")
-    out_passed = rounded(
-        widened(out_keep[:, tok:]) + widened(out_received[:, tok:])
-    )
-    out_across = exchange(out_passed, "y", 1, "out_y")
+    grad_mid_rows = gather_row(rounded(grad_mid), At.dmid_y)
+    out_across = exchange(out_passed, "y", 1, At.out_y)
+    gateup_total = with_own(ffn_input, grad_pair, gateup_moves, At.ggu)
+    gateup_grads = resplit(gateup_total, At.ggu_z)
+    grad_mid_full = hold(At.dmid, jnp.concatenate(grad_mid_rows))
     grad_qkv = attend_back(
-        attn_index,
-        after(grad_mid_full, out_passed),
+        hold(At.attend_back, attn_index),
+        grad_mid_full,
         out_w,
         queries,
         keyvals,
@@ -907,41 +1115,59 @@
         local_heads,
         group_size,
     )
-    qkv_pieces = parts_of(
-        rounded(dot_cols(attn_input, grad_qkv))
-    )
-    qkv_moves = part_moves(qkv_pieces, "gqkv")
-    out_pieces = parts_of(
-        rounded(dot_cols(after(grad_mid_full, *qkv_moves), context))
-    )
-    out_moves = part_moves(out_pieces, "gout")
-    gateup_grads = resplit(after(part_sum(gateup_moves), down_grads), "ggu_z")
+    note(At.attend_back, grad_qkv)
+    qkv_moves = others(attn_input, grad_qkv, At.gqkv)
+    out_moves = others(grad_mid_full, context, At.gout)
+    *down_new, down_sq = lamb_turned(
+        hold(At.lamb_down, down_grads), moment_down, second_down, w_down, 1, "lamb_down"
+    )
+    note(At.lamb_down, down_sq)
+    grad_parts_send = rows_out(
+        hold(At.grad_rows, attn_index), grad_qkv, qkv_w, 0, "grad_rows"
+    )
+    note(At.grad_rows, grad_parts_send[1])
+    grad_attn_in = scatter_row(*grad_parts_send, At.da_c)
     out_total = rounded(
         widened(out_keep[:, :tok]) + widened(out_received[:, :tok]) + widened(out_across)
     )
-    *down_new, down_sq = lamb_turned(
-        after(down_grads, qkv_pieces[-1]), moment_down, second_down, w_down, 1, "lamb_down"
-    )
-    ffn_out = resplit(after(out_total, gateup_grads, down_sq, qkv_pieces[-1]), "out_z")
-    *gateup_new, gateup_sq = lamb_gateup(gateup_grads, moment_gateup, second_gateup, w_gateup)
-    out_grads = resplit(after(part_sum(out_moves), ffn_out, gateup_sq), "gout_z")
-    qkv_total = part_sum(qkv_moves)
-    block_out = rounded(mid_stream + jnp.sum(widened(ffn_out), axis=0))[None]
-    grad_attn_in = scatter_row(*rows_out(attn_index, grad_qkv, qkv_w, 0, "grad_rows"), "da")
+    ffn_out = resplit(out_total, At.out_z)
+    *gateup_new, gateup_sq = lamb_gateup(
+        hold(At.lamb_gateup, gateup_grads), moment_gateup, second_gateup, w_gateup
+    )
+    note(At.lamb_gateup, gateup_sq)
+    wout_total = with_own(grad_mid_full, context, out_moves, At.gout)
+    qkv_total = with_own(attn_input, grad_qkv, qkv_moves, At.gqkv)
+    out_grads = resplit(wout_total, At.gout_z)
     gain_grad_attn = jnp.sum(grad_attn_in * normed_one, axis=0)
     grad_normed_one = grad_attn_in * gain_attn
     input_grad = grad_mid + inv_one * (
         grad_normed_one
         - normed_one * jnp.mean(grad_normed_one * normed_one, axis=-1, keepdims=True)
     )
+    note(At.input_grad, input_grad)
+    qkv_grads = resplit(qkv_total, At.gqkv_z)
+    block_out = rounded(mid_stream + jnp.sum(widened(ffn_out), axis=0))[None]
+    note(At.block_out, block_out)
     gain_rows = 2 * width // 128
     packed = all_sum(
-        jnp.concatenate(
-            [gain_grad_attn.reshape(-1, 128), gain_grad_ffn.reshape(-1, 128)]
-            + [gateup_sq.reshape(-1, 128), down_sq.reshape(-1, 128)]
+        hold(
+            At.sums,
+            jnp.concatenate(
+                [gain_grad_attn.reshape(-1, 128), gain_grad_ffn.reshape(-1, 128)]
+                + [gateup_sq.reshape(-1, 128), down_sq.reshape(-1, 128)]
+            ),
         )
     )
-    qkv_grads = resplit(after(qkv_total, out_grads), "gqkv_z")
+    note(At.sums, packed)
+
+    def ratios_of(totals):
+        norms = jnp.sqrt(jnp.sum(totals.reshape(-1, 2, 1024), axis=2))
+        return norms[:, 1], norms[:, 0], norms[:, 1] / norms[:, 0]
+
+    def stepped(weight, entry, ratio):
+        update = entry[1] / (jnp.sqrt(entry[2]) + LAMB_EPS) + DECAY * weight
+        return weight - RATE * (update * ratio)
+
     ffn_norms = ratios_of(packed[gain_rows:])
     new_gateup = stepped(w_gateup, gateup_new, ffn_norms[2][:2][:, None, None])
     new_down = stepped(w_down, down_new, ffn_norms[2][2])
@@ -954,18 +1180,25 @@
     )
     gain_norms = gain_norms + (gain_norms[0] / gain_norms[1],)
     new_gains = norm_gains - RATE * gain_norms[2][:, None] * gain_update
+    note(At.new_gateup, new_gateup)
+    note(At.new_down, new_down)
+    note(At.new_gains, new_gains)
 
     *out_new, out_sq = lamb_turned(out_grads, moment_out, second_out, w_out, n_z, "lamb_out")
+    note(At.lamb_out, out_sq)
     *qkv_new, qkv_sq = lamb_qkv(
-        after(qkv_grads, new_gateup, new_down, new_gains, out_sq, block_out, input_grad),
+        hold(At.lamb_qkv, qkv_grads),
         (moment_query, second_query, w_query),
         (moment_keyval, second_keyval, w_keyval),
     )
     attn_sq = all_sum(jnp.concatenate([qkv_sq, out_sq[None]]).reshape(-1, 128))
-    attn_norms = ratios_of(attn_sq)
-    new_query = stepped(w_query, qkv_new[:3], attn_norms[2][0])
-    new_keyval = stepped(w_keyval, qkv_new[3:], attn_norms[2][1:3][:, None, None])
-    new_out = stepped(w_out, out_new, attn_norms[2][3])
+    new_query, new_keyval, new_out, norms = attn_step(
+        attn_sq.reshape(4, 2, 8, 128),
+        (w_query, qkv_new[1], qkv_new[2]),
+        (w_keyval, qkv_new[4], qkv_new[5]),
+        (w_out, out_new[1], out_new[2]),
+    )
+    attn_norms = norms[:3, :4]
     results = (qkv_new[:3], qkv_new[3:], out_new, gateup_new, down_new)
     grad_parts = tuple((entry[0] for entry in results))
     new_moments = tuple((entry[1] for entry in results))

time: 671 us -> 640 us (0.954)
  waiting for transfers between devices: 292 us -> 237 us
  Pallas kernels: 133 us -> 185 us
  matrix products: 25 us -> 0 us
  local copies, waits for them, and re-layouts: 29.2 us -> 21.3 us
    pallas_call x0 -> x9, Pallas kernels: none -> 56.5 us  [the longest x8 52.8 us: weight_grad(): pl.pallas_call(weight_grad_body, grid_spec=pltpu.PrefetchScalarGridSpec(n...]
    ppermute x62, waiting for transfers between devices: 262 us -> 212 us  [exchange(): return note(what, lax.ppermute(hold(what, value), axis, pairs))]
    dot_general x4 -> x0, matrix products: 25 us -> none  [dot_cols(): lax.dot_general(left_side, right_side, (((0,), (0,)), ((), ())), preferre...]
    sub x5 -> x2, other arithmetic: 19.2 us -> 14.1 us  [stepped(): return weight - RATE * (update * ratio)]
    concatenate x5 -> x6, other arithmetic: 11.6 us -> 14.3 us  [gather_core(): pair = jnp.concatenate([value, after(across, *waits)])]
    unnamed x150 -> x102, local copies, waits for them, and re-layouts: 13.7 us -> 11.9 us
  transfers between devices with their start and end apart: 69 -> 69, of which waited for: 38 -> 29; matrix products, arithmetic and copies ran while one was open for 19% -> 17% of each run, Pallas kernels for 20% -> 28%
where the time goes in v3:
time: 640 us; the launch traced here: 629 us
  waiting for transfers between devices  237 us (37%)
  Pallas kernels  185 us (29%)
  other arithmetic  99.6 us (16%)
  starting transfers between devices  85.3 us (13%)
  local copies, waits for them, and re-layouts  21.3 us (3%)
    ppermute x62, waiting for transfers between devices, exchange(): return note(what, lax.ppermute(hold(what, value), axis, pairs))  212 us
    ppermute x62, starting transfers between devices, exchange(): return note(what, lax.ppermute(hold(what, value), axis, pairs))  53.1 us
    pallas_call x8, Pallas kernels, weight_grad(): pl.pallas_call(weight_grad_body, grid_spec=pltpu.PrefetchScalarGridSpec(n...  52.8 us
    pallas_call x4, Pallas kernels, ffn_rows(): pl.pallas_call(lambda *refs: ffn_body(n_parts, n_z, n_alias, *refs), grid...  48.3 us
    convert_element_type x19, other arithmetic, rounded(): return value.astype(jnp.bfloat16)  43.3 us
    all_to_all x7, starting transfers between devices, resplit(): return note(what, lax.all_to_all(hold(what, value), 'z', 0, 0, tiled=True))  32.2 us
    all_to_all x7, waiting for transfers between devices, resplit(): return note(what, lax.all_to_all(hold(what, value), 'z', 0, 0, tiled=True))  24.9 us
    pallas_call x1, Pallas kernels, attend_back(): pl.pallas_call(lambda *refs: attend_back_body(n_blocks, heads, group, *re...  16.6 us
  transfers between devices with their start and end apart: 69, of which 29 were waited for; matrix products, arithmetic and copies ran while one was open for 17% of the time, Pallas kernels for 28%

profile of v3, /device:TPU:0, one launch (start us, length us, event | category | flops | bytes accessed | tf_op | source)
XLA Modules:
  0.0 629.2 jit_solution(5452980242620123653)
XLA Ops:
  2.9 4.1 collective-permute-start
  10.9 13.8 %collective-permute-done.refs_6_.refs_4_ = bf16[256,768]{1,0:T(8,128)(2,1)} collective-permute-done((bf16[256,768]{1,0:T(8,128)(2,1)S(1)}, bf16[256,768]{1,0:T(8,128)(2,1)}, u32[]{:S(2)}, u32[]{:S(2)}) %collective-permute-start) | collective-permute-done | bytes 393248 | tf_op jit(solution)/shard_map/ppermute | solution.py:251
  42.7 5.0 collective-permute-done.6.refs_10_.refs_8_
  50.0 5.0 collective-permute-start.9
  55.0 9.5 %collective-permute-done.10.refs_4_ = bf16[256,512]{1,0:T(8,128)(2,1)} collective-permute-done((bf16[256,512]{1,0:T(8,128)(2,1)S(1)}, bf16[256,512]{1,0:T(8,128)(2,1)}, u32[]{:S(2)}, u32[]{:S(2)}) %collective-permute-start.10) | collective-permute-done | bytes 262176 | tf_op jit(solution)/shard_map/ppermute | solution.py:251
  69.5 4.6 collective-permute-done.12.refs_5_
  76.3 5.6 all-to-all-start
  81.9 14.7 %attend.1 = (bf16[512,2048]{1,0:T(8,128)(2,1)}, bf16[8,512,128]{2,1,0:T(8,128)(2,1)}, bf16[2,512,128]{2,1,0:T(8,128)(2,1)}, bf16[512,512]{1,0:T(8,128)(2,1)}, f32[512,128]{1,0:T(8,128)}) custom-call(s32[8]{0:T(128)} %add.295.refs_0_, bf16[128,2048]{1,0:T(8,128)(2,1)} %copy-done.27, bf16[128,2048]{1,0:T(8,128)(2,1)} %collective-permute-done.2.refs_2_, ...), custom_call_target="tpu_custom_call" | custom-call | flops 2684354560 | bytes 8388608 | tf_op jit(solution)/shard_map/attend/pallas_call | solution.py:568
  96.6 4.9 mid_rows.1
  106.2 13.5 %collective-permute-done.17 = bf16[128,2048]{1,0:T(8,128)(2,1)S(1)} collective-permute-done((bf16[128,2048]{1,0:T(8,128)(2,1)S(1)}, bf16[128,2048]{1,0:T(8,128)(2,1)S(1)}, u32[]{:S(2)}, u32[]{:S(2)}) %collective-permute-start.17) | collective-permute-done | bytes 524320 | tf_op jit(solution)/shard_map/ppermute | solution.py:251
  122.3 6.5 %all-to-all-done.refs_4_ = bf16[4,2,256,512]{3,2,1,0:T(8,128)(2,1)S(1)} async-done(((bf16[4,2,256,512]{3,2,1,0:T(8,128)(2,1)}), bf16[4,2,256,512]{3,2,1,0:T(8,128)(2,1)S(1)}, u32[]{:S(2)}, u32[]{:S(2)}) %all-to-all-start) | async-done | bytes 2097184 | tf_op jit(solution)/shard_map/all_to_all | solution.py:255
  138.6 28.9 %collective-permute-done.20.refs_1_ = bf16[256,2048]{1,0:T(8,128)(2,1)} collective-permute-done((bf16[256,2048]{1,0:T(8,128)(2,1)}, bf16[256,2048]{1,0:T(8,128)(2,1)}, u32[]{:S(2)}, u32[]{:S(2)}) %collective-permute-start.20) | collective-permute-done | bytes 1048608 | tf_op jit(solution)/shard_map/ppermute | solution.py:251
  171.1 17.8 %collective-permute-done.28.refs_2_ = bf16[256,2048]{1,0:T(8,128)(2,1)S(1)} collective-permute-done((bf16[256,2048]{1,0:T(8,128)(2,1)}, bf16[256,2048]{1,0:T(8,128)(2,1)S(1)}, u32[]{:S(2)}, u32[]{:S(2)}) %collective-permute-start.28) | collective-permute-done | bytes 1048608 | tf_op jit(solution)/shard_map/ppermute | solution.py:251
  192.8 26.6 %collective-permute-done.18.refs_1_ = bf16[256,2048]{1,0:T(8,128)(2,1)} collective-permute-done((bf16[256,2048]{1,0:T(8,128)(2,1)}, bf16[256,2048]{1,0:T(8,128)(2,1)}, u32[]{:S(2)}, u32[]{:S(2)}) %collective-permute-start.18) | collective-permute-done | bytes 1048608 | tf_op jit(solution)/shard_map/ppermute | solution.py:251
  222.5 11.9 %ffn_rows.4 = (bf16[2048,2048]{1,0:T(8,128)(2,1)}, bf16[2048,2048]{1,0:T(8,128)(2,1)}, bf16[2048,512]{1,0:T(8,128)(2,1)}, bf16[2048,1024]{1,0:T(8,128)(2,1)}, bf...) custom-call(s32[15]{0:T(128)} %concatenate.75.refs_0_, bf16[256,2048]{1,0:T(8,128)(2,1)} %pad_maximum_fusion.6.refs_1_, ...), custom_call_target="tpu_custom_call" | custom-call | flops 1048576 | bytes 1048576 | tf_op jit(solution)/shard_map/ffn_rows/pallas_call | solution.py:637
  234.5 10.2 %collective-permute-done.19.refs_1_ = bf16[256,2048]{1,0:T(8,128)(2,1)S(1)} collective-permute-done((bf16[256,2048]{1,0:T(8,128)(2,1)}, bf16[256,2048]{1,0:T(8,128)(2,1)S(1)}, u32[]{:S(2)}, u32[]{:S(2)}) %collective-permute-start.19) | collective-permute-done | bytes 1048608 | tf_op jit(solution)/shard_map/ppermute | solution.py:251
  249.9 12.3 %ffn_rows.5 = (bf16[2048,2048]{1,0:T(8,128)(2,1)}, bf16[2048,2048]{1,0:T(8,128)(2,1)}, bf16[2048,512]{1,0:T(8,128)(2,1)}, bf16[2048,1024]{1,0:T(8,128)(2,1)}, bf...) custom-call(s32[15]{0:T(128)} %concatenate.82.refs_0_, ...), custom_call_target="tpu_custom_call", output_to_operand_aliasing={{0}: (8, {}), {1}: (9, {}), {2}: (10, {}), {3}: (11, {})} | custom-call | flops 1048576 | bytes 1048576 | tf_op jit(solution)/shard_map/ffn_rows/pallas_call | solution.py:637
  262.4 6.7 %collective-permute-done.25.refs_2_ = bf16[256,2048]{1,0:T(8,128)(2,1)S(1)} collective-permute-done((bf16[256,2048]{1,0:T(8,128)(2,1)S(1)}, bf16[256,2048]{1,0:T(8,128)(2,1)S(1)}, u32[]{:S(2)}, u32[]{:S(2)}) %collective-permute-start.25) | collective-permute-done | bytes 1048608 | tf_op jit(solution)/shard_map/ppermute | solution.py:251
  271.9 12.0 %ffn_rows.6 = (bf16[2048,2048]{1,0:T(8,128)(2,1)}, bf16[2048,2048]{1,0:T(8,128)(2,1)}, bf16[2048,512]{1,0:T(8,128)(2,1)}, bf16[2048,1024]{1,0:T(8,128)(2,1)}, bf...) custom-call(s32[15]{0:T(128)} %concatenate.80.refs_0_, ...), custom_call_target="tpu_custom_call", output_to_operand_aliasing={{0}: (8, {}), {1}: (9, {}), {2}: (10, {}), {3}: (11, {})} | custom-call | flops 1048576 | bytes 1048576 | tf_op jit(solution)/shard_map/ffn_rows/pallas_call | solution.py:637
  286.3 12.1 %ffn_rows.7 = (bf16[2048,2048]{1,0:T(8,128)(2,1)}, bf16[2048,2048]{1,0:T(8,128)(2,1)}, bf16[2048,512]{1,0:T(8,128)(2,1)}, bf16[2048,1024]{1,0:T(8,128)(2,1)}, bf...) custom-call(s32[15]{0:T(128)} %concatenate.76.refs_0_, ...), custom_call_target="tpu_custom_call", output_to_operand_aliasing={{0}: (8, {}), {1}: (9, {}), {2}: (10, {}), {3}: (11, {})} | custom-call | flops 1048576 | bytes 1048576 | tf_op jit(solution)/shard_map/ffn_rows/pallas_call | solution.py:637
  302.6 11.1 %out_rows.1 = (bf16[4,256,2048]{2,1,0:T(8,128)(2,1)}, bf16[4,256,2048]{2,1,0:T(8,128)(2,1)}) custom-call(s32[15]{0:T(128)} %concatenate.75.refs_0_, bf16[2048,512]{1,0:T(8,128)(2,1)} %get-tuple-element.170.refs_1_.right, bf16[4,256,512]{2,1,0:T(8,128)(2,1)} %copy-done.1, bf16[4,256,512]{2,1,0:T(8,128)(2,1)} %copy-done.2), custom_call_target="tpu_custom_call" | custom-call | flops 4194304 | bytes 1048576 | tf_op jit(solution)/shard_map/out_rows/pallas_call | solution.py:724
  322.9 7.0 %weight_grad.9 = bf16[4,256,512]{2,1,0:T(8,128)(2,1)} custom-call(s32[8]{0:T(128)} %copy-done.38, bf16[2048,2048]{1,0:T(8,128)(2,1)} %get-tuple-element.175.left, bf16[2048,512]{1,0:T(8,128)(2,1)} %get-tuple-element.170.refs_1_.right), custom_call_target="tpu_custom_call" | custom-call | flops 1048576 | bytes 1048576 | tf_op jit(solution)/shard_map/weight_grad/pallas_call | solution.py:675
  336.0 9.3 %weight_grad.10 = bf16[4,256,1024]{2,1,0:T(8,128)(2,1)} custom-call(s32[8]{0:T(128)} %copy-done.38, bf16[2048,2048]{1,0:T(8,128)(2,1)} %get-tuple-element.191.left, bf16[2048,1024]{1,0:T(8,128)(2,1)} %get-tuple-element.192.right), custom_call_target="tpu_custom_call" | custom-call | flops 2097152 | bytes 1048576 | tf_op jit(solution)/shard_map/weight_grad/pallas_call | solution.py:675
  349.0 7.3 %collective-permute-done.35 = bf16[4,256,512]{2,1,0:T(8,128)(2,1)} collective-permute-done((bf16[4,256,512]{2,1,0:T(8,128)(2,1)}, bf16[4,256,512]{2,1,0:T(8,128)(2,1)}, u32[]{:S(2)}, u32[]{:S(2)}) %collective-permute-start.35) | collective-permute-done | bytes 1048608 | tf_op jit(solution)/shard_map/ppermute | solution.py:251
  356.3 7.0 %weight_grad.8 = bf16[4,256,512]{2,1,0:T(8,128)(2,1)} custom-call(s32[8]{0:T(128)} %copy-done.38, bf16[2048,2048]{1,0:T(8,128)(2,1)} %get-tuple-element.175.left, bf16[2048,512]{1,0:T(8,128)(2,1)} %get-tuple-element.170.refs_1_.right), custom_call_target="tpu_custom_call" | custom-call | flops 1048576 | bytes 1048576 | tf_op jit(solution)/shard_map/weight_grad/pallas_call | solution.py:675
  366.1 5.1 all-to-all-start.2
  371.2 9.3 %weight_grad.12 = bf16[4,256,1024]{2,1,0:T(8,128)(2,1)} custom-call(s32[8]{0:T(128)} %copy-done.38, bf16[2048,2048]{1,0:T(8,128)(2,1)} %get-tuple-element.191.left, bf16[2048,1024]{1,0:T(8,128)(2,1)} %get-tuple-element.192.right), custom_call_target="tpu_custom_call" | custom-call | flops 2097152 | bytes 1048576 | tf_op jit(solution)/shard_map/weight_grad/pallas_call | solution.py:675
  380.5 11.3 %collective-permute-done.44 = bf16[128,2048]{1,0:T(8,128)(2,1)} collective-permute-done((bf16[128,2048]{1,0:T(8,128)(2,1)}, bf16[128,2048]{1,0:T(8,128)(2,1)}, u32[]{:S(2)}, u32[]{:S(2)}) %collective-permute-start.44) | collective-permute-done | bytes 524320 | tf_op jit(solution)/shard_map/ppermute | solution.py:251
  408.3 4.4 add_convert_fusion.2
  420.1 16.6 %attend_back.1.right.refs_1_ = bf16[512,768]{1,0:T(8,128)(2,1)} custom-call(s32[8]{0:T(128)} %add.295.refs_0_, bf16[512,2048]{1,0:T(8,128)(2,1)} %pad_maximum_fusion.4.refs_1_.left, bf16[256,512]{1,0:T(8,128)(2,1)} %bitcast.76, bf16[256,512]{1,0:T(8,128)(2,1)} %collective-permute-done.9.refs_3_, bf16[256,512]{1,0:T(8,128)(2,1)} %collective-permute-done.10.refs_4_, ...), custom_call_target="tpu_custom_call" | custom-call | flops 3758096384 | bytes 8388608 | tf_op jit(solution)/shard_map/attend_back/pallas_call | solution.py:591
  436.7 5.2 weight_grad.11
  442.4 6.7 %lamb_down.1 = (f32[2048,256]{1,0:T(8,128)}, f32[2048,256]{1,0:T(8,128)}, f32[2048,256]{1,0:T(8,128)}, f32[2,8,128]{2,1,0:T(8,128)}) custom-call(bf16[4,256,512]{2,1,0:T(8,128)(2,1)} %copy-done.20, f32[2048,256]{1,0:T(8,128)} %refs_1_.4, f32[2048,256]{1,0:T(8,128)} %refs_2_.4, f32[2048,256]{1,0:T(8,128)} %refs_3_.4), custom_call_target="tpu_custom_call" | custom-call | flops 10485760 | bytes 13631488 | tf_op jit(solution)/shard_map/lamb_down/pallas_call | solution.py:817
  449.1 10.0 %collective-permute-done.36 = bf16[4,128,2048]{2,1,0:T(8,128)(2,1)} collective-permute-done((bf16[4,128,2048]{2,1,0:T(8,128)(2,1)}, bf16[4,128,2048]{2,1,0:T(8,128)(2,1)}, u32[]{:S(2)}, u32[]{:S(2)}) %collective-permute-start.36) | collective-permute-done | bytes 2097184 | tf_op jit(solution)/shard_map/ppermute | solution.py:251
  459.2 5.6 add_convert_fusion.1
  466.0 5.0 all-to-all-start.3
  471.1 5.8 grad_rows.1
  478.6 4.9 weight_grad.13
  487.6 12.9 %lamb_gateup.1 = (f32[2,256,2048]{2,1,0:T(8,128)}, f32[2,256,2048]{2,1,0:T(8,128)}, f32[2,256,2048]{2,1,0:T(8,128)}, f32[2,2,8,128]{3,2,1,0:T(8,128)}) custom-call(bf16[4,256,1024]{2,1,0:T(8,128)(2,1)} %copy-done.12, f32[2,256,2048]{2,1,0:T(8,128)} %refs_0_.3, f32[2,256,2048]{2,1,0:T(8,128)} %refs_1_.5, f32[2,256,2048]{2,1,0:T(8,128)} %refs_2_.5), custom_call_target="tpu_custom_call" | custom-call | flops 20971520 | bytes 27262976 | tf_op jit(solution)/shard_map/lamb_gateup/pallas_call | solution.py:786
  500.4 5.3 weight_grad.14
  510.3 4.8 weight_grad.15
  518.5 5.1 all-to-all-start.5
  529.1 12.2 %collective-permute-done.54 = f32[80,128]{1,0:T(8,128)S(1)} collective-permute-done((f32[80,128]{1,0:T(8,128)S(1)}, f32[80,128]{1,0:T(8,128)S(1)}, u32[]{:S(2)}, u32[]{:S(2)}) %collective-permute-start.54) | collective-permute-done | bytes 40992 | tf_op jit(solution)/shard_map/ppermute | solution.py:251
  541.3 4.6 collective-permute-start.55
  545.9 4.9 collective-permute-done.55
  552.6 5.2 multiply_subtract_fusion.1
  562.4 8.9 %multiply_subtract_fusion = f32[2,256,2048]{2,1,0:T(8,128)} fusion(f32[2,256,2048]{2,1,0:T(8,128)} %refs_2_.5, f32[2,256,2048]{2,1,0:T(8,128)} %get-tuple-element.120, f32[2,256,2048]{2,1,0:T(8,128)} %get-tuple-element.126, f32[2]{0:T(128)S(1)} %bitcast.91), kind=kLoop, calls=%fused_computation | loop fusion | flops 7340032 | bytes 16777224 | tf_op jit(solution)/shard_map/sub | solution.py:1169
  579.8 18.4 %all-to-all-done.6.grads = bf16[4,256,768]{2,1,0:T(8,128)(2,1)S(1)} async-done(((bf16[4,256,768]{2,1,0:T(8,128)(2,1)}), bf16[4,256,768]{2,1,0:T(8,128)(2,1)S(1)}, u32[]{:S(2)}, u32[]{:S(2)}) %all-to-all-start.6) | async-done | bytes 1572896 | tf_op jit(solution)/shard_map/all_to_all | solution.py:255
  617.0 4.9 collective-permute-done.61
  (310 shorter events, 182.7 us)
Async XLA Ops:
  2.9 21.9 %collective-permute-start = (bf16[256,768]{1,0:T(8,128)(2,1)S(1)}, bf16[256,768]{1,0:T(8,128)(2,1)}, u32[]{:S(2)}, u32[]{:S(2)}) collective-permute-start(bf16[256,768]{1,0:T(8,128)(2,1)S(1)} %pad_maximum_fusion.8.refs_4_.refs_2_), channel_id=1, source_target_pairs={{0,16},{8,24},{16,0},{24,8},{1,17},{9,25},{17,1},{25,9},{2,18},{10... | collective-permute-start | bytes 1179656 | tf_op jit(solution)/shard_map/ppermute | solution.py:251
  7.0 17.8 %collective-permute-start.1 = (bf16[256,768]{1,0:T(8,128)(2,1)S(1)}, bf16[256,768]{1,0:T(8,128)(2,1)S(1)}, u32[]{:S(2)}, u32[]{:S(2)}) collective-permute-start(bf16[256,768]{1,0:T(8,128)(2,1)S(1)} %pad_maximum_fusion.8.refs_4_.refs_2_), channel_id=1, source_target_pairs={{0,4},{4,0},{1,5},{5,1},{2,6},{6,2},{3,7},{7,3},{8,12},{12,8},{9,1... | collective-permute-start | bytes 1179656 | tf_op jit(solution)/shard_map/ppermute | solution.py:251
  8.5 20.8 %collective-permute-start.3 = (bf16[256,768]{1,0:T(8,128)(2,1)S(1)}, bf16[256,768]{1,0:T(8,128)(2,1)}, u32[]{:S(2)}, u32[]{:S(2)}) collective-permute-start(bf16[256,768]{1,0:T(8,128)(2,1)S(1)} %pad_maximum_fusion.8.refs_4_.refs_2_), channel_id=1, source_target_pairs={{0,8},{8,0},{16,24},{24,16},{1,9},{9,1},{17,25},{25,17},{2,10},{10... | collective-permute-start | bytes 1179656 | tf_op jit(solution)/shard_map/ppermute | solution.py:251
  24.8 15.8 %collective-permute-start.2 = (bf16[128,2048]{1,0:T(8,128)(2,1)S(1)}, bf16[128,2048]{1,0:T(8,128)(2,1)}, u32[]{:S(2)}, u32[]{:S(2)}) collective-permute-start(bf16[128,2048]{1,0:T(8,128)(2,1)S(1)} %fusion.4.refs_1_), channel_id=1, source_target_pairs={{0,2},{2,0},{1,3},{3,1},{4,6},{6,4},{5,7},{7,5},{8,10},{10,8},{9,1... | collective-permute-start | bytes 1572872 | tf_op jit(solution)/shard_map/ppermute | solution.py:251
  31.2 16.5 %collective-permute-start.6 = (bf16[256,768]{1,0:T(8,128)(2,1)}, bf16[256,768]{1,0:T(8,128)(2,1)}, u32[]{:S(2)}, u32[]{:S(2)}) collective-permute-start(bf16[256,768]{1,0:T(8,128)(2,1)} %collective-permute-done.refs_6_.refs_4_), channel_id=1, source_target_pairs={{0,4},{4,0},{1,5},{5,1},{2,6},{6,2},{3,7},{7,3},{8,12},{12,8},{9,1... | collective-permute-start | bytes 1179656 | tf_op jit(solution)/shard_map/ppermute | solution.py:251
  47.7 34.2 %collective-permute-start.7 = (bf16[256,2048]{1,0:T(8,128)(2,1)}, bf16[256,2048]{1,0:T(8,128)(2,1)}, u32[]{:S(2)}, u32[]{:S(2)}) collective-permute-start(bf16[256,2048]{1,0:T(8,128)(2,1)} %pad_maximum_fusion.5), channel_id=1, source_target_pairs={{0,1},{1,0},{2,3},{3,2},{4,5},{5,4},{6,7},{7,6},{8,9},{9,8},{10,11... | collective-permute-start | bytes 3145736 | tf_op jit(solution)/shard_map/ppermute | solution.py:251
  47.7 17.4 %collective-permute-start.8 = (bf16[256,768]{1,0:T(8,128)(2,1)}, bf16[256,768]{1,0:T(8,128)(2,1)S(1)}, u32[]{:S(2)}, u32[]{:S(2)}) collective-permute-start(bf16[256,768]{1,0:T(8,128)(2,1)} %collective-permute-done.4.refs_7_.refs_5_), channel_id=1, source_target_pairs={{0,4},{4,0},{1,5},{5,1},{2,6},{6,2},{3,7},{7,3},{8,12},{12,8},{9,1... | collective-permute-start | bytes 1179656 | tf_op jit(solution)/shard_map/ppermute | solution.py:251
  49.3 15.2 %collective-permute-start.10 = (bf16[256,512]{1,0:T(8,128)(2,1)S(1)}, bf16[256,512]{1,0:T(8,128)(2,1)}, u32[]{:S(2)}, u32[]{:S(2)}) collective-permute-start(bf16[256,512]{1,0:T(8,128)(2,1)S(1)} %bitcast.72), channel_id=1, source_target_pairs={{0,16},{8,24},{16,0},{24,8},{1,17},{9,25},{17,1},{25,9},{2,18},{10... | collective-permute-start | bytes 786440 | tf_op jit(solution)/shard_map/ppermute | solution.py:251
  49.4 15.6 %collective-permute-start.11 = (bf16[256,512]{1,0:T(8,128)(2,1)S(1)}, bf16[256,512]{1,0:T(8,128)(2,1)S(1)}, u32[]{:S(2)}, u32[]{:S(2)}) collective-permute-start(bf16[256,512]{1,0:T(8,128)(2,1)S(1)} %bitcast.73), channel_id=1, source_target_pairs={{0,4},{4,0},{1,5},{5,1},{2,6},{6,2},{3,7},{7,3},{8,12},{12,8},{9,1... | collective-permute-start | bytes 786440 | tf_op jit(solution)/shard_map/ppermute | solution.py:251
  50.0 17.3 %collective-permute-start.9 = (bf16[256,512]{1,0:T(8,128)(2,1)S(1)}, bf16[256,512]{1,0:T(8,128)(2,1)}, u32[]{:S(2)}, u32[]{:S(2)}) collective-permute-start(bf16[256,512]{1,0:T(8,128)(2,1)S(1)} %bitcast.74), channel_id=1, source_target_pairs={{0,8},{8,0},{16,24},{24,16},{1,9},{9,1},{17,25},{25,17},{2,10},{10... | collective-permute-start | bytes 786440 | tf_op jit(solution)/shard_map/ppermute | solution.py:251
  67.4 29.2 %collective-permute-start.14 = (bf16[256,512]{1,0:T(8,128)(2,1)}, bf16[256,512]{1,0:T(8,128)(2,1)}, u32[]{:S(2)}, u32[]{:S(2)}) collective-permute-start(bf16[256,512]{1,0:T(8,128)(2,1)} %collective-permute-done.10.refs_4_), channel_id=1, source_target_pairs={{0,4},{4,0},{1,5},{5,1},{2,6},{6,2},{3,7},{7,3},{8,12},{12,8},{9,1... | collective-permute-start | bytes 786440 | tf_op jit(solution)/shard_map/ppermute | solution.py:251
  68.9 27.7 %collective-permute-start.13 = (bf16[256,512]{1,0:T(8,128)(2,1)}, bf16[256,512]{1,0:T(8,128)(2,1)}, u32[]{:S(2)}, u32[]{:S(2)}) collective-permute-start(bf16[256,512]{1,0:T(8,128)(2,1)} %collective-permute-done.9.refs_3_), channel_id=1, source_target_pairs={{0,4},{4,0},{1,5},{5,1},{2,6},{6,2},{3,7},{7,3},{8,12},{12,8},{9,1... | collective-permute-start | bytes 786440 | tf_op jit(solution)/shard_map/ppermute | solution.py:251
  74.1 22.5 %collective-permute-start.15 = (bf16[256,512]{1,0:T(8,128)(2,1)}, bf16[256,512]{1,0:T(8,128)(2,1)}, u32[]{:S(2)}, u32[]{:S(2)}) collective-permute-start(bf16[256,512]{1,0:T(8,128)(2,1)} %collective-permute-done.12.refs_5_), channel_id=1, source_target_pairs={{0,4},{4,0},{1,5},{5,1},{2,6},{6,2},{3,7},{7,3},{8,12},{12,8},{9,1... | collective-permute-start | bytes 786440 | tf_op jit(solution)/shard_map/ppermute | solution.py:251
  76.3 52.6 %all-to-all-start = ((bf16[4,2,256,512]{3,2,1,0:T(8,128)(2,1)}), bf16[4,2,256,512]{3,2,1,0:T(8,128)(2,1)S(1)}, u32[]{:S(2)}, u32[]{:S(2)}) async-start(bf16[4,2,256,512]{3,2,1,0:T(8,128)(2,1)} %bitcast.66), calls=%async_computation | async-start | bytes 4194304 | tf_op jit(solution)/shard_map/all_to_all | solution.py:255
  129.9 37.6 %collective-permute-start.20 = (bf16[256,2048]{1,0:T(8,128)(2,1)}, bf16[256,2048]{1,0:T(8,128)(2,1)}, u32[]{:S(2)}, u32[]{:S(2)}) collective-permute-start(bf16[256,2048]{1,0:T(8,128)(2,1)} %pad_maximum_fusion.6.refs_1_), channel_id=1, source_target_pairs={{0,8},{8,0},{16,24},{24,16},{1,9},{9,1},{17,25},{25,17},{2,10},{10... | collective-permute-start | bytes 3145736 | tf_op jit(solution)/shard_map/ppermute | solution.py:251
  129.9 37.6 %collective-permute-start.21 = (bf16[256,2048]{1,0:T(8,128)(2,1)}, bf16[256,2048]{1,0:T(8,128)(2,1)}, u32[]{:S(2)}, u32[]{:S(2)}) collective-permute-start(bf16[256,2048]{1,0:T(8,128)(2,1)} %pad_maximum_fusion.6.refs_1_), channel_id=1, source_target_pairs={{0,2},{2,0},{1,3},{3,1},{4,6},{6,4},{5,7},{7,5},{8,10},{10,8},{9,1... | collective-permute-start | bytes 3145736 | tf_op jit(solution)/shard_map/ppermute | solution.py:251
  130.4 61.8 %collective-permute-start.23 = (bf16[4,2,256,512]{3,2,1,0:T(8,128)(2,1)S(1)}, bf16[4,2,256,512]{3,2,1,0:T(8,128)(2,1)}, u32[]{:S(2)}, u32[]{:S(2)}) collective-permute-start(bf16[4,2,256,512]{3,2,1,0:T(8,128)(2,1)S(1)} %all-to-all-done.refs_4_), channel_id=1, source_target_pairs={{0,4},{4,0},{1,5},{5,1},{2,6},{6,2},{3,7},{7,3},{8,12},{12,8},{9,1... | collective-permute-start | bytes 6291464 | tf_op jit(solution)/shard_map/ppermute | solution.py:251
  134.9 57.2 %all-to-all-start.1 = ((bf16[4,256,512]{2,1,0:T(8,128)(2,1)}), bf16[4,256,512]{2,1,0:T(8,128)(2,1)S(1)}, u32[]{:S(2)}, u32[]{:S(2)}) async-start(bf16[4,256,512]{2,1,0:T(8,128)(2,1)} %bitcast.70), calls=%async_computation.1 | async-start | bytes 2097152 | tf_op jit(solution)/shard_map/all_to_all | solution.py:255
  167.5 21.4 %collective-permute-start.28 = (bf16[256,2048]{1,0:T(8,128)(2,1)}, bf16[256,2048]{1,0:T(8,128)(2,1)S(1)}, u32[]{:S(2)}, u32[]{:S(2)}) collective-permute-start(bf16[256,2048]{1,0:T(8,128)(2,1)} %collective-permute-done.20.refs_1_), channel_id=1, source_target_pairs={{0,2},{2,0},{1,3},{3,1},{4,6},{6,4},{5,7},{7,5},{8,10},{10,8},{9,1... | collective-permute-start | bytes 3145736 | tf_op jit(solution)/shard_map/ppermute | solution.py:251
  171.1 50.5 %collective-permute-start.22 = (bf16[512,2048]{1,0:T(8,128)(2,1)}, bf16[512,2048]{1,0:T(8,128)(2,1)}, u32[]{:S(2)}, u32[]{:S(2)}) collective-permute-start(bf16[512,2048]{1,0:T(8,128)(2,1)} %pad_maximum_fusion), channel_id=1, source_target_pairs={{0,1},{1,0},{2,3},{3,2},{4,5},{5,4},{6,7},{7,6},{8,9},{9,8},{10,11... | collective-permute-start | bytes 6291464 | tf_op jit(solution)/shard_map/ppermute | solution.py:251
  171.1 48.2 %collective-permute-start.18 = (bf16[256,2048]{1,0:T(8,128)(2,1)}, bf16[256,2048]{1,0:T(8,128)(2,1)}, u32[]{:S(2)}, u32[]{:S(2)}) collective-permute-start(bf16[256,2048]{1,0:T(8,128)(2,1)} %pad_maximum_fusion.6.refs_1_), channel_id=1, source_target_pairs={{0,16},{8,24},{16,0},{24,8},{1,17},{9,25},{17,1},{25,9},{2,18},{10... | collective-permute-start | bytes 3145736 | tf_op jit(solution)/shard_map/ppermute | solution.py:251
  192.1 57.8 %collective-permute-start.29 = (bf16[512,2048]{1,0:T(8,128)(2,1)}, bf16[512,2048]{1,0:T(8,128)(2,1)}, u32[]{:S(2)}, u32[]{:S(2)}) collective-permute-start(bf16[512,2048]{1,0:T(8,128)(2,1)} %pad_maximum_fusion.3), channel_id=1, source_target_pairs={{0,1},{1,0},{2,3},{3,2},{4,5},{5,4},{6,7},{7,6},{8,9},{9,8},{10,11... | collective-permute-start | bytes 6291464 | tf_op jit(solution)/shard_map/ppermute | solution.py:251
  192.2 29.4 %collective-permute-start.24 = (bf16[4,256,512]{2,1,0:T(8,128)(2,1)S(1)}, bf16[4,256,512]{2,1,0:T(8,128)(2,1)S(1)}, u32[]{:S(2)}, u32[]{:S(2)}) collective-permute-start(bf16[4,256,512]{2,1,0:T(8,128)(2,1)S(1)} %all-to-all-done.1.refs_6_.refs_2_), channel_id=1, source_target_pairs={{0,4},{4,0},{1,5},{5,1},{2,6},{6,2},{3,7},{7,3},{8,12},{12,8},{9,1... | collective-permute-start | bytes 3145736 | tf_op jit(solution)/shard_map/ppermute | solution.py:251
  219.4 25.3 %collective-permute-start.19 = (bf16[256,2048]{1,0:T(8,128)(2,1)}, bf16[256,2048]{1,0:T(8,128)(2,1)S(1)}, u32[]{:S(2)}, u32[]{:S(2)}) collective-permute-start(bf16[256,2048]{1,0:T(8,128)(2,1)} %collective-permute-done.18.refs_1_), channel_id=1, source_target_pairs={{0,8},{8,0},{16,24},{24,16},{1,9},{9,1},{17,25},{25,17},{2,10},{10... | collective-permute-start | bytes 3145736 | tf_op jit(solution)/shard_map/ppermute | solution.py:251
  219.4 27.5 %collective-permute-start.27 = (bf16[256,2048]{1,0:T(8,128)(2,1)}, bf16[256,2048]{1,0:T(8,128)(2,1)}, u32[]{:S(2)}, u32[]{:S(2)}) collective-permute-start(bf16[256,2048]{1,0:T(8,128)(2,1)} %collective-permute-done.18.refs_1_), channel_id=1, source_target_pairs={{0,2},{2,0},{1,3},{3,1},{4,6},{6,4},{5,7},{7,5},{8,10},{10,8},{9,1... | collective-permute-start | bytes 3145736 | tf_op jit(solution)/shard_map/ppermute | solution.py:251
  244.7 24.4 %collective-permute-start.25 = (bf16[256,2048]{1,0:T(8,128)(2,1)S(1)}, bf16[256,2048]{1,0:T(8,128)(2,1)S(1)}, u32[]{:S(2)}, u32[]{:S(2)}) collective-permute-start(bf16[256,2048]{1,0:T(8,128)(2,1)S(1)} %collective-permute-done.19.refs_1_), channel_id=1, source_target_pairs={{0,2},{2,0},{1,3},{3,1},{4,6},{6,4},{5,7},{7,5},{8,10},{10,8},{9,1... | collective-permute-start | bytes 3145736 | tf_op jit(solution)/shard_map/ppermute | solution.py:251
  271.4 27.2 %collective-permute-start.32 = (bf16[256,2048]{1,0:T(8,128)(2,1)}, bf16[256,2048]{1,0:T(8,128)(2,1)S(1)}, u32[]{:S(2)}, u32[]{:S(2)}) collective-permute-start(bf16[256,2048]{1,0:T(8,128)(2,1)} %get-tuple-element.150), channel_id=1, source_target_pairs={{0,1},{1,0},{2,3},{3,2},{4,5},{5,4},{6,7},{7,6},{8,9},{9,8},{10,11... | collective-permute-start | bytes 3145736 | tf_op jit(solution)/shard_map/ppermute | solution.py:251
  271.8 26.8 %collective-permute-start.37 = (bf16[256,2048]{1,0:T(8,128)(2,1)}, bf16[256,2048]{1,0:T(8,128)(2,1)}, u32[]{:S(2)}, u32[]{:S(2)}) collective-permute-start(bf16[256,2048]{1,0:T(8,128)(2,1)} %get-tuple-element.160), channel_id=1, source_target_pairs={{0,1},{1,0},{2,3},{3,2},{4,5},{5,4},{6,7},{7,6},{8,9},{9,8},{10,11... | collective-permute-start | bytes 3145736 | tf_op jit(solution)/shard_map/ppermute | solution.py:251
  298.4 15.5 %collective-permute-start.34 = (bf16[256,2048]{1,0:T(8,128)(2,1)}, bf16[256,2048]{1,0:T(8,128)(2,1)}, u32[]{:S(2)}, u32[]{:S(2)}) collective-permute-start(bf16[256,2048]{1,0:T(8,128)(2,1)} %get-tuple-element.176), channel_id=1, source_target_pairs={{0,1},{1,0},{2,3},{3,2},{4,5},{5,4},{6,7},{7,6},{8,9},{9,8},{10,11... | collective-permute-start | bytes 3145736 | tf_op jit(solution)/shard_map/ppermute | solution.py:251
  301.1 15.5 %collective-permute-start.39 = (bf16[128,2048]{1,0:T(8,128)(2,1)}, bf16[128,2048]{1,0:T(8,128)(2,1)}, u32[]{:S(2)}, u32[]{:S(2)}) collective-permute-start(bf16[128,2048]{1,0:T(8,128)(2,1)} %add_convert_fusion.13), channel_id=1, source_target_pairs={{0,2},{2,0},{1,3},{3,1},{4,6},{6,4},{5,7},{7,5},{8,10},{10,8},{9,1... | collective-permute-start | bytes 1572872 | tf_op jit(solution)/shard_map/ppermute | solution.py:251
  313.7 94.7 %collective-permute-start.31 = (bf16[4,256,2048]{2,1,0:T(8,128)(2,1)}, bf16[4,256,2048]{2,1,0:T(8,128)(2,1)}, u32[]{:S(2)}, u32[]{:S(2)}) collective-permute-start(bf16[4,256,2048]{2,1,0:T(8,128)(2,1)} %get-tuple-element.172), channel_id=1, source_target_pairs={{0,1},{1,0},{2,3},{3,2},{4,5},{5,4},{6,7},{7,6},{8,9},{9,8},{10,11... | collective-permute-start | bytes 12582920 | tf_op jit(solution)/shard_map/ppermute | solution.py:251
  316.1 15.1 %collective-permute-start.42 = (bf16[128,2048]{1,0:T(8,128)(2,1)}, bf16[128,2048]{1,0:T(8,128)(2,1)}, u32[]{:S(2)}, u32[]{:S(2)}) collective-permute-start(bf16[128,2048]{1,0:T(8,128)(2,1)} %add_convert_fusion.10), channel_id=1, source_target_pairs={{0,2},{2,0},{1,3},{3,1},{4,6},{6,4},{5,7},{7,5},{8,10},{10,8},{9,1... | collective-permute-start | bytes 1572872 | tf_op jit(solution)/shard_map/ppermute | solution.py:251
  321.4 24.0 %collective-permute-start.41 = (bf16[128,2048]{1,0:T(8,128)(2,1)}, bf16[128,2048]{1,0:T(8,128)(2,1)}, u32[]{:S(2)}, u32[]{:S(2)}) collective-permute-start(bf16[128,2048]{1,0:T(8,128)(2,1)} %add_convert_fusion.11), channel_id=1, source_target_pairs={{0,2},{2,0},{1,3},{3,1},{4,6},{6,4},{5,7},{7,5},{8,10},{10,8},{9,1... | collective-permute-start | bytes 1572872 | tf_op jit(solution)/shard_map/ppermute | solution.py:251
  329.9 26.4 %collective-permute-start.35 = (bf16[4,256,512]{2,1,0:T(8,128)(2,1)}, bf16[4,256,512]{2,1,0:T(8,128)(2,1)}, u32[]{:S(2)}, u32[]{:S(2)}) collective-permute-start(bf16[4,256,512]{2,1,0:T(8,128)(2,1)} %weight_grad.9), channel_id=1, source_target_pairs={{0,4},{4,0},{1,5},{5,1},{2,6},{6,2},{3,7},{7,3},{8,12},{12,8},{9,1... | collective-permute-start | bytes 3145736 | tf_op jit(solution)/shard_map/ppermute | solution.py:251
  335.2 21.1 %collective-permute-start.33 = (bf16[128,2048]{1,0:T(8,128)(2,1)}, bf16[128,2048]{1,0:T(8,128)(2,1)S(1)}, u32[]{:S(2)}, u32[]{:S(2)}) collective-permute-start(bf16[128,2048]{1,0:T(8,128)(2,1)} %add_convert_fusion.14), channel_id=1, source_target_pairs={{0,2},{2,0},{1,3},{3,1},{4,6},{6,4},{5,7},{7,5},{8,10},{10,8},{9,1... | collective-permute-start | bytes 1572872 | tf_op jit(solution)/shard_map/ppermute | solution.py:251
  345.4 54.3 %collective-permute-start.47 = (bf16[4,256,1024]{2,1,0:T(8,128)(2,1)}, bf16[4,256,1024]{2,1,0:T(8,128)(2,1)}, u32[]{:S(2)}, u32[]{:S(2)}) collective-permute-start(bf16[4,256,1024]{2,1,0:T(8,128)(2,1)} %weight_grad.10), channel_id=1, source_target_pairs={{0,4},{4,0},{1,5},{5,1},{2,6},{6,2},{3,7},{7,3},{8,12},{12,8},{9,1... | collective-permute-start | bytes 6291464 | tf_op jit(solution)/shard_map/ppermute | solution.py:251
  356.3 35.5 %collective-permute-start.44 = (bf16[128,2048]{1,0:T(8,128)(2,1)}, bf16[128,2048]{1,0:T(8,128)(2,1)}, u32[]{:S(2)}, u32[]{:S(2)}) collective-permute-start(bf16[128,2048]{1,0:T(8,128)(2,1)} %add_convert_fusion.8), channel_id=1, source_target_pairs={{0,16},{8,24},{16,0},{24,8},{1,17},{9,25},{17,1},{25,9},{2,18},{10... | collective-permute-start | bytes 1572872 | tf_op jit(solution)/shard_map/ppermute | solution.py:251
  366.1 37.4 %all-to-all-start.2 = ((bf16[4,256,512]{2,1,0:T(8,128)(2,1)}), bf16[4,256,512]{2,1,0:T(8,128)(2,1)S(1)}, u32[]{:S(2)}, u32[]{:S(2)}) async-start(bf16[4,256,512]{2,1,0:T(8,128)(2,1)} %add_convert_fusion.5), calls=%async_computation.2 | async-start | bytes 2097152 | tf_op jit(solution)/shard_map/all_to_all | solution.py:255
  395.3 18.0 %collective-permute-start.45 = (bf16[128,2048]{1,0:T(8,128)(2,1)}, bf16[128,2048]{1,0:T(8,128)(2,1)}, u32[]{:S(2)}, u32[]{:S(2)}) collective-permute-start(bf16[128,2048]{1,0:T(8,128)(2,1)} %fusion.16), channel_id=1, source_target_pairs={{0,2},{2,0},{1,3},{3,1},{4,6},{6,4},{5,7},{7,5},{8,10},{10,8},{9,1... | collective-permute-start | bytes 1572872 | tf_op jit(solution)/shard_map/ppermute | solution.py:251
  404.5 60.2 %all-to-all-start.4 = ((bf16[4,256,1024]{2,1,0:T(8,128)(2,1)}), bf16[4,256,1024]{2,1,0:T(8,128)(2,1)S(1)}, u32[]{:S(2)}, u32[]{:S(2)}) async-start(bf16[4,256,1024]{2,1,0:T(8,128)(2,1)} %add_convert_fusion), calls=%async_computation.4 | async-start | bytes 4194304 | tf_op jit(solution)/shard_map/all_to_all | solution.py:255
  412.8 46.4 %collective-permute-start.36 = (bf16[4,128,2048]{2,1,0:T(8,128)(2,1)}, bf16[4,128,2048]{2,1,0:T(8,128)(2,1)}, u32[]{:S(2)}, u32[]{:S(2)}) collective-permute-start(bf16[4,128,2048]{2,1,0:T(8,128)(2,1)} %add_convert_fusion.2), channel_id=1, source_target_pairs={{0,2},{2,0},{1,3},{3,1},{4,6},{6,4},{5,7},{7,5},{8,10},{10,8},{9,1... | collective-permute-start | bytes 6291464 | tf_op jit(solution)/shard_map/ppermute | solution.py:251
  441.9 36.8 %collective-permute-start.50 = (bf16[4,256,768]{2,1,0:T(8,128)(2,1)}, bf16[4,256,768]{2,1,0:T(8,128)(2,1)}, u32[]{:S(2)}, u32[]{:S(2)}) collective-permute-start(bf16[4,256,768]{2,1,0:T(8,128)(2,1)} %weight_grad.11), channel_id=1, source_target_pairs={{0,4},{4,0},{1,5},{5,1},{2,6},{6,2},{3,7},{7,3},{8,12},{12,8},{9,1... | collective-permute-start | bytes 4718600 | tf_op jit(solution)/shard_map/ppermute | solution.py:251
  466.0 52.5 %all-to-all-start.3 = ((bf16[4,128,2048]{2,1,0:T(8,128)(2,1)}), bf16[4,128,2048]{2,1,0:T(8,128)(2,1)}, u32[]{:S(2)}, u32[]{:S(2)}) async-start(bf16[4,128,2048]{2,1,0:T(8,128)(2,1)} %add_convert_fusion.1), calls=%async_computation.3 | async-start | bytes 4194304 | tf_op jit(solution)/shard_map/all_to_all | solution.py:255
  483.5 32.2 %collective-permute-start.56 = (bf16[4,256,512]{2,1,0:T(8,128)(2,1)}, bf16[4,256,512]{2,1,0:T(8,128)(2,1)}, u32[]{:S(2)}, u32[]{:S(2)}) collective-permute-start(bf16[4,256,512]{2,1,0:T(8,128)(2,1)} %weight_grad.13), channel_id=1, source_target_pairs={{0,4},{4,0},{1,5},{5,1},{2,6},{6,2},{3,7},{7,3},{8,12},{12,8},{9,1... | collective-permute-start | bytes 3145736 | tf_op jit(solution)/shard_map/ppermute | solution.py:251
  486.0 19.7 %collective-permute-start.49 = (bf16[128,2048]{1,0:T(8,128)(2,1)}, bf16[128,2048]{1,0:T(8,128)(2,1)S(1)}, u32[]{:S(2)}, u32[]{:S(2)}) collective-permute-start(bf16[128,2048]{1,0:T(8,128)(2,1)} %add_convert_fusion.6), channel_id=1, source_target_pairs={{0,2},{2,0},{1,3},{3,1},{4,6},{6,4},{5,7},{7,5},{8,10},{10,8},{9,1... | collective-permute-start | bytes 1572872 | tf_op jit(solution)/shard_map/ppermute | solution.py:251
  518.5 39.3 %all-to-all-start.5 = ((bf16[4,256,512]{2,1,0:T(8,128)(2,1)}), bf16[4,256,512]{2,1,0:T(8,128)(2,1)}, u32[]{:S(2)}, u32[]{:S(2)}) async-start(bf16[4,256,512]{2,1,0:T(8,128)(2,1)} %add_convert_fusion.4), calls=%async_computation.5 | async-start | bytes 2097152 | tf_op jit(solution)/shard_map/all_to_all | solution.py:255
  523.6 17.6 %collective-permute-start.54 = (f32[80,128]{1,0:T(8,128)S(1)}, f32[80,128]{1,0:T(8,128)S(1)}, u32[]{:S(2)}, u32[]{:S(2)}) collective-permute-start(f32[80,128]{1,0:T(8,128)S(1)} %add.346), channel_id=1, source_target_pairs={{0,8},{8,0},{16,24},{24,16},{1,9},{9,1},{17,25},{25,17},{2,10},{10... | collective-permute-start | bytes 122888 | tf_op jit(solution)/shard_map/ppermute | solution.py:251
  557.8 40.4 %all-to-all-start.6 = ((bf16[4,256,768]{2,1,0:T(8,128)(2,1)}), bf16[4,256,768]{2,1,0:T(8,128)(2,1)S(1)}, u32[]{:S(2)}, u32[]{:S(2)}) async-start(bf16[4,256,768]{2,1,0:T(8,128)(2,1)} %add_convert_fusion.3), calls=%async_computation.6 | async-start | bytes 3145728 | tf_op jit(solution)/shard_map/all_to_all | solution.py:255
  (71 other events, 770.6 us)

commit v4 on v3

--- a/solution.py
+++ b/solution.py
@@ -183,17 +183,17 @@
 
 GATES = {
     At.wqkv_z3: (At.wqkv_z1, At.wqkv_x0),
-    At.wqkv_x1: (At.wqkv_z2, At.wqkv_x0),
-    At.wqkv_x2: (At.wqkv_x0, At.wqkv_z2),
+    At.wqkv_x1: (At.wqkv_x0,),
+    At.wqkv_x2: (At.wqkv_z2,),
     At.a_y: (At.wqkv_z2, At.wqkv_x0),
     At.wout_z1: (At.wqkv_z3, At.wqkv_x1, At.wqkv_x2, At.a_y, At.pack, At.tables, At.cosine, At.sine),
     At.wout_z2: (At.wqkv_z3, At.wqkv_x1, At.wqkv_x2, At.a_y, At.pack, At.tables, At.cosine, At.sine),
     At.wout_x0: (At.wqkv_z3, At.wqkv_x1, At.wqkv_x2, At.a_y, At.pack, At.tables, At.cosine, At.sine),
-    At.wqkv_x3: (At.wqkv_z3, At.wqkv_x1, At.wqkv_x2, At.a_y, At.pack, At.tables, At.cosine, At.sine),
+    At.wqkv_x3: (At.wqkv_z3, At.wqkv_x1, At.wqkv_x2, At.a_y, At.pack, At.tables, At.cosine),
     At.a_c: (At.wqkv_z3, At.wqkv_x1, At.wqkv_x2, At.a_y, At.pack, At.tables, At.cosine, At.sine),
-    At.wout_z3: (At.wout_z2, At.wout_x0, At.wqkv_x3),
+    At.wout_z3: (At.wout_z2, At.wout_x0),
     At.wout_x1: (At.wout_z1, At.wout_z2, At.wout_x0, At.wqkv_x3, At.wqkv_x1),
-    At.wout_x2: (At.wout_z1, At.wout_z2, At.wout_x0, At.wqkv_x3),
+    At.wout_x2: (At.wout_z2, At.wout_x0, At.wqkv_x3),
     At.wgu_z: (At.wout_z3, At.pack),
     At.pair: (At.wgu_z,),
     At.wd_x: (At.wgu_x,),
@@ -201,8 +201,8 @@
     At.bd1_y: (At.bd0_y,),
     At.ffn0: (At.bd_z1,),
     At.bd2_y: (At.bd_z1,),
-    At.ffn1: (At.bd_z3,),
-    At.bd2_c: (At.ffn1, At.wgu_x),
+    At.ffn1: (At.bd_z3, At.ffn0),
+    At.bd2_c: (At.ffn1,),
     At.bd3_y: (At.ffn0,),
     At.db1_add: (At.bd3_y, At.db2_c, At.ffn2, At.db0_c),
     At.db2_add: (At.bd3_y,),
@@ -212,22 +212,25 @@
     At.ggu_own: (At.gdown_x,),
     At.db3_z: (At.db1_z,),
     At.db2_z: (At.gdown_x,),
-    At.ffnin: (At.out_rows, At.gdown_x),
-    At.dmid: (At.ggu_x,),
+    At.ffnin: (At.gdown_x,),
     At.attend_back: (At.out_add,),
     At.gout: (At.gqkv_x,),
     At.out_z: (At.lamb_down, At.gqkv),
-    At.gout_z: (At.out_z,),
+    At.gout_z: (At.out_z, At.lamb_down),
     At.gqkv_z: (At.gout_z,),
     At.lamb_down: (At.gqkv,),
     At.gqkv_own: (At.gqkv, At.gout),
     At.gout_own: (At.gout,),
-    At.lamb_qkv: (At.new_gateup, At.new_down, At.new_gains, At.lamb_out, At.block_out, At.input_grad),
+    At.lamb_qkv: (At.new_gateup, At.new_down, At.new_gains, At.lamb_out, At.block_out, At.input_grad, At.gout_own, At.da_c),
     At.sums: (At.gqkv_own,),
-    At.grad_rows: (At.out_c,),
-    At.bd_z1: (At.wout_x0, At.pair),
-    At.out_add: (At.gdown_z,),
-    At.ffn2: (At.bd3_y,),
+    At.bd_z1: (At.mid_y,),
+    At.out_add: (At.gdown_z, At.gdown),
+    At.ffn2: (At.bd3_y, At.bd_z3),
+    At.wgu_x: (At.a_c,),
+    At.gqkv: (At.gdown_z,),
+    At.bd0_c: (At.bd_z1,),
+    At.out_c: (At.ffn3,),
+    At.wout_x3: (At.a_y,),
 }
 MADE = {}
 
@@ -297,7 +300,7 @@
 
 
 def all_sum(value):
-    for axis in ("c", "x", "y", "z", "o"):
+    for axis in ("c", "z", "x", "y", "o"):
         mask = 1
         while mask < lax.axis_size(axis):
             value = value + exchange(value, axis, mask)

time: 640 us -> 632 us (0.988)
  starting transfers between devices: 85.3 us -> 74.6 us
    all_to_all x7, waiting for transfers between devices: 24.9 us -> 35.5 us  [resplit(): return note(what, lax.all_to_all(hold(what, value), 'z', 0, 0, tiled=True))]
    ppermute x62, waiting for transfers between devices: 212 us -> 204 us  [exchange(): return note(what, lax.ppermute(hold(what, value), axis, pairs))]
    ppermute x62, starting transfers between devices: 53.1 us -> 46.1 us  [exchange(): return note(what, lax.ppermute(hold(what, value), axis, pairs))]
  transfers between devices with their start and end apart: 69 -> 69, of which waited for: 29 -> 30; matrix products, arithmetic and copies ran while one was open for 17% -> 17% of each run, Pallas kernels for 28% -> 28%
where the time goes in v4:
time: 632 us; the launch traced here: 621 us
  waiting for transfers between devices  239 us (38%)
  Pallas kernels  185 us (29%)
  other arithmetic  99.6 us (16%)
  starting transfers between devices  74.6 us (12%)
  local copies, waits for them, and re-layouts  21.3 us (3%)
    ppermute x62, waiting for transfers between devices, exchange(): return note(what, lax.ppermute(hold(what, value), axis, pairs))  204 us
    pallas_call x8, Pallas kernels, weight_grad(): pl.pallas_call(weight_grad_body, grid_spec=pltpu.PrefetchScalarGridSpec(n...  52.8 us
    pallas_call x4, Pallas kernels, ffn_rows(): pl.pallas_call(lambda *refs: ffn_body(n_parts, n_z, n_alias, *refs), grid...  48.3 us
    ppermute x62, starting transfers between devices, exchange(): return note(what, lax.ppermute(hold(what, value), axis, pairs))  46.1 us
    convert_element_type x19, other arithmetic, rounded(): return value.astype(jnp.bfloat16)  43.3 us
    all_to_all x7, waiting for transfers between devices, resplit(): return note(what, lax.all_to_all(hold(what, value), 'z', 0, 0, tiled=True))  35.5 us
    all_to_all x7, starting transfers between devices, resplit(): return note(what, lax.all_to_all(hold(what, value), 'z', 0, 0, tiled=True))  28.5 us
    pallas_call x1, Pallas kernels, attend_back(): pl.pallas_call(lambda *refs: attend_back_body(n_blocks, heads, group, *re...  16.6 us
  transfers between devices with their start and end apart: 69, of which 30 were waited for; matrix products, arithmetic and copies ran while one was open for 17% of the time, Pallas kernels for 28%

profile of v4, /device:TPU:0, one launch (start us, length us, event | category | flops | bytes accessed | tf_op | source)
XLA Modules:
  0.0 621.5 jit_solution(2188864467664037449)
XLA Ops:
  2.9 4.1 collective-permute-start
  10.9 13.8 %collective-permute-done.refs_6_.refs_4_ = bf16[256,768]{1,0:T(8,128)(2,1)} collective-permute-done((bf16[256,768]{1,0:T(8,128)(2,1)S(1)}, bf16[256,768]{1,0:T(8,128)(2,1)}, u32[]{:S(2)}, u32[]{:S(2)}) %collective-permute-start) | collective-permute-done | bytes 393248 | tf_op jit(solution)/shard_map/ppermute | solution.py:254
  42.7 6.3 %collective-permute-done.6.refs_10_.refs_8_ = bf16[256,768]{1,0:T(8,128)(2,1)} collective-permute-done((bf16[256,768]{1,0:T(8,128)(2,1)}, bf16[256,768]{1,0:T(8,128)(2,1)}, u32[]{:S(2)}, u32[]{:S(2)}) %collective-permute-start.6) | collective-permute-done | bytes 393248 | tf_op jit(solution)/shard_map/ppermute | solution.py:254
  55.0 10.2 %collective-permute-done.10.refs_4_ = bf16[256,512]{1,0:T(8,128)(2,1)} collective-permute-done((bf16[256,512]{1,0:T(8,128)(2,1)S(1)}, bf16[256,512]{1,0:T(8,128)(2,1)}, u32[]{:S(2)}, u32[]{:S(2)}) %collective-permute-start.10) | collective-permute-done | bytes 262176 | tf_op jit(solution)/shard_map/ppermute | solution.py:254
  80.3 14.7 %attend.1 = (bf16[512,2048]{1,0:T(8,128)(2,1)}, bf16[8,512,128]{2,1,0:T(8,128)(2,1)}, bf16[2,512,128]{2,1,0:T(8,128)(2,1)}, bf16[512,512]{1,0:T(8,128)(2,1)}, f32[512,128]{1,0:T(8,128)}) custom-call(s32[8]{0:T(128)} %add.295.refs_0_, bf16[128,2048]{1,0:T(8,128)(2,1)} %copy-done.27, bf16[128,2048]{1,0:T(8,128)(2,1)} %collective-permute-done.2.refs_2_, ...), custom_call_target="tpu_custom_call" | custom-call | flops 2684354560 | bytes 8388608 | tf_op jit(solution)/shard_map/attend/pallas_call | solution.py:571
  95.0 4.9 mid_rows.1
  104.6 13.5 %collective-permute-done.17 = bf16[128,2048]{1,0:T(8,128)(2,1)S(1)} collective-permute-done((bf16[128,2048]{1,0:T(8,128)(2,1)S(1)}, bf16[128,2048]{1,0:T(8,128)(2,1)S(1)}, u32[]{:S(2)}, u32[]{:S(2)}) %collective-permute-start.17) | collective-permute-done | bytes 524320 | tf_op jit(solution)/shard_map/ppermute | solution.py:254
  120.7 7.1 %all-to-all-done.refs_4_ = bf16[4,2,256,512]{3,2,1,0:T(8,128)(2,1)S(1)} async-done(((bf16[4,2,256,512]{3,2,1,0:T(8,128)(2,1)}), bf16[4,2,256,512]{3,2,1,0:T(8,128)(2,1)S(1)}, u32[]{:S(2)}, u32[]{:S(2)}) %all-to-all-start) | async-done | bytes 2097184 | tf_op jit(solution)/shard_map/all_to_all | solution.py:258
  137.6 28.9 %collective-permute-done.20.refs_1_ = bf16[256,2048]{1,0:T(8,128)(2,1)} collective-permute-done((bf16[256,2048]{1,0:T(8,128)(2,1)}, bf16[256,2048]{1,0:T(8,128)(2,1)}, u32[]{:S(2)}, u32[]{:S(2)}) %collective-permute-start.20) | collective-permute-done | bytes 1048608 | tf_op jit(solution)/shard_map/ppermute | solution.py:254
  170.1 17.8 %collective-permute-done.28.refs_2_ = bf16[256,2048]{1,0:T(8,128)(2,1)S(1)} collective-permute-done((bf16[256,2048]{1,0:T(8,128)(2,1)}, bf16[256,2048]{1,0:T(8,128)(2,1)S(1)}, u32[]{:S(2)}, u32[]{:S(2)}) %collective-permute-start.28) | collective-permute-done | bytes 1048608 | tf_op jit(solution)/shard_map/ppermute | solution.py:254
  191.7 26.6 %collective-permute-done.18.refs_1_ = bf16[256,2048]{1,0:T(8,128)(2,1)} collective-permute-done((bf16[256,2048]{1,0:T(8,128)(2,1)}, bf16[256,2048]{1,0:T(8,128)(2,1)}, u32[]{:S(2)}, u32[]{:S(2)}) %collective-permute-start.18) | collective-permute-done | bytes 1048608 | tf_op jit(solution)/shard_map/ppermute | solution.py:254
  221.5 11.9 %ffn_rows.4 = (bf16[2048,2048]{1,0:T(8,128)(2,1)}, bf16[2048,2048]{1,0:T(8,128)(2,1)}, bf16[2048,512]{1,0:T(8,128)(2,1)}, bf16[2048,1024]{1,0:T(8,128)(2,1)}, bf...) custom-call(s32[15]{0:T(128)} %concatenate.75.refs_0_, bf16[256,2048]{1,0:T(8,128)(2,1)} %pad_maximum_fusion.6.refs_1_, ...), custom_call_target="tpu_custom_call" | custom-call | flops 1048576 | bytes 1048576 | tf_op jit(solution)/shard_map/ffn_rows/pallas_call | solution.py:640
  233.4 10.2 %collective-permute-done.19.refs_1_ = bf16[256,2048]{1,0:T(8,128)(2,1)S(1)} collective-permute-done((bf16[256,2048]{1,0:T(8,128)(2,1)}, bf16[256,2048]{1,0:T(8,128)(2,1)S(1)}, u32[]{:S(2)}, u32[]{:S(2)}) %collective-permute-start.19) | collective-permute-done | bytes 1048608 | tf_op jit(solution)/shard_map/ppermute | solution.py:254
  248.9 12.3 %ffn_rows.5 = (bf16[2048,2048]{1,0:T(8,128)(2,1)}, bf16[2048,2048]{1,0:T(8,128)(2,1)}, bf16[2048,512]{1,0:T(8,128)(2,1)}, bf16[2048,1024]{1,0:T(8,128)(2,1)}, bf...) custom-call(s32[15]{0:T(128)} %concatenate.82.refs_0_, ...), custom_call_target="tpu_custom_call", output_to_operand_aliasing={{0}: (8, {}), {1}: (9, {}), {2}: (10, {}), {3}: (11, {})} | custom-call | flops 1048576 | bytes 1048576 | tf_op jit(solution)/shard_map/ffn_rows/pallas_call | solution.py:640
  261.3 6.7 %collective-permute-done.25.refs_2_ = bf16[256,2048]{1,0:T(8,128)(2,1)S(1)} collective-permute-done((bf16[256,2048]{1,0:T(8,128)(2,1)S(1)}, bf16[256,2048]{1,0:T(8,128)(2,1)S(1)}, u32[]{:S(2)}, u32[]{:S(2)}) %collective-permute-start.25) | collective-permute-done | bytes 1048608 | tf_op jit(solution)/shard_map/ppermute | solution.py:254
  270.8 12.0 %ffn_rows.6 = (bf16[2048,2048]{1,0:T(8,128)(2,1)}, bf16[2048,2048]{1,0:T(8,128)(2,1)}, bf16[2048,512]{1,0:T(8,128)(2,1)}, bf16[2048,1024]{1,0:T(8,128)(2,1)}, bf...) custom-call(s32[15]{0:T(128)} %concatenate.80.refs_0_, ...), custom_call_target="tpu_custom_call", output_to_operand_aliasing={{0}: (8, {}), {1}: (9, {}), {2}: (10, {}), {3}: (11, {})} | custom-call | flops 1048576 | bytes 1048576 | tf_op jit(solution)/shard_map/ffn_rows/pallas_call | solution.py:640
  285.2 12.1 %ffn_rows.7 = (bf16[2048,2048]{1,0:T(8,128)(2,1)}, bf16[2048,2048]{1,0:T(8,128)(2,1)}, bf16[2048,512]{1,0:T(8,128)(2,1)}, bf16[2048,1024]{1,0:T(8,128)(2,1)}, bf...) custom-call(s32[15]{0:T(128)} %concatenate.76.refs_0_, ...), custom_call_target="tpu_custom_call", output_to_operand_aliasing={{0}: (8, {}), {1}: (9, {}), {2}: (10, {}), {3}: (11, {})} | custom-call | flops 1048576 | bytes 1048576 | tf_op jit(solution)/shard_map/ffn_rows/pallas_call | solution.py:640
  301.5 11.1 %out_rows.1 = (bf16[4,256,2048]{2,1,0:T(8,128)(2,1)}, bf16[4,256,2048]{2,1,0:T(8,128)(2,1)}) custom-call(s32[15]{0:T(128)} %concatenate.75.refs_0_, bf16[2048,512]{1,0:T(8,128)(2,1)} %get-tuple-element.176.refs_1_.right, bf16[4,256,512]{2,1,0:T(8,128)(2,1)} %copy-done.1, bf16[4,256,512]{2,1,0:T(8,128)(2,1)} %copy-done.2), custom_call_target="tpu_custom_call" | custom-call | flops 4194304 | bytes 1048576 | tf_op jit(solution)/shard_map/out_rows/pallas_call | solution.py:727
  321.9 7.0 %weight_grad.9 = bf16[4,256,512]{2,1,0:T(8,128)(2,1)} custom-call(s32[8]{0:T(128)} %copy-done.38, bf16[2048,2048]{1,0:T(8,128)(2,1)} %get-tuple-element.183.left, bf16[2048,512]{1,0:T(8,128)(2,1)} %get-tuple-element.176.refs_1_.right), custom_call_target="tpu_custom_call" | custom-call | flops 1048576 | bytes 1048576 | tf_op jit(solution)/shard_map/weight_grad/pallas_call | solution.py:678
  335.0 9.3 %weight_grad.12 = bf16[4,256,1024]{2,1,0:T(8,128)(2,1)} custom-call(s32[8]{0:T(128)} %copy-done.38, bf16[2048,2048]{1,0:T(8,128)(2,1)} %get-tuple-element.207.left, bf16[2048,1024]{1,0:T(8,128)(2,1)} %get-tuple-element.208.right), custom_call_target="tpu_custom_call" | custom-call | flops 2097152 | bytes 1048576 | tf_op jit(solution)/shard_map/weight_grad/pallas_call | solution.py:678
  348.0 7.3 %collective-permute-done.35 = bf16[4,256,512]{2,1,0:T(8,128)(2,1)} collective-permute-done((bf16[4,256,512]{2,1,0:T(8,128)(2,1)}, bf16[4,256,512]{2,1,0:T(8,128)(2,1)}, u32[]{:S(2)}, u32[]{:S(2)}) %collective-permute-start.35) | collective-permute-done | bytes 1048608 | tf_op jit(solution)/shard_map/ppermute | solution.py:254
  356.1 7.0 %weight_grad.8 = bf16[4,256,512]{2,1,0:T(8,128)(2,1)} custom-call(s32[8]{0:T(128)} %copy-done.38, bf16[2048,2048]{1,0:T(8,128)(2,1)} %get-tuple-element.183.left, bf16[2048,512]{1,0:T(8,128)(2,1)} %get-tuple-element.176.refs_1_.right), custom_call_target="tpu_custom_call" | custom-call | flops 1048576 | bytes 1048576 | tf_op jit(solution)/shard_map/weight_grad/pallas_call | solution.py:678
  365.9 4.2 all-to-all-start.2
  370.1 9.3 %weight_grad.11 = bf16[4,256,1024]{2,1,0:T(8,128)(2,1)} custom-call(s32[8]{0:T(128)} %copy-done.38, bf16[2048,2048]{1,0:T(8,128)(2,1)} %get-tuple-element.207.left, bf16[2048,1024]{1,0:T(8,128)(2,1)} %get-tuple-element.208.right), custom_call_target="tpu_custom_call" | custom-call | flops 2097152 | bytes 1048576 | tf_op jit(solution)/shard_map/weight_grad/pallas_call | solution.py:678
  379.4 11.3 %collective-permute-done.44 = bf16[128,2048]{1,0:T(8,128)(2,1)} collective-permute-done((bf16[128,2048]{1,0:T(8,128)(2,1)}, bf16[128,2048]{1,0:T(8,128)(2,1)}, u32[]{:S(2)}, u32[]{:S(2)}) %collective-permute-start.44) | collective-permute-done | bytes 524320 | tf_op jit(solution)/shard_map/ppermute | solution.py:254
  394.8 3.9 collective-permute-done.49
  398.6 3.9 add_convert_fusion
  407.3 4.4 add_convert_fusion.2
  419.0 16.6 %attend_back.1.right.refs_1_ = bf16[512,768]{1,0:T(8,128)(2,1)} custom-call(s32[8]{0:T(128)} %add.295.refs_0_, bf16[512,2048]{1,0:T(8,128)(2,1)} %pad_maximum_fusion.4.refs_1_.left, bf16[256,512]{1,0:T(8,128)(2,1)} %bitcast.76, bf16[256,512]{1,0:T(8,128)(2,1)} %collective-permute-done.9.refs_3_, bf16[256,512]{1,0:T(8,128)(2,1)} %collective-permute-done.10.refs_4_, ...), custom_call_target="tpu_custom_call" | custom-call | flops 3758096384 | bytes 8388608 | tf_op jit(solution)/shard_map/attend_back/pallas_call | solution.py:594
  435.6 5.2 weight_grad.10
  441.4 6.7 %lamb_down.1 = (f32[2048,256]{1,0:T(8,128)}, f32[2048,256]{1,0:T(8,128)}, f32[2048,256]{1,0:T(8,128)}, f32[2,8,128]{2,1,0:T(8,128)}) custom-call(bf16[4,256,512]{2,1,0:T(8,128)(2,1)} %copy-done.20, f32[2048,256]{1,0:T(8,128)} %refs_1_.4, f32[2048,256]{1,0:T(8,128)} %refs_2_.4, f32[2048,256]{1,0:T(8,128)} %refs_3_.4), custom_call_target="tpu_custom_call" | custom-call | flops 10485760 | bytes 13631488 | tf_op jit(solution)/shard_map/lamb_down/pallas_call | solution.py:820
  448.1 10.0 %collective-permute-done.36 = bf16[4,128,2048]{2,1,0:T(8,128)(2,1)} collective-permute-done((bf16[4,128,2048]{2,1,0:T(8,128)(2,1)}, bf16[4,128,2048]{2,1,0:T(8,128)(2,1)}, u32[]{:S(2)}, u32[]{:S(2)}) %collective-permute-start.36) | collective-permute-done | bytes 2097184 | tf_op jit(solution)/shard_map/ppermute | solution.py:254
  458.1 5.6 add_convert_fusion.1
  465.0 5.0 all-to-all-start.3
  470.0 5.8 grad_rows.1
  477.6 4.9 weight_grad.13
  486.5 12.9 %lamb_gateup.1 = (f32[2,256,2048]{2,1,0:T(8,128)}, f32[2,256,2048]{2,1,0:T(8,128)}, f32[2,256,2048]{2,1,0:T(8,128)}, f32[2,2,8,128]{3,2,1,0:T(8,128)}) custom-call(bf16[4,256,1024]{2,1,0:T(8,128)(2,1)} %copy-done.12, f32[2,256,2048]{2,1,0:T(8,128)} %refs_0_.3, f32[2,256,2048]{2,1,0:T(8,128)} %refs_1_.5, f32[2,256,2048]{2,1,0:T(8,128)} %refs_2_.5), custom_call_target="tpu_custom_call" | custom-call | flops 20971520 | bytes 27262976 | tf_op jit(solution)/shard_map/lamb_gateup/pallas_call | solution.py:789
  499.4 5.3 weight_grad.14
  509.8 4.8 weight_grad.15
  519.9 4.2 all-to-all-start.5
  534.9 5.2 multiply_subtract_fusion.1
  540.2 10.0 %all-to-all-done.5.refs_0_ = bf16[4,256,512]{2,1,0:T(8,128)(2,1)} async-done(((bf16[4,256,512]{2,1,0:T(8,128)(2,1)}), bf16[4,256,512]{2,1,0:T(8,128)(2,1)}, u32[]{:S(2)}, u32[]{:S(2)}) %all-to-all-start.5) | async-done | bytes 1048608 | tf_op jit(solution)/shard_map/all_to_all | solution.py:258
  550.2 3.9 all-to-all-start.6
  554.8 8.9 %multiply_subtract_fusion = f32[2,256,2048]{2,1,0:T(8,128)} fusion(f32[2,256,2048]{2,1,0:T(8,128)} %refs_2_.5, f32[2,256,2048]{2,1,0:T(8,128)} %get-tuple-element.123, f32[2,256,2048]{2,1,0:T(8,128)} %get-tuple-element.129, f32[2]{0:T(128)S(1)} %bitcast.91), kind=kLoop, calls=%fused_computation | loop fusion | flops 7340032 | bytes 16777224 | tf_op jit(solution)/shard_map/sub | solution.py:1172
  572.2 18.3 %all-to-all-done.6.grads = bf16[4,256,768]{2,1,0:T(8,128)(2,1)S(1)} async-done(((bf16[4,256,768]{2,1,0:T(8,128)(2,1)}), bf16[4,256,768]{2,1,0:T(8,128)(2,1)S(1)}, u32[]{:S(2)}, u32[]{:S(2)}) %all-to-all-start.6) | async-done | bytes 1572896 | tf_op jit(solution)/shard_map/all_to_all | solution.py:258
  591.7 3.9 lamb_qkv.1
  597.5 3.9 collective-permute-done.58
  601.5 4.8 collective-permute-done.59
  (310 shorter events, 181.6 us)
Async XLA Ops:
  2.9 21.9 %collective-permute-start = (bf16[256,768]{1,0:T(8,128)(2,1)S(1)}, bf16[256,768]{1,0:T(8,128)(2,1)}, u32[]{:S(2)}, u32[]{:S(2)}) collective-permute-start(bf16[256,768]{1,0:T(8,128)(2,1)S(1)} %pad_maximum_fusion.8.refs_4_.refs_2_), channel_id=1, source_target_pairs={{0,16},{8,24},{16,0},{24,8},{1,17},{9,25},{17,1},{25,9},{2,18},{10... | collective-permute-start | bytes 1179656 | tf_op jit(solution)/shard_map/ppermute | solution.py:254
  7.0 17.8 %collective-permute-start.1 = (bf16[256,768]{1,0:T(8,128)(2,1)S(1)}, bf16[256,768]{1,0:T(8,128)(2,1)S(1)}, u32[]{:S(2)}, u32[]{:S(2)}) collective-permute-start(bf16[256,768]{1,0:T(8,128)(2,1)S(1)} %pad_maximum_fusion.8.refs_4_.refs_2_), channel_id=1, source_target_pairs={{0,4},{4,0},{1,5},{5,1},{2,6},{6,2},{3,7},{7,3},{8,12},{12,8},{9,1... | collective-permute-start | bytes 1179656 | tf_op jit(solution)/shard_map/ppermute | solution.py:254
  8.5 20.8 %collective-permute-start.3 = (bf16[256,768]{1,0:T(8,128)(2,1)S(1)}, bf16[256,768]{1,0:T(8,128)(2,1)}, u32[]{:S(2)}, u32[]{:S(2)}) collective-permute-start(bf16[256,768]{1,0:T(8,128)(2,1)S(1)} %pad_maximum_fusion.8.refs_4_.refs_2_), channel_id=1, source_target_pairs={{0,8},{8,0},{16,24},{24,16},{1,9},{9,1},{17,25},{25,17},{2,10},{10... | collective-permute-start | bytes 1179656 | tf_op jit(solution)/shard_map/ppermute | solution.py:254
  24.8 15.8 %collective-permute-start.2 = (bf16[128,2048]{1,0:T(8,128)(2,1)S(1)}, bf16[128,2048]{1,0:T(8,128)(2,1)}, u32[]{:S(2)}, u32[]{:S(2)}) collective-permute-start(bf16[128,2048]{1,0:T(8,128)(2,1)S(1)} %fusion.4.refs_1_), channel_id=1, source_target_pairs={{0,2},{2,0},{1,3},{3,1},{4,6},{6,4},{5,7},{7,5},{8,10},{10,8},{9,1... | collective-permute-start | bytes 1572872 | tf_op jit(solution)/shard_map/ppermute | solution.py:254
  31.2 17.8 %collective-permute-start.6 = (bf16[256,768]{1,0:T(8,128)(2,1)}, bf16[256,768]{1,0:T(8,128)(2,1)}, u32[]{:S(2)}, u32[]{:S(2)}) collective-permute-start(bf16[256,768]{1,0:T(8,128)(2,1)} %collective-permute-done.refs_6_.refs_4_), channel_id=1, source_target_pairs={{0,4},{4,0},{1,5},{5,1},{2,6},{6,2},{3,7},{7,3},{8,12},{12,8},{9,1... | collective-permute-start | bytes 1179656 | tf_op jit(solution)/shard_map/ppermute | solution.py:254
  49.0 31.3 %collective-permute-start.7 = (bf16[256,2048]{1,0:T(8,128)(2,1)}, bf16[256,2048]{1,0:T(8,128)(2,1)}, u32[]{:S(2)}, u32[]{:S(2)}) collective-permute-start(bf16[256,2048]{1,0:T(8,128)(2,1)} %pad_maximum_fusion.5), channel_id=1, source_target_pairs={{0,1},{1,0},{2,3},{3,2},{4,5},{5,4},{6,7},{7,6},{8,9},{9,8},{10,11... | collective-permute-start | bytes 3145736 | tf_op jit(solution)/shard_map/ppermute | solution.py:254
  49.2 16.1 %collective-permute-start.10 = (bf16[256,512]{1,0:T(8,128)(2,1)S(1)}, bf16[256,512]{1,0:T(8,128)(2,1)}, u32[]{:S(2)}, u32[]{:S(2)}) collective-permute-start(bf16[256,512]{1,0:T(8,128)(2,1)S(1)} %bitcast.72), channel_id=1, source_target_pairs={{0,16},{8,24},{16,0},{24,8},{1,17},{9,25},{17,1},{25,9},{2,18},{10... | collective-permute-start | bytes 786440 | tf_op jit(solution)/shard_map/ppermute | solution.py:254
  54.2 15.4 %collective-permute-start.8 = (bf16[256,768]{1,0:T(8,128)(2,1)}, bf16[256,768]{1,0:T(8,128)(2,1)S(1)}, u32[]{:S(2)}, u32[]{:S(2)}) collective-permute-start(bf16[256,768]{1,0:T(8,128)(2,1)} %collective-permute-done.4.refs_7_.refs_5_), channel_id=1, source_target_pairs={{0,4},{4,0},{1,5},{5,1},{2,6},{6,2},{3,7},{7,3},{8,12},{12,8},{9,1... | collective-permute-start | bytes 1179656 | tf_op jit(solution)/shard_map/ppermute | solution.py:254
  54.7 16.3 %collective-permute-start.9 = (bf16[256,512]{1,0:T(8,128)(2,1)S(1)}, bf16[256,512]{1,0:T(8,128)(2,1)}, u32[]{:S(2)}, u32[]{:S(2)}) collective-permute-start(bf16[256,512]{1,0:T(8,128)(2,1)S(1)} %bitcast.74), channel_id=1, source_target_pairs={{0,8},{8,0},{16,24},{24,16},{1,9},{9,1},{17,25},{25,17},{2,10},{10... | collective-permute-start | bytes 786440 | tf_op jit(solution)/shard_map/ppermute | solution.py:254
  69.6 25.4 %collective-permute-start.14 = (bf16[256,512]{1,0:T(8,128)(2,1)}, bf16[256,512]{1,0:T(8,128)(2,1)}, u32[]{:S(2)}, u32[]{:S(2)}) collective-permute-start(bf16[256,512]{1,0:T(8,128)(2,1)} %collective-permute-done.10.refs_4_), channel_id=1, source_target_pairs={{0,4},{4,0},{1,5},{5,1},{2,6},{6,2},{3,7},{7,3},{8,12},{12,8},{9,1... | collective-permute-start | bytes 786440 | tf_op jit(solution)/shard_map/ppermute | solution.py:254
  71.0 23.9 %collective-permute-start.13 = (bf16[256,512]{1,0:T(8,128)(2,1)}, bf16[256,512]{1,0:T(8,128)(2,1)}, u32[]{:S(2)}, u32[]{:S(2)}) collective-permute-start(bf16[256,512]{1,0:T(8,128)(2,1)} %collective-permute-done.9.refs_3_), channel_id=1, source_target_pairs={{0,4},{4,0},{1,5},{5,1},{2,6},{6,2},{3,7},{7,3},{8,12},{12,8},{9,1... | collective-permute-start | bytes 786440 | tf_op jit(solution)/shard_map/ppermute | solution.py:254
  74.5 20.5 %collective-permute-start.15 = (bf16[256,512]{1,0:T(8,128)(2,1)}, bf16[256,512]{1,0:T(8,128)(2,1)}, u32[]{:S(2)}, u32[]{:S(2)}) collective-permute-start(bf16[256,512]{1,0:T(8,128)(2,1)} %collective-permute-done.12.refs_5_), channel_id=1, source_target_pairs={{0,4},{4,0},{1,5},{5,1},{2,6},{6,2},{3,7},{7,3},{8,12},{12,8},{9,1... | collective-permute-start | bytes 786440 | tf_op jit(solution)/shard_map/ppermute | solution.py:254
  76.6 51.1 %all-to-all-start = ((bf16[4,2,256,512]{3,2,1,0:T(8,128)(2,1)}), bf16[4,2,256,512]{3,2,1,0:T(8,128)(2,1)S(1)}, u32[]{:S(2)}, u32[]{:S(2)}) async-start(bf16[4,2,256,512]{3,2,1,0:T(8,128)(2,1)} %bitcast.66), calls=%async_computation | async-start | bytes 4194304 | tf_op jit(solution)/shard_map/all_to_all | solution.py:258
  128.8 37.6 %collective-permute-start.20 = (bf16[256,2048]{1,0:T(8,128)(2,1)}, bf16[256,2048]{1,0:T(8,128)(2,1)}, u32[]{:S(2)}, u32[]{:S(2)}) collective-permute-start(bf16[256,2048]{1,0:T(8,128)(2,1)} %pad_maximum_fusion.6.refs_1_), channel_id=1, source_target_pairs={{0,8},{8,0},{16,24},{24,16},{1,9},{9,1},{17,25},{25,17},{2,10},{10... | collective-permute-start | bytes 3145736 | tf_op jit(solution)/shard_map/ppermute | solution.py:254
  128.8 37.6 %collective-permute-start.21 = (bf16[256,2048]{1,0:T(8,128)(2,1)}, bf16[256,2048]{1,0:T(8,128)(2,1)}, u32[]{:S(2)}, u32[]{:S(2)}) collective-permute-start(bf16[256,2048]{1,0:T(8,128)(2,1)} %pad_maximum_fusion.6.refs_1_), channel_id=1, source_target_pairs={{0,2},{2,0},{1,3},{3,1},{4,6},{6,4},{5,7},{7,5},{8,10},{10,8},{9,1... | collective-permute-start | bytes 3145736 | tf_op jit(solution)/shard_map/ppermute | solution.py:254
  129.3 61.8 %collective-permute-start.23 = (bf16[4,2,256,512]{3,2,1,0:T(8,128)(2,1)S(1)}, bf16[4,2,256,512]{3,2,1,0:T(8,128)(2,1)}, u32[]{:S(2)}, u32[]{:S(2)}) collective-permute-start(bf16[4,2,256,512]{3,2,1,0:T(8,128)(2,1)S(1)} %all-to-all-done.refs_4_), channel_id=1, source_target_pairs={{0,4},{4,0},{1,5},{5,1},{2,6},{6,2},{3,7},{7,3},{8,12},{12,8},{9,1... | collective-permute-start | bytes 6291464 | tf_op jit(solution)/shard_map/ppermute | solution.py:254
  133.8 57.2 %all-to-all-start.1 = ((bf16[4,256,512]{2,1,0:T(8,128)(2,1)}), bf16[4,256,512]{2,1,0:T(8,128)(2,1)S(1)}, u32[]{:S(2)}, u32[]{:S(2)}) async-start(bf16[4,256,512]{2,1,0:T(8,128)(2,1)} %bitcast.70), calls=%async_computation.1 | async-start | bytes 2097152 | tf_op jit(solution)/shard_map/all_to_all | solution.py:258
  166.5 21.4 %collective-permute-start.28 = (bf16[256,2048]{1,0:T(8,128)(2,1)}, bf16[256,2048]{1,0:T(8,128)(2,1)S(1)}, u32[]{:S(2)}, u32[]{:S(2)}) collective-permute-start(bf16[256,2048]{1,0:T(8,128)(2,1)} %collective-permute-done.20.refs_1_), channel_id=1, source_target_pairs={{0,2},{2,0},{1,3},{3,1},{4,6},{6,4},{5,7},{7,5},{8,10},{10,8},{9,1... | collective-permute-start | bytes 3145736 | tf_op jit(solution)/shard_map/ppermute | solution.py:254
  170.1 50.5 %collective-permute-start.22 = (bf16[512,2048]{1,0:T(8,128)(2,1)}, bf16[512,2048]{1,0:T(8,128)(2,1)}, u32[]{:S(2)}, u32[]{:S(2)}) collective-permute-start(bf16[512,2048]{1,0:T(8,128)(2,1)} %pad_maximum_fusion), channel_id=1, source_target_pairs={{0,1},{1,0},{2,3},{3,2},{4,5},{5,4},{6,7},{7,6},{8,9},{9,8},{10,11... | collective-permute-start | bytes 6291464 | tf_op jit(solution)/shard_map/ppermute | solution.py:254
  170.1 48.2 %collective-permute-start.18 = (bf16[256,2048]{1,0:T(8,128)(2,1)}, bf16[256,2048]{1,0:T(8,128)(2,1)}, u32[]{:S(2)}, u32[]{:S(2)}) collective-permute-start(bf16[256,2048]{1,0:T(8,128)(2,1)} %pad_maximum_fusion.6.refs_1_), channel_id=1, source_target_pairs={{0,16},{8,24},{16,0},{24,8},{1,17},{9,25},{17,1},{25,9},{2,18},{10... | collective-permute-start | bytes 3145736 | tf_op jit(solution)/shard_map/ppermute | solution.py:254
  191.1 57.8 %collective-permute-start.29 = (bf16[512,2048]{1,0:T(8,128)(2,1)}, bf16[512,2048]{1,0:T(8,128)(2,1)}, u32[]{:S(2)}, u32[]{:S(2)}) collective-permute-start(bf16[512,2048]{1,0:T(8,128)(2,1)} %pad_maximum_fusion.3), channel_id=1, source_target_pairs={{0,1},{1,0},{2,3},{3,2},{4,5},{5,4},{6,7},{7,6},{8,9},{9,8},{10,11... | collective-permute-start | bytes 6291464 | tf_op jit(solution)/shard_map/ppermute | solution.py:254
  191.1 29.4 %collective-permute-start.24 = (bf16[4,256,512]{2,1,0:T(8,128)(2,1)S(1)}, bf16[4,256,512]{2,1,0:T(8,128)(2,1)S(1)}, u32[]{:S(2)}, u32[]{:S(2)}) collective-permute-start(bf16[4,256,512]{2,1,0:T(8,128)(2,1)S(1)} %all-to-all-done.1.refs_6_.refs_2_), channel_id=1, source_target_pairs={{0,4},{4,0},{1,5},{5,1},{2,6},{6,2},{3,7},{7,3},{8,12},{12,8},{9,1... | collective-permute-start | bytes 3145736 | tf_op jit(solution)/shard_map/ppermute | solution.py:254
  218.3 25.3 %collective-permute-start.19 = (bf16[256,2048]{1,0:T(8,128)(2,1)}, bf16[256,2048]{1,0:T(8,128)(2,1)S(1)}, u32[]{:S(2)}, u32[]{:S(2)}) collective-permute-start(bf16[256,2048]{1,0:T(8,128)(2,1)} %collective-permute-done.18.refs_1_), channel_id=1, source_target_pairs={{0,8},{8,0},{16,24},{24,16},{1,9},{9,1},{17,25},{25,17},{2,10},{10... | collective-permute-start | bytes 3145736 | tf_op jit(solution)/shard_map/ppermute | solution.py:254
  218.3 27.5 %collective-permute-start.27 = (bf16[256,2048]{1,0:T(8,128)(2,1)}, bf16[256,2048]{1,0:T(8,128)(2,1)}, u32[]{:S(2)}, u32[]{:S(2)}) collective-permute-start(bf16[256,2048]{1,0:T(8,128)(2,1)} %collective-permute-done.18.refs_1_), channel_id=1, source_target_pairs={{0,2},{2,0},{1,3},{3,1},{4,6},{6,4},{5,7},{7,5},{8,10},{10,8},{9,1... | collective-permute-start | bytes 3145736 | tf_op jit(solution)/shard_map/ppermute | solution.py:254
  243.6 24.4 %collective-permute-start.25 = (bf16[256,2048]{1,0:T(8,128)(2,1)S(1)}, bf16[256,2048]{1,0:T(8,128)(2,1)S(1)}, u32[]{:S(2)}, u32[]{:S(2)}) collective-permute-start(bf16[256,2048]{1,0:T(8,128)(2,1)S(1)} %collective-permute-done.19.refs_1_), channel_id=1, source_target_pairs={{0,2},{2,0},{1,3},{3,1},{4,6},{6,4},{5,7},{7,5},{8,10},{10,8},{9,1... | collective-permute-start | bytes 3145736 | tf_op jit(solution)/shard_map/ppermute | solution.py:254
  270.3 27.2 %collective-permute-start.32 = (bf16[256,2048]{1,0:T(8,128)(2,1)}, bf16[256,2048]{1,0:T(8,128)(2,1)S(1)}, u32[]{:S(2)}, u32[]{:S(2)}) collective-permute-start(bf16[256,2048]{1,0:T(8,128)(2,1)} %get-tuple-element.156), channel_id=1, source_target_pairs={{0,1},{1,0},{2,3},{3,2},{4,5},{5,4},{6,7},{7,6},{8,9},{9,8},{10,11... | collective-permute-start | bytes 3145736 | tf_op jit(solution)/shard_map/ppermute | solution.py:254
  270.7 26.8 %collective-permute-start.37 = (bf16[256,2048]{1,0:T(8,128)(2,1)}, bf16[256,2048]{1,0:T(8,128)(2,1)}, u32[]{:S(2)}, u32[]{:S(2)}) collective-permute-start(bf16[256,2048]{1,0:T(8,128)(2,1)} %get-tuple-element.166), channel_id=1, source_target_pairs={{0,1},{1,0},{2,3},{3,2},{4,5},{5,4},{6,7},{7,6},{8,9},{9,8},{10,11... | collective-permute-start | bytes 3145736 | tf_op jit(solution)/shard_map/ppermute | solution.py:254
  282.8 14.7 %collective-permute-start.38 = (bf16[256,2048]{1,0:T(8,128)(2,1)}, bf16[256,2048]{1,0:T(8,128)(2,1)}, u32[]{:S(2)}, u32[]{:S(2)}) collective-permute-start(bf16[256,2048]{1,0:T(8,128)(2,1)} %get-tuple-element.190), channel_id=1, source_target_pairs={{0,1},{1,0},{2,3},{3,2},{4,5},{5,4},{6,7},{7,6},{8,9},{9,8},{10,11... | collective-permute-start | bytes 3145736 | tf_op jit(solution)/shard_map/ppermute | solution.py:254
  297.3 15.5 %collective-permute-start.34 = (bf16[256,2048]{1,0:T(8,128)(2,1)}, bf16[256,2048]{1,0:T(8,128)(2,1)}, u32[]{:S(2)}, u32[]{:S(2)}) collective-permute-start(bf16[256,2048]{1,0:T(8,128)(2,1)} %get-tuple-element.179), channel_id=1, source_target_pairs={{0,1},{1,0},{2,3},{3,2},{4,5},{5,4},{6,7},{7,6},{8,9},{9,8},{10,11... | collective-permute-start | bytes 3145736 | tf_op jit(solution)/shard_map/ppermute | solution.py:254
  300.0 15.5 %collective-permute-start.39 = (bf16[128,2048]{1,0:T(8,128)(2,1)}, bf16[128,2048]{1,0:T(8,128)(2,1)}, u32[]{:S(2)}, u32[]{:S(2)}) collective-permute-start(bf16[128,2048]{1,0:T(8,128)(2,1)} %add_convert_fusion.13), channel_id=1, source_target_pairs={{0,2},{2,0},{1,3},{3,1},{4,6},{6,4},{5,7},{7,5},{8,10},{10,8},{9,1... | collective-permute-start | bytes 1572872 | tf_op jit(solution)/shard_map/ppermute | solution.py:254
  312.6 94.7 %collective-permute-start.31 = (bf16[4,256,2048]{2,1,0:T(8,128)(2,1)}, bf16[4,256,2048]{2,1,0:T(8,128)(2,1)}, u32[]{:S(2)}, u32[]{:S(2)}) collective-permute-start(bf16[4,256,2048]{2,1,0:T(8,128)(2,1)} %get-tuple-element.180), channel_id=1, source_target_pairs={{0,1},{1,0},{2,3},{3,2},{4,5},{5,4},{6,7},{7,6},{8,9},{9,8},{10,11... | collective-permute-start | bytes 12582920 | tf_op jit(solution)/shard_map/ppermute | solution.py:254
  315.0 15.1 %collective-permute-start.42 = (bf16[128,2048]{1,0:T(8,128)(2,1)}, bf16[128,2048]{1,0:T(8,128)(2,1)}, u32[]{:S(2)}, u32[]{:S(2)}) collective-permute-start(bf16[128,2048]{1,0:T(8,128)(2,1)} %add_convert_fusion.10), channel_id=1, source_target_pairs={{0,2},{2,0},{1,3},{3,1},{4,6},{6,4},{5,7},{7,5},{8,10},{10,8},{9,1... | collective-permute-start | bytes 1572872 | tf_op jit(solution)/shard_map/ppermute | solution.py:254
  317.8 14.7 %collective-permute-start.40 = (bf16[128,2048]{1,0:T(8,128)(2,1)}, bf16[128,2048]{1,0:T(8,128)(2,1)}, u32[]{:S(2)}, u32[]{:S(2)}) collective-permute-start(bf16[128,2048]{1,0:T(8,128)(2,1)} %add_convert_fusion.12), channel_id=1, source_target_pairs={{0,8},{8,0},{16,24},{24,16},{1,9},{9,1},{17,25},{25,17},{2,10},{10... | collective-permute-start | bytes 1572872 | tf_op jit(solution)/shard_map/ppermute | solution.py:254
  320.3 24.0 %collective-permute-start.41 = (bf16[128,2048]{1,0:T(8,128)(2,1)}, bf16[128,2048]{1,0:T(8,128)(2,1)}, u32[]{:S(2)}, u32[]{:S(2)}) collective-permute-start(bf16[128,2048]{1,0:T(8,128)(2,1)} %add_convert_fusion.11), channel_id=1, source_target_pairs={{0,2},{2,0},{1,3},{3,1},{4,6},{6,4},{5,7},{7,5},{8,10},{10,8},{9,1... | collective-permute-start | bytes 1572872 | tf_op jit(solution)/shard_map/ppermute | solution.py:254
  328.8 26.4 %collective-permute-start.35 = (bf16[4,256,512]{2,1,0:T(8,128)(2,1)}, bf16[4,256,512]{2,1,0:T(8,128)(2,1)}, u32[]{:S(2)}, u32[]{:S(2)}) collective-permute-start(bf16[4,256,512]{2,1,0:T(8,128)(2,1)} %weight_grad.9), channel_id=1, source_target_pairs={{0,4},{4,0},{1,5},{5,1},{2,6},{6,2},{3,7},{7,3},{8,12},{12,8},{9,1... | collective-permute-start | bytes 3145736 | tf_op jit(solution)/shard_map/ppermute | solution.py:254
  334.2 21.9 %collective-permute-start.33 = (bf16[128,2048]{1,0:T(8,128)(2,1)}, bf16[128,2048]{1,0:T(8,128)(2,1)S(1)}, u32[]{:S(2)}, u32[]{:S(2)}) collective-permute-start(bf16[128,2048]{1,0:T(8,128)(2,1)} %add_convert_fusion.14), channel_id=1, source_target_pairs={{0,2},{2,0},{1,3},{3,1},{4,6},{6,4},{5,7},{7,5},{8,10},{10,8},{9,1... | collective-permute-start | bytes 1572872 | tf_op jit(solution)/shard_map/ppermute | solution.py:254
  344.3 54.3 %collective-permute-start.49 = (bf16[4,256,1024]{2,1,0:T(8,128)(2,1)}, bf16[4,256,1024]{2,1,0:T(8,128)(2,1)}, u32[]{:S(2)}, u32[]{:S(2)}) collective-permute-start(bf16[4,256,1024]{2,1,0:T(8,128)(2,1)} %weight_grad.12), channel_id=1, source_target_pairs={{0,4},{4,0},{1,5},{5,1},{2,6},{6,2},{3,7},{7,3},{8,12},{12,8},{9,1... | collective-permute-start | bytes 6291464 | tf_op jit(solution)/shard_map/ppermute | solution.py:254
  355.3 35.5 %collective-permute-start.44 = (bf16[128,2048]{1,0:T(8,128)(2,1)}, bf16[128,2048]{1,0:T(8,128)(2,1)}, u32[]{:S(2)}, u32[]{:S(2)}) collective-permute-start(bf16[128,2048]{1,0:T(8,128)(2,1)} %add_convert_fusion.8), channel_id=1, source_target_pairs={{0,16},{8,24},{16,0},{24,8},{1,17},{9,25},{17,1},{25,9},{2,18},{10... | collective-permute-start | bytes 1572872 | tf_op jit(solution)/shard_map/ppermute | solution.py:254
  365.9 36.6 %all-to-all-start.2 = ((bf16[4,256,512]{2,1,0:T(8,128)(2,1)}), bf16[4,256,512]{2,1,0:T(8,128)(2,1)S(1)}, u32[]{:S(2)}, u32[]{:S(2)}) async-start(bf16[4,256,512]{2,1,0:T(8,128)(2,1)} %add_convert_fusion.5), calls=%async_computation.2 | async-start | bytes 2097152 | tf_op jit(solution)/shard_map/all_to_all | solution.py:258
  394.2 18.0 %collective-permute-start.45 = (bf16[128,2048]{1,0:T(8,128)(2,1)}, bf16[128,2048]{1,0:T(8,128)(2,1)}, u32[]{:S(2)}, u32[]{:S(2)}) collective-permute-start(bf16[128,2048]{1,0:T(8,128)(2,1)} %fusion.16), channel_id=1, source_target_pairs={{0,2},{2,0},{1,3},{3,1},{4,6},{6,4},{5,7},{7,5},{8,10},{10,8},{9,1... | collective-permute-start | bytes 1572872 | tf_op jit(solution)/shard_map/ppermute | solution.py:254
  403.5 60.2 %all-to-all-start.4 = ((bf16[4,256,1024]{2,1,0:T(8,128)(2,1)}), bf16[4,256,1024]{2,1,0:T(8,128)(2,1)S(1)}, u32[]{:S(2)}, u32[]{:S(2)}) async-start(bf16[4,256,1024]{2,1,0:T(8,128)(2,1)} %add_convert_fusion), calls=%async_computation.4 | async-start | bytes 4194304 | tf_op jit(solution)/shard_map/all_to_all | solution.py:258
  411.7 46.4 %collective-permute-start.36 = (bf16[4,128,2048]{2,1,0:T(8,128)(2,1)}, bf16[4,128,2048]{2,1,0:T(8,128)(2,1)}, u32[]{:S(2)}, u32[]{:S(2)}) collective-permute-start(bf16[4,128,2048]{2,1,0:T(8,128)(2,1)} %add_convert_fusion.2), channel_id=1, source_target_pairs={{0,2},{2,0},{1,3},{3,1},{4,6},{6,4},{5,7},{7,5},{8,10},{10,8},{9,1... | collective-permute-start | bytes 6291464 | tf_op jit(solution)/shard_map/ppermute | solution.py:254
  440.8 36.8 %collective-permute-start.50 = (bf16[4,256,768]{2,1,0:T(8,128)(2,1)}, bf16[4,256,768]{2,1,0:T(8,128)(2,1)}, u32[]{:S(2)}, u32[]{:S(2)}) collective-permute-start(bf16[4,256,768]{2,1,0:T(8,128)(2,1)} %weight_grad.10), channel_id=1, source_target_pairs={{0,4},{4,0},{1,5},{5,1},{2,6},{6,2},{3,7},{7,3},{8,12},{12,8},{9,1... | collective-permute-start | bytes 4718600 | tf_op jit(solution)/shard_map/ppermute | solution.py:254
  465.0 54.9 %all-to-all-start.3 = ((bf16[4,128,2048]{2,1,0:T(8,128)(2,1)}), bf16[4,128,2048]{2,1,0:T(8,128)(2,1)}, u32[]{:S(2)}, u32[]{:S(2)}) async-start(bf16[4,128,2048]{2,1,0:T(8,128)(2,1)} %add_convert_fusion.1), calls=%async_computation.3 | async-start | bytes 4194304 | tf_op jit(solution)/shard_map/all_to_all | solution.py:258
  482.4 34.6 %collective-permute-start.56 = (bf16[4,256,512]{2,1,0:T(8,128)(2,1)}, bf16[4,256,512]{2,1,0:T(8,128)(2,1)}, u32[]{:S(2)}, u32[]{:S(2)}) collective-permute-start(bf16[4,256,512]{2,1,0:T(8,128)(2,1)} %weight_grad.13), channel_id=1, source_target_pairs={{0,4},{4,0},{1,5},{5,1},{2,6},{6,2},{3,7},{7,3},{8,12},{12,8},{9,1... | collective-permute-start | bytes 3145736 | tf_op jit(solution)/shard_map/ppermute | solution.py:254
  485.0 19.7 %collective-permute-start.48 = (bf16[128,2048]{1,0:T(8,128)(2,1)}, bf16[128,2048]{1,0:T(8,128)(2,1)S(1)}, u32[]{:S(2)}, u32[]{:S(2)}) collective-permute-start(bf16[128,2048]{1,0:T(8,128)(2,1)} %add_convert_fusion.6), channel_id=1, source_target_pairs={{0,2},{2,0},{1,3},{3,1},{4,6},{6,4},{5,7},{7,5},{8,10},{10,8},{9,1... | collective-permute-start | bytes 1572872 | tf_op jit(solution)/shard_map/ppermute | solution.py:254
  519.9 30.3 %all-to-all-start.5 = ((bf16[4,256,512]{2,1,0:T(8,128)(2,1)}), bf16[4,256,512]{2,1,0:T(8,128)(2,1)}, u32[]{:S(2)}, u32[]{:S(2)}) async-start(bf16[4,256,512]{2,1,0:T(8,128)(2,1)} %add_convert_fusion.4), calls=%async_computation.5 | async-start | bytes 2097152 | tf_op jit(solution)/shard_map/all_to_all | solution.py:258
  550.2 40.3 %all-to-all-start.6 = ((bf16[4,256,768]{2,1,0:T(8,128)(2,1)}), bf16[4,256,768]{2,1,0:T(8,128)(2,1)S(1)}, u32[]{:S(2)}, u32[]{:S(2)}) async-start(bf16[4,256,768]{2,1,0:T(8,128)(2,1)} %add_convert_fusion.3), calls=%async_computation.6 | async-start | bytes 3145728 | tf_op jit(solution)/shard_map/all_to_all | solution.py:258
  (71 other events, 699.8 us)
